TPU v7x, 32 devices: a whole 2x2x4 slice. The times are simulated.
32 devices in a mesh: fsdp: 2 (over core), expert: 16 (over z, y, x).
Axes of the slice: x: 2, y: 2, z: 4, core: 2. Of those that a mesh axis runs over, the one named last changes fastest.
Arguments:
- tokens: bfloat16 [16, 2048, 1024], P('expert', 'fsdp'), may hold values from -6 to 6
- out_grad: bfloat16 [16, 2048, 1024], P('expert', 'fsdp'), may hold values from -8 to 8
- routes: int32 [16, 2048, 1], P('expert', 'fsdp'), may hold values from 0 to 15; in each aligned block of 1024 rows (0 to 1023, 1024 to 2047, ..., all dimensions but the last counted through in order) at most 128 rows name the same one
- prefix: int32 [16], P('expert'), may hold values from 204 to 1024
- ln1_gain: bfloat16 [1024], P('fsdp'), may hold values from 0.5 to 1.5
- ln1_bias: bfloat16 [1024], P('fsdp'), may hold values from -0.625 to 0.625
- w_qkv: bfloat16 [1024, 3072], P('fsdp'), may hold values from -0.1875 to 0.1875
- q_bias: bfloat16 [1024], P('fsdp'), may hold values from -0.625 to 0.625
- v_bias: bfloat16 [1024], P('fsdp'), may hold values from -0.625 to 0.625
- attention_output_weight: bfloat16 [1024, 1024], P('fsdp'), may hold values from -4 to 4
- attention_output_bias: bfloat16 [1024], P('fsdp'), may hold values from -0.625 to 0.625
- ln2_gain: bfloat16 [1024], P('fsdp'), may hold values from 0.5 to 1.5
- ln2_bias: bfloat16 [1024], P('fsdp'), may hold values from -0.625 to 0.625
- w_router: bfloat16 [1024, 16], P('fsdp'), may hold values from -0.09375 to 0.09375
- moe_bias: bfloat16 [1024], P('fsdp'), may hold values from -0.625 to 0.625
- w_in: bfloat16 [16, 1024, 4096], P('expert', None, 'fsdp'), may hold values from -0.1875 to 0.1875
- w_down: bfloat16 [16, 4096, 1024], P('expert', 'fsdp'), may hold values from -1.5 to 1.5
Outputs:
- out: bfloat16 [16, 2048, 1024], P('expert', 'fsdp')
- d_tokens: bfloat16 [16, 2048, 1024], P('expert', 'fsdp')
- d_ln1_gain: float32 [1024], P(('fsdp', 'expert'))
- d_ln1_bias: float32 [1024], P(('fsdp', 'expert'))
- d_w_qkv: float32 [1024, 3072], P(('fsdp', 'expert'))
- d_q_bias: float32 [1024], P(('fsdp', 'expert'))
- d_v_bias: float32 [1024], P(('fsdp', 'expert'))
- d_w_out: float32 [1024, 1024], P(('fsdp', 'expert'))
- d_out_bias: float32 [1024], P(('fsdp', 'expert'))
- d_ln2_gain: float32 [1024], P(('fsdp', 'expert'))
- d_ln2_bias: float32 [1024], P(('fsdp', 'expert'))
- d_w_router: float32 [1024, 16], P(('fsdp', 'expert'))
- d_moe_bias: float32 [1024], P(('fsdp', 'expert'))
- d_w_in: float32 [16, 1024, 4096], P('expert', None, 'fsdp')
- d_w_down: float32 [16, 4096, 1024], P('expert', 'fsdp')
Inputs may be any that keep to these rules, and one draw needn't show every extreme that they name: `routes`: in each aligned block of 1024 rows (the positions of one sequence on one device) at most 128 rows name the same expert, and some block has 128 that do.
All inputs are finite; a program needn't handle non-finite values.
Results may differ from a plain program's by a relative error of at most 0.02.
Values may be sent and summed in bfloat16 or wider, within the bound.
No kernel may reach another device: no remote copies, remote signals or barrier semaphores. Data moves between devices by JAX's collectives and lax.ppermute only.
A program may use at most 384 MiB of HBM per device.

v0:
```python
from functools import partial
import math

import jax
import jax.numpy as jnp
from jax import lax
from jax.sharding import PartitionSpec as P

HEAD_DIM = 64


NORM_EPSILON = 1e-05
MASK_FILL = -1e30


def passed_along(array, axis, by):
    size = lax.axis_size(axis)
    pairs = [(i, i + by) for i in range(size) if 0 <= i + by < size]
    return lax.ppermute(array, axis, pairs)


def layer_norm(values, norm_gain, norm_bias):
    center = values - jnp.mean(values, axis=-1, keepdims=True)
    inv_std = lax.rsqrt(jnp.mean(center * center, axis=-1, keepdims=True) + NORM_EPSILON)
    normed = center * inv_std
    return (normed * norm_gain + norm_bias, normed, inv_std)


def norm_backward(grad_out, normed, inv_std, norm_gain):
    scaled = grad_out * norm_gain
    return inv_std * (
        scaled
        - jnp.mean(scaled, axis=-1, keepdims=True)
        - normed * jnp.mean(scaled * normed, axis=-1, keepdims=True)
    )


def contract_rows(left_side, right_side):
    return lax.dot_general(
        left_side, right_side, (((0,), (0,)), ((), ())), preferred_element_type=jnp.float32
    )


def contract_last(left_side, right_side):
    return lax.dot_general(
        left_side, right_side, (((1,), (1,)), ((), ())), preferred_element_type=jnp.float32
    )


def visible(query_pos, key_pos, prefix_len):
    keys_row = key_pos[None, :]
    return ((keys_row <= query_pos[:, None]) | (keys_row < prefix_len)) & (keys_row >= 0)


def body(
    tokens,
    out_grad,
    routes,
    prefix,
    ln1_gain,
    ln1_bias,
    w_qkv,
    q_bias,
    v_bias,
    attention_output_weight,
    attention_output_bias,
    ln2_gain,
    ln2_bias,
    w_router,
    moe_bias,
    w_in,
    w_down,
):
    gathered = (
        lax.all_gather(ln1_gain, "fsdp", axis=0, tiled=True),
        lax.all_gather(ln1_bias, "fsdp", axis=0, tiled=True),
        lax.all_gather(w_qkv, "fsdp", axis=0, tiled=True),
        lax.all_gather(q_bias, "fsdp", axis=0, tiled=True),
        lax.all_gather(v_bias, "fsdp", axis=0, tiled=True),
        lax.all_gather(attention_output_weight, "fsdp", axis=0, tiled=True),
        lax.all_gather(attention_output_bias, "fsdp", axis=0, tiled=True),
        lax.all_gather(ln2_gain, "fsdp", axis=0, tiled=True),
        lax.all_gather(ln2_bias, "fsdp", axis=0, tiled=True),
        lax.all_gather(w_router, "fsdp", axis=0, tiled=True),
        lax.all_gather(moe_bias, "fsdp", axis=0, tiled=True),
    )
    qkv_weight = gathered[2]
    out_weight = gathered[5]
    router_weight = gathered[9]
    norm1_gain = gathered[0].astype(jnp.float32)
    norm1_bias = gathered[1].astype(jnp.float32)
    query_bias = gathered[3].astype(jnp.float32)
    value_bias = gathered[4].astype(jnp.float32)
    output_bias = gathered[6].astype(jnp.float32)
    norm2_gain = gathered[7].astype(jnp.float32)
    norm2_bias = gathered[8].astype(jnp.float32)
    expert_bias = gathered[10].astype(jnp.float32)
    row_count = tokens.shape[1]
    model_width = tokens.shape[2]
    head_count = model_width // HEAD_DIM
    query_scale = HEAD_DIM ** (-0.5)
    experts_all = router_weight.shape[1]
    most_slots = max(2, 2 * row_count // experts_all)
    half_index = lax.axis_index("fsdp")
    query_pos = half_index * row_count + jnp.arange(row_count, dtype=jnp.int32)
    key_pos = jnp.concatenate([query_pos - row_count, query_pos])
    prefix_len = prefix[0]
    residual = tokens[0].astype(jnp.float32)
    norm1_out, normed1, inv_std1 = layer_norm(residual, norm1_gain, norm1_bias)
    attn_in = norm1_out.astype(jnp.bfloat16)
    projected = jnp.dot(attn_in, qkv_weight, preferred_element_type=jnp.float32)
    queries = ((projected[:, :model_width] + query_bias) * query_scale).astype(jnp.bfloat16)
    key_value = jnp.concatenate(
        [projected[:, model_width : 2 * model_width], projected[:, 2 * model_width :] + value_bias],
        axis=1,
    ).astype(jnp.bfloat16)
    earlier = passed_along(key_value, "fsdp", 1)
    all_keys = jnp.concatenate([earlier, key_value], axis=0)
    query_heads = queries.reshape(row_count, head_count, HEAD_DIM)
    key_count = all_keys.shape[0]
    block_rows = math.gcd(key_count, 512)

    def key_block(block_index):
        offset = block_index * block_rows
        key_part = lax.dynamic_slice_in_dim(all_keys, offset, block_rows, 0)
        key_heads = key_part[:, :model_width].reshape(block_rows, head_count, HEAD_DIM)
        value_heads = key_part[:, model_width:].reshape(block_rows, head_count, HEAD_DIM)
        allowed = visible(
            query_pos, lax.dynamic_slice_in_dim(key_pos, offset, block_rows, 0), prefix_len
        )[None]
        return (key_heads, value_heads, allowed)

    def forward_block(carried, block_index):
        run_max, run_sum, run_acc = carried
        key_heads, value_heads, allowed = key_block(block_index)
        scores = jnp.einsum(
            "qhd,khd->hqk", query_heads, key_heads, preferred_element_type=jnp.float32
        )
        updated_maximum = jnp.maximum(
            run_max, jnp.max(jnp.where(allowed, scores, MASK_FILL), axis=-1)
        )
        weights = jnp.where(allowed, jnp.exp(scores - updated_maximum[..., None]), 0.0)
        factor = jnp.exp(run_max - updated_maximum)
        run_sum = run_sum * factor + jnp.sum(weights, axis=-1)
        run_acc = run_acc * factor[..., None] + jnp.einsum(
            "hqk,khd->hqd",
            weights.astype(jnp.bfloat16),
            value_heads,
            preferred_element_type=jnp.float32,
        )
        return ((updated_maximum, run_sum, run_acc), None)

    start_state = (
        jnp.full((head_count, row_count), MASK_FILL, jnp.float32),
        jnp.zeros((head_count, row_count), jnp.float32),
        jnp.zeros((head_count, row_count, HEAD_DIM), jnp.float32),
    )
    final_state, unused = lax.scan(forward_block, start_state, jnp.arange(key_count // block_rows))
    run_max, run_sum, run_acc = final_state
    log_sum = run_max + jnp.log(run_sum)
    context_heads = run_acc / run_sum[..., None]
    context_vectors = jnp.transpose(context_heads, (1, 0, 2)).reshape(row_count, model_width)
    context_low = context_vectors.astype(jnp.bfloat16)
    attention_result = (
        jnp.dot(context_low, out_weight, preferred_element_type=jnp.float32) + output_bias
    )
    hidden = residual + attention_result
    norm2_out, normed2, inv_std2 = layer_norm(hidden, norm2_gain, norm2_bias)
    mixed_low = norm2_out.astype(jnp.bfloat16)
    logits = jnp.dot(mixed_low, router_weight, preferred_element_type=jnp.float32)
    router_probs = jax.nn.softmax(logits, axis=-1)
    token_route = routes[0, :, 0]
    one_hot = (token_route[:, None] == jnp.arange(experts_all, dtype=jnp.int32)[None, :]).astype(
        jnp.float32
    )
    gate_value = jnp.sum(router_probs * one_hot, axis=-1)
    earlier_same = jnp.cumsum(one_hot, axis=0) - one_hot
    slot_index = jnp.sum(earlier_same * one_hot, axis=-1).astype(jnp.int32)

    def dispatch(row_values):
        empty_buffer = jnp.zeros((experts_all, most_slots, model_width), row_values.dtype)
        return empty_buffer.at[token_route, slot_index].set(row_values)

    def collect(buffer):
        return buffer[token_route, slot_index]

    arrived = lax.all_to_all(dispatch(mixed_low), "expert", split_axis=0, concat_axis=1, tiled=True)
    owner_in = lax.all_gather(arrived, "fsdp", axis=1, tiled=True)
    pre_act = jnp.einsum("erd,edh->erh", owner_in, w_in, preferred_element_type=jnp.float32)
    activation = jax.nn.gelu(pre_act, approximate=True).astype(jnp.bfloat16)
    partial_out = jnp.einsum("erh,ehd->erd", activation, w_down, preferred_element_type=jnp.float32)
    expert_rows = lax.psum_scatter(
        partial_out.astype(jnp.bfloat16), "fsdp", scatter_dimension=1, tiled=True
    )
    returned = lax.all_to_all(expert_rows, "expert", split_axis=1, concat_axis=0, tiled=True)
    expert_value = collect(returned).astype(jnp.float32)
    output = hidden + gate_value[:, None] * expert_value + expert_bias
    out_cot = out_grad[0].astype(jnp.float32)
    d_expert_bias = jnp.sum(out_cot, axis=0)
    d_gate = jnp.sum(out_cot * expert_value, axis=-1)
    d_expert_value = (gate_value[:, None] * out_cot).astype(jnp.bfloat16)
    grads_arrived = lax.all_to_all(
        dispatch(d_expert_value), "expert", split_axis=0, concat_axis=1, tiled=True
    )
    unused_out, gelu_back = jax.vjp(partial(jax.nn.gelu, approximate=True), pre_act)
    grad_in = lax.all_gather(grads_arrived, "fsdp", axis=1, tiled=True)
    d_activ = jnp.einsum("erd,ehd->erh", grad_in, w_down, preferred_element_type=jnp.float32)
    d_w_down_out = jnp.einsum(
        "erh,erd->ehd", activation, grad_in, preferred_element_type=jnp.float32
    )
    d_pre = gelu_back(d_activ)[0].astype(jnp.bfloat16)
    d_w_in_out = jnp.einsum("erd,erh->edh", owner_in, d_pre, preferred_element_type=jnp.float32)
    d_rows_part = jnp.einsum("erh,edh->erd", d_pre, w_in, preferred_element_type=jnp.float32)
    d_rows = lax.psum_scatter(
        d_rows_part.astype(jnp.bfloat16), "fsdp", scatter_dimension=1, tiled=True
    )
    d_mixed_expert = collect(
        lax.all_to_all(d_rows, "expert", split_axis=1, concat_axis=0, tiled=True)
    ).astype(jnp.float32)
    d_logits = ((d_gate * gate_value)[:, None] * (one_hot - router_probs)).astype(jnp.bfloat16)
    d_mixed = contract_last(d_logits, router_weight) + d_mixed_expert
    d_router = contract_rows(mixed_low, d_logits)
    d_norm2_gain = jnp.sum(d_mixed * normed2, axis=0)
    d_norm2_bias = jnp.sum(d_mixed, axis=0)
    d_hidden = out_cot + norm_backward(d_mixed, normed2, inv_std2, norm2_gain)
    d_attn = d_hidden.astype(jnp.bfloat16)
    d_output_bias = jnp.sum(d_attn.astype(jnp.float32), axis=0)
    d_out_weight = contract_rows(context_low, d_attn)
    d_context = contract_last(d_attn, out_weight).astype(jnp.bfloat16)
    d_context_heads = d_context.reshape(row_count, head_count, HEAD_DIM)
    row_delta = jnp.sum(
        jnp.transpose(d_context_heads.astype(jnp.float32), (1, 0, 2)) * context_heads, axis=-1
    )

    def backward_block(d_query_acc, block_index):
        key_heads, value_heads, allowed = key_block(block_index)
        scores = jnp.einsum(
            "qhd,khd->hqk", query_heads, key_heads, preferred_element_type=jnp.float32
        )
        probs_part = jnp.where(allowed, jnp.exp(scores - log_sum[..., None]), 0.0)
        d_probs = jnp.einsum(
            "qhd,khd->hqk", d_context_heads, value_heads, preferred_element_type=jnp.float32
        )
        d_scores = (probs_part * (d_probs - row_delta[..., None])).astype(jnp.bfloat16)
        d_query_acc = d_query_acc + jnp.einsum(
            "hqk,khd->qhd", d_scores, key_heads, preferred_element_type=jnp.float32
        )
        d_key_part = jnp.einsum(
            "hqk,qhd->khd", d_scores, query_heads, preferred_element_type=jnp.float32
        ).reshape(block_rows, model_width)
        d_value_part = jnp.einsum(
            "hqk,qhd->khd",
            probs_part.astype(jnp.bfloat16),
            d_context_heads,
            preferred_element_type=jnp.float32,
        ).reshape(block_rows, model_width)
        return (d_query_acc, jnp.concatenate([d_key_part, d_value_part], axis=1))

    d_query_sum, d_kv_blocks = lax.scan(
        backward_block,
        jnp.zeros((row_count, head_count, HEAD_DIM), jnp.float32),
        jnp.arange(key_count // block_rows),
    )
    d_kv_all = d_kv_blocks.reshape(key_count, 2 * model_width)
    returned_kv = passed_along(d_kv_all[:row_count].astype(jnp.bfloat16), "fsdp", -1).astype(
        jnp.float32
    )
    d_key_value = (d_kv_all[row_count:] + returned_kv).astype(jnp.bfloat16)
    d_query = (d_query_sum.reshape(row_count, model_width) * query_scale).astype(jnp.bfloat16)
    d_qkv = jnp.concatenate([d_query, d_key_value], axis=1)
    d_query_bias = jnp.sum(d_query.astype(jnp.float32), axis=0)
    d_value_bias = jnp.sum(d_key_value[:, model_width:].astype(jnp.float32), axis=0)
    query_key_value_weight_grad = contract_rows(attn_in, d_qkv)
    d_norm1_out = contract_last(d_qkv, qkv_weight)
    d_norm1_gain = jnp.sum(d_norm1_out * normed1, axis=0)
    d_norm1_bias = jnp.sum(d_norm1_out, axis=0)
    d_tokens = (d_hidden + norm_backward(d_norm1_out, normed1, inv_std1, norm1_gain)).astype(
        jnp.bfloat16
    )
    summed = (
        lax.psum_scatter(d_norm1_gain, ("fsdp", "expert"), scatter_dimension=0, tiled=True),
        lax.psum_scatter(d_norm1_bias, ("fsdp", "expert"), scatter_dimension=0, tiled=True),
        lax.psum_scatter(
            query_key_value_weight_grad, ("fsdp", "expert"), scatter_dimension=0, tiled=True
        ),
        lax.psum_scatter(d_query_bias, ("fsdp", "expert"), scatter_dimension=0, tiled=True),
        lax.psum_scatter(d_value_bias, ("fsdp", "expert"), scatter_dimension=0, tiled=True),
        lax.psum_scatter(d_out_weight, ("fsdp", "expert"), scatter_dimension=0, tiled=True),
        lax.psum_scatter(d_output_bias, ("fsdp", "expert"), scatter_dimension=0, tiled=True),
        lax.psum_scatter(d_norm2_gain, ("fsdp", "expert"), scatter_dimension=0, tiled=True),
        lax.psum_scatter(d_norm2_bias, ("fsdp", "expert"), scatter_dimension=0, tiled=True),
        lax.psum_scatter(d_router, ("fsdp", "expert"), scatter_dimension=0, tiled=True),
        lax.psum_scatter(d_expert_bias, ("fsdp", "expert"), scatter_dimension=0, tiled=True),
    )
    return (
        output.astype(jnp.bfloat16)[None],
        d_tokens[None],
        summed[0],
        summed[1],
        summed[2],
        summed[3],
        summed[4],
        summed[5],
        summed[6],
        summed[7],
        summed[8],
        summed[9],
        summed[10],
        d_w_in_out,
        d_w_down_out,
    )


def solution(mesh):
    return jax.shard_map(
        body,
        mesh=mesh,
        in_specs=(
            P("expert", "fsdp", None),
            P("expert", "fsdp", None),
            P("expert", "fsdp", None),
            P("expert"),
            P("fsdp"),
            P("fsdp"),
            P("fsdp", None),
            P("fsdp"),
            P("fsdp"),
            P("fsdp", None),
            P("fsdp"),
            P("fsdp"),
            P("fsdp"),
            P("fsdp", None),
            P("fsdp"),
            P("expert", None, "fsdp"),
            P("expert", "fsdp", None),
        ),
        out_specs=(
            P("expert", "fsdp", None),
            P("expert", "fsdp", None),
            P(("fsdp", "expert")),
            P(("fsdp", "expert")),
            P(("fsdp", "expert"), None),
            P(("fsdp", "expert")),
            P(("fsdp", "expert")),
            P(("fsdp", "expert"), None),
            P(("fsdp", "expert")),
            P(("fsdp", "expert")),
            P(("fsdp", "expert")),
            P(("fsdp", "expert"), None),
            P(("fsdp", "expert")),
            P("expert", None, "fsdp"),
            P("expert", "fsdp", None),
        ),
        check_vma=False,
    )
```

profile of v0, /device:TPU:0, one launch (start us, length us, event | category | flops | bytes accessed | tf_op | source)
XLA Modules:
  0.0 1677.8 jit_solution(17687012517512811270)
XLA Ops:
  92.2 196.7 %while.28 = (s32[]{:T(128)}, f32[16,1024]{1,0:T(8,128)S(1)}, f32[16,1024]{1,0:T(8,128)S(1)}, f32[16,1024,64]{1,2,0:T(8,128)}, s32[4]{0:T(128)S(1)}, /*index=5*/s...) while((s32[]{:T(128)}, f32[16,1024]{1,0:T(8,128)S(1)}, ...), condition=%wide.region_5.6_spmd.clone, body=%wide.region_2.5_spmd.clone.sunk | while | flops 2219395072 | bytes 120604920 | solution.py:158
  124.4 16.0 fusion.170
  172.7 17.2 %fusion.170 = f32[16,1024,64]{1,2,0:T(8,128)} fusion(f32[16,1024,64]{1,2,0:T(8,128)} %get-tuple-element.670, f32[16,1024]{1,0:T(8,128)S(1)} %get-tuple-element.634, pred[]{:T(512)S(6)} %compare.12, bf16[512,16,64]{0,2,1:T(8,128)(2,1)} %bitcast.278, f32[16,512,1024]{2,1,0:T(8,128)} %get-tuple-element.632, f32[16,1024]{1,0:T(8,128)S(1)} %select_maximum_fusion.2, ...), kind=kOutput, calls=%fused_computation.18.clone.1 | convolution fusion | flops 1102053376 | bytes 43646976 | tf_op jit(solution)/shard_map/while/body/eval_jaxpr/hqk,khd->hqd/dot_general | solution.py:145
  222.1 17.2 %fusion.170 = f32[16,1024,64]{1,2,0:T(8,128)} fusion(f32[16,1024,64]{1,2,0:T(8,128)} %get-tuple-element.670, f32[16,1024]{1,0:T(8,128)S(1)} %get-tuple-element.634, pred[]{:T(512)S(6)} %compare.12, bf16[512,16,64]{0,2,1:T(8,128)(2,1)} %bitcast.278, f32[16,512,1024]{2,1,0:T(8,128)} %get-tuple-element.632, f32[16,1024]{1,0:T(8,128)S(1)} %select_maximum_fusion.2, ...), kind=kOutput, calls=%fused_computation.18.clone.1 | convolution fusion | flops 1102053376 | bytes 43646976 | tf_op jit(solution)/shard_map/while/body/eval_jaxpr/hqk,khd->hqd/dot_general | solution.py:145
  271.5 17.2 %fusion.170 = f32[16,1024,64]{1,2,0:T(8,128)} fusion(f32[16,1024,64]{1,2,0:T(8,128)} %get-tuple-element.670, f32[16,1024]{1,0:T(8,128)S(1)} %get-tuple-element.634, pred[]{:T(512)S(6)} %compare.12, bf16[512,16,64]{0,2,1:T(8,128)(2,1)} %bitcast.278, f32[16,512,1024]{2,1,0:T(8,128)} %get-tuple-element.632, f32[16,1024]{1,0:T(8,128)S(1)} %select_maximum_fusion.2, ...), kind=kOutput, calls=%fused_computation.18.clone.1 | convolution fusion | flops 1102053376 | bytes 43646976 | tf_op jit(solution)/shard_map/while/body/eval_jaxpr/hqk,khd->hqd/dot_general | solution.py:145
  314.6 101.1 %all_to_all.48 = bf16[16,128,1024]{2,1,0:T(8,128)(2,1)} all-to-all(bf16[16,128,1024]{2,1,0:T(8,128)(2,1)} %bitcast.290), channel_id=1, replica_groups=mesh['fsdp'=2,'expert'=16] {'expert'}, dimensions={0} | all-to-all | bytes 8388608 | tf_op jit(solution)/shard_map/all_to_all | solution.py:187
  415.8 18.4 %all-gather.17.cloned.1.call-done = bf16[1,4096,1024]{2,1,0:T(8,128)(2,1)} async-done(((bf16[1,2048,1024]{2,1,0:T(8,128)(2,1)}), bf16[1,4096,1024]{2,1,0:T(8,128)(2,1)}) %all-gather.17.cloned.1.call-update) | async-done | bytes 8388624 | tf_op jit(solution)/shard_map/all_gather | solution.py:188
  434.2 25.4 %fusion.38 = f32[4096,2048]{1,0:T(8,128)} fusion(bf16[1,4096,1024]{2,1,0:T(8,128)(2,1)} %all-gather.17.cloned.1.call-done, bf16[1,1024,2048]{2,1,0:T(8,128)(2,1)} %param.36), kind=kOutput, calls=%fused_computation.63 | convolution fusion | flops 17179869184 | bytes 46137344 | tf_op jit(solution)/shard_map/erd,edh->erh/dot_general | solution.py:189
  459.6 27.6 %convert_bitcast_fusion.1 = bf16[1,4096,1024]{2,1,0:T(8,128)(2,1)} fusion(bf16[1,2048,1024]{2,1,0:T(8,128)(2,1)S(1)} %copy-done.73, f32[4096,2048]{1,0:T(8,128)} %fusion.38), kind=kOutput, calls=%fused_computation.66 | convolution fusion | flops 17259560960 | bytes 46137344 | tf_op jit(solution)/shard_map/erh,ehd->erd/dot_general | solution.py:191
  487.3 18.1 %reduce-scatter.8.cloned.1.call-done = bf16[1,2048,1024]{2,1,0:T(8,128)(2,1)} async-done(((bf16[1,4096,1024]{2,1,0:T(8,128)(2,1)}), bf16[1,2048,1024]{2,1,0:T(8,128)(2,1)}) %reduce-scatter.8.cloned.1.call-update) | async-done | bytes 4194320 | tf_op jit(solution)/shard_map/reduce_scatter | solution.py:192
  514.9 26.0 %reduce.9 = bf16[2048,1024]{1,0:T(8,128)(2,1)} reduce(bf16[2048,1,1024]{2,1,0:T(2,128)(2,1)} %bitcast.282, bf16[]{:T(256)} %broadcast.411), dimensions={1}, to_apply=%bitcast.212.reduce_sub_computation | reduce | bytes 8388610
  562.2 77.5 %all-to-all-done.1 = bf16[16,2,65536]{2,1,0:T(2,128)(2,1)} async-done(((bf16[16,2,65536]{2,1,0:T(2,128)(2,1)}), bf16[16,2,65536]{2,1,0:T(2,128)(2,1)}, u32[]{:S(2)}, u32[]{:S(2)}) %all-to-all-start.1) | async-done | bytes 4194336 | tf_op jit(solution)/shard_map/all_to_all | solution.py:195
  659.1 20.9 %gather_fusion = bf16[1024,1024]{1,0:T(8,128)(2,1)} fusion(bf16[16,128,1024]{2,1,0:T(8,128)(2,1)} %bitcast.279, s32[1024]{0:T(1024)S(1)} %bitcast.275), kind=kCustom, calls=%fused_computation | custom fusion | bytes 4202496 | tf_op jit(solution)/shard_map/gather | solution.py:185
  698.9 113.7 %all_to_all.49 = bf16[16,128,1024]{2,1,0:T(8,128)(2,1)} all-to-all(bf16[16,128,1024]{2,1,0:T(8,128)(2,1)} %bitcast.289), channel_id=1, replica_groups=mesh['fsdp'=2,'expert'=16] {'expert'}, dimensions={0} | all-to-all | bytes 8388608 | tf_op jit(solution)/shard_map/all_to_all | solution.py:202
  812.7 18.4 %all-gather.19.cloned.1.call-done = bf16[1,4096,1024]{2,1,0:T(8,128)(2,1)} async-done(((bf16[1,2048,1024]{2,1,0:T(8,128)(2,1)}), bf16[1,4096,1024]{2,1,0:T(8,128)(2,1)}) %all-gather.19.cloned.1.call-update) | async-done | bytes 8388624 | tf_op jit(solution)/shard_map/all_gather | solution.py:206
  831.0 42.2 %fusion.31 = bf16[4096,2048]{1,0:T(8,128)(2,1)} fusion(f32[4096,2048]{1,0:T(8,128)} %fusion.38, bf16[1,4096,1024]{2,1,0:T(8,128)(2,1)} %all-gather.19.cloned.1.call-done, bf16[1,2048,1024]{2,1,0:T(8,128)(2,1)} %param.37), kind=kOutput, calls=%fused_computation.52 | convolution fusion | flops 17347641344 | bytes 62914560 | tf_op jit(solution)/shard_map/erd,ehd->erh/dot_general | solution.py:207
  873.3 23.7 %convert_bitcast_fusion = bf16[1,4096,1024]{2,1,0:T(8,128)(2,1)} fusion(bf16[4096,2048]{1,0:T(8,128)(2,1)} %fusion.31, bf16[1,1024,2048]{2,1,0:T(8,128)(2,1)} %param.36), kind=kOutput, calls=%fused_computation.65 | convolution fusion | flops 17184063488 | bytes 29360128 | tf_op jit(solution)/shard_map/erh,edh->erd/dot_general | solution.py:213
  897.0 18.1 %reduce-scatter.10.cloned.1.call-done = bf16[1,2048,1024]{2,1,0:T(8,128)(2,1)} async-done(((bf16[1,4096,1024]{2,1,0:T(8,128)(2,1)}), bf16[1,2048,1024]{2,1,0:T(8,128)(2,1)}) %reduce-scatter.10.cloned.1.call-update) | async-done | bytes 4194320 | tf_op jit(solution)/shard_map/reduce_scatter | solution.py:214
  923.7 26.0 %reduce.10 = bf16[2048,1024]{1,0:T(8,128)(2,1)} reduce(bf16[2048,1,1024]{2,1,0:T(2,128)(2,1)} %bitcast.283, bf16[]{:T(256)} %broadcast.411), dimensions={1}, to_apply=%bitcast.211.reduce_sub_computation | reduce | bytes 8388610
  971.8 78.2 %all-to-all-done.3 = bf16[16,2,65536]{2,1,0:T(2,128)(2,1)} async-done(((bf16[16,2,65536]{2,1,0:T(2,128)(2,1)}), bf16[16,2,65536]{2,1,0:T(2,128)(2,1)}, u32[]{:S(2)}, u32[]{:S(2)}) %all-to-all-start.3) | async-done | bytes 4194336 | tf_op jit(solution)/shard_map/all_to_all | solution.py:218
  1069.9 15.5 gather_fusion.1
  1109.2 351.1 %while.29 = (s32[]{:T(128)}, f32[1024,16,64]{0,2,1:T(8,128)}, f32[4,512,2048]{2,1,0:T(8,128)}, s32[4]{0:T(128)S(1)}, bf16[2048,2048]{0,1:T(8,128)(2,1)}, /*index...) while((s32[]{:T(128)}, f32[1024,16,64]{0,2,1:T(8,128)}, ...), condition=%wide.region_23.24_spmd.clone, body=%wide.region_22.23_spmd.clone.sunk | while | flops 5440538624 | bytes 305875520 | solution.py:259
  1129.2 15.5 fusion.184
  1144.7 20.7 %fusion.183 = bf16[16,1024,512]{1,2,0:T(8,128)(2,1)} fusion(f32[16,512,1024]{2,1,0:T(8,128)} %fusion.182, f32[16,1024]{1,0:T(8,128)S(1)} %get-tuple-element.741, f32[16,1024]{1,0:T(8,128)S(1)} %get-tuple-element.739, pred[1024,512]{0,1:T(8,128)(4,1)S(1)} %copy-done.21, bf16[512,16,64]{0,2,1:T(8,128)(2,1)S(1)} %bitcast.286, ...), kind=kOutput, calls=%fused_computation.30.clone.1 | convolution fusion | flops 1115684864 | bytes 54132736 | tf_op jit(solution)/shard_map/while/body/eval_jaxpr/qhd,khd->hqk/dot_general | solution.py:241
  1215.2 15.6 fusion.184
  1230.8 20.8 %fusion.183 = bf16[16,1024,512]{1,2,0:T(8,128)(2,1)} fusion(f32[16,512,1024]{2,1,0:T(8,128)} %fusion.182, f32[16,1024]{1,0:T(8,128)S(1)} %get-tuple-element.741, f32[16,1024]{1,0:T(8,128)S(1)} %get-tuple-element.739, pred[1024,512]{0,1:T(8,128)(4,1)S(1)} %copy-done.21, bf16[512,16,64]{0,2,1:T(8,128)(2,1)S(1)} %bitcast.286, ...), kind=kOutput, calls=%fused_computation.30.clone.1 | convolution fusion | flops 1115684864 | bytes 54132736 | tf_op jit(solution)/shard_map/while/body/eval_jaxpr/qhd,khd->hqk/dot_general | solution.py:241
  1319.2 20.7 %fusion.183 = bf16[16,1024,512]{1,2,0:T(8,128)(2,1)} fusion(f32[16,512,1024]{2,1,0:T(8,128)} %fusion.182, f32[16,1024]{1,0:T(8,128)S(1)} %get-tuple-element.741, f32[16,1024]{1,0:T(8,128)S(1)} %get-tuple-element.739, pred[1024,512]{0,1:T(8,128)(4,1)S(1)} %copy-done.21, bf16[512,16,64]{0,2,1:T(8,128)(2,1)S(1)} %bitcast.286, ...), kind=kOutput, calls=%fused_computation.30.clone.1 | convolution fusion | flops 1115684864 | bytes 54132736 | tf_op jit(solution)/shard_map/while/body/eval_jaxpr/qhd,khd->hqk/dot_general | solution.py:241
  1407.3 20.7 %fusion.183 = bf16[16,1024,512]{1,2,0:T(8,128)(2,1)} fusion(f32[16,512,1024]{2,1,0:T(8,128)} %fusion.182, f32[16,1024]{1,0:T(8,128)S(1)} %get-tuple-element.741, f32[16,1024]{1,0:T(8,128)S(1)} %get-tuple-element.739, pred[1024,512]{0,1:T(8,128)(4,1)S(1)} %copy-done.21, bf16[512,16,64]{0,2,1:T(8,128)(2,1)S(1)} %bitcast.286, ...), kind=kOutput, calls=%fused_computation.30.clone.1 | convolution fusion | flops 1115684864 | bytes 54132736 | tf_op jit(solution)/shard_map/while/body/eval_jaxpr/qhd,khd->hqk/dot_general | solution.py:241
  1500.4 24.1 %fusion.51 = f32[1,1024,2048]{2,1,0:T(8,128)} fusion(bf16[4096,2048]{1,0:T(8,128)(2,1)} %fusion.31, bf16[1,4096,1024]{2,1,0:T(8,128)(2,1)} %all-gather.17.cloned.1.call-done), kind=kOutput, calls=%fused_computation.84 | convolution fusion | flops 17179869184 | bytes 33554432 | tf_op jit(solution)/shard_map/erd,erh->edh/dot_general | solution.py:212
  1524.5 26.9 %fusion.54 = f32[1,2048,1024]{2,1,0:T(8,128)} fusion(bf16[1,4096,1024]{2,1,0:T(8,128)(2,1)} %all-gather.19.cloned.1.call-done, f32[4096,2048]{1,0:T(8,128)} %fusion.38), kind=kOutput, calls=%fused_computation.85 | convolution fusion | flops 17255366656 | bytes 50331648 | tf_op jit(solution)/shard_map/erh,erd->ehd/dot_general | solution.py:208
  1579.0 59.3 %all-reduce.8 = (f32[1024]{0:T(1024)S(1)}, f32[1024]{0:T(1024)S(1)}, f32[1024]{0:T(1024)S(1)}, f32[1024]{0:T(1024)S(1)}, f32[1024]{0:T(1024)S(1)}, /*index=5*/f3...) all-reduce(f32[1024]{0:T(1024)S(1)} %get-tuple-element.402, ...), channel_id=4, replica_groups=mesh['fsdp'=2,'expert'=16] {'fsdp','expert'}, use_global_device_ids=true, to_apply=%region_27.28.clone | all-reduce | flops 8192 | bytes 65536
  1653.1 17.9 %reduce-scatter.12.cloned.1.call-done = f32[32,3072]{1,0:T(8,128)} async-done(((f32[1024,3072]{1,0:T(8,128)}), f32[32,3072]{1,0:T(8,128)}) %reduce-scatter.12.cloned.1.call-update) | async-done | bytes 393232 | tf_op jit(solution)/shard_map/reduce_scatter | solution.py:283
  (453 shorter events, 695.6 us)
Async XLA Ops:
  7.2 21.9 %all-gather.13.cloned.1.call-start = ((), (), s32[]{:S(2)}) async-start(), calls=%async_computation.9 | async-start | bytes 9437184 | tf_op jit(solution)/shard_map/all_gather | solution.py:77
  7.9 286.0 %all-gather.15.cloned.1.call-start = ((), (), s32[]{:S(2)}) async-start(), calls=%async_computation.10 | async-start | bytes 3145728 | tf_op jit(solution)/shard_map/all_gather | solution.py:80
  10.6 18.5 %copy-start.49 = (f32[2,1,512]{2,1,0:T(1,128)}, f32[2,1,512]{2,1,0:T(1,128)S(1)}, u32[]{:S(2)}) copy-start(f32[2,1,512]{2,1,0:T(1,128)S(1)} %convert_element_type.200) | copy-start | bytes 12292
  13.0 16.0 copy-start.62
  21.0 17.3 %copy-start.7 = (bf16[1,1024,1024]{1,2,0:T(8,128)(2,1)}, bf16[1,1024,1024]{1,2,0:T(8,128)(2,1)S(1)}, u32[]{:S(2)}) copy-start(bf16[1,1024,1024]{1,2,0:T(8,128)(2,1)S(1)} %copy.127) | copy-start | bytes 6291460
  21.4 16.9 %copy-start.38 = (f32[1024]{0:T(1024)}, f32[1024]{0:T(1024)S(1)}, u32[]{:S(2)}) copy-start(f32[1024]{0:T(1024)S(1)} %broadcast_multiply_fusion.5) | copy-start | bytes 12292
  22.0 16.3 copy-start.51
  41.4 17.0 %copy-start.42 = (s32[1,1024,1]{1,2,0:T(1,128)S(1)}, s32[1,1024,1]{1,2,0:T(1,128)}, u32[]{:S(2)}) copy-start(s32[1,1024,1]{1,2,0:T(1,128)} %param.23) | copy-start | bytes 12292
  41.4 21.8 %copy-start.61 = (bf16[512,16]{0,1:T(8,128)(2,1)S(1)}, bf16[512,16]{0,1:T(8,128)(2,1)}, u32[]{:S(2)}) copy-start(bf16[512,16]{0,1:T(8,128)(2,1)} %param.34) | copy-start | bytes 49156
  44.1 25.2 %collective-permute-start = (bf16[1024,2048]{1,0:T(8,128)(2,1)}, bf16[1024,2048]{1,0:T(8,128)(2,1)}, u32[]{:S(2)}, u32[]{:S(2)}) collective-permute-start(bf16[1024,2048]{1,0:T(8,128)(2,1)} %pad_maximum_fusion.1), channel_id=1, source_target_pairs={{0,16},{1,17},{2,18},{3,19},{4,20},{5,21},{6,22},{7,23},{8,24},{9,... | collective-permute-start | bytes 12582920 | tf_op jit(solution)/shard_map/ppermute | solution.py:19
  48.2 386.0 %all-gather.17.cloned.1.call-start = ((), (), s32[]{:S(2)}) async-start(), calls=%async_computation.11 | async-start | bytes 12582912 | tf_op jit(solution)/shard_map/all_gather | solution.py:188
  305.2 110.6 %copy-start.40 = (f32[1024]{0:T(1024)}, f32[1024]{0:T(1024)S(1)}, u32[]{:S(2)}) copy-start(f32[1024]{0:T(1024)S(1)} %get-tuple-element.487) | copy-start | bytes 12292
  305.2 110.5 %copy-start.57 = (f32[1024]{0:T(1024)}, f32[1024]{0:T(1024)S(1)}, u32[]{:S(2)}) copy-start(f32[1024]{0:T(1024)S(1)} %fusion.94) | copy-start | bytes 12292
  415.8 89.7 %reduce-scatter.8.cloned.1.call-start = ((), (), s32[]{:S(2)}) async-start(), calls=%async_computation.12 | async-start | bytes 12582912 | tf_op jit(solution)/shard_map/reduce_scatter | solution.py:192
  434.2 25.5 %copy-start.73 = (bf16[1,2048,1024]{2,1,0:T(8,128)(2,1)S(1)}, bf16[1,2048,1024]{2,1,0:T(8,128)(2,1)}, u32[]{:S(2)}) copy-start(bf16[1,2048,1024]{2,1,0:T(8,128)(2,1)} %param.37) | copy-start | bytes 12582916
  552.3 87.4 %all-to-all-start.1 = ((bf16[16,2,65536]{2,1,0:T(2,128)(2,1)}), bf16[16,2,65536]{2,1,0:T(2,128)(2,1)}, u32[]{:S(2)}, u32[]{:S(2)}) async-start(bf16[16,2,65536]{2,1,0:T(2,128)(2,1)} %reshape.458), calls=%async_computation.2 | async-start | bytes 8388608 | tf_op jit(solution)/shard_map/all_to_all | solution.py:195
  559.2 271.8 %all-gather.19.cloned.1.call-start = ((), (), s32[]{:S(2)}) async-start(), calls=%async_computation.13 | async-start | bytes 12582912 | tf_op jit(solution)/shard_map/all_gather | solution.py:206
  562.2 121.7 %copy-start.12 = (bf16[1,1024,1024]{1,2,0:T(8,128)(2,1)}, bf16[1,1024,1024]{1,2,0:T(8,128)(2,1)S(1)}, u32[]{:S(2)}) copy-start(bf16[1,1024,1024]{1,2,0:T(8,128)(2,1)S(1)} %copy.135) | copy-start | bytes 6291460
  812.6 102.5 %reduce-scatter.10.cloned.1.call-start = ((), (), s32[]{:S(2)}) async-start(), calls=%async_computation.14 | async-start | bytes 12582912 | tf_op jit(solution)/shard_map/reduce_scatter | solution.py:214
  961.2 88.9 %all-to-all-start.3 = ((bf16[16,2,65536]{2,1,0:T(2,128)(2,1)}), bf16[16,2,65536]{2,1,0:T(2,128)(2,1)}, u32[]{:S(2)}, u32[]{:S(2)}) async-start(bf16[16,2,65536]{2,1,0:T(2,128)(2,1)} %reshape.460), calls=%async_computation.5 | async-start | bytes 8388608 | tf_op jit(solution)/shard_map/all_to_all | solution.py:218
  968.3 530.7 %reduce-scatter.16.cloned.1.call-start = ((), (), s32[]{:S(2)}) async-start(), calls=%async_computation.17 | async-start | bytes 540672
  971.8 681.4 %reduce-scatter.14.cloned.1.call-start = ((), (), s32[]{:S(2)}) async-start(), calls=%async_computation.16 | async-start | bytes 4325376 | tf_op jit(solution)/shard_map/reduce_scatter | solution.py:288
  1107.7 563.4 %reduce-scatter.12.cloned.1.call-start = ((), (), s32[]{:S(2)}) async-start(), calls=%async_computation.15 | async-start | bytes 12976128 | tf_op jit(solution)/shard_map/reduce_scatter | solution.py:283
  1109.4 35.3 %copy-start.36 = (f32[16,1024]{1,0:T(8,128)}, f32[16,1024]{1,0:T(8,128)S(1)}, u32[]{:S(2)}) copy-start(f32[16,1024]{1,0:T(8,128)S(1)} %get-tuple-element.741) | copy-start | bytes 196612 | tf_op jit(solution)/shard_map/while
  1109.4 35.3 %copy-start.45 = (f32[16,1024]{1,0:T(8,128)}, f32[16,1024]{1,0:T(8,128)S(1)}, u32[]{:S(2)}) copy-start(f32[16,1024]{1,0:T(8,128)S(1)} %get-tuple-element.739) | copy-start | bytes 196612 | tf_op jit(solution)/shard_map/while
  1195.4 35.4 %copy-start.36 = (f32[16,1024]{1,0:T(8,128)}, f32[16,1024]{1,0:T(8,128)S(1)}, u32[]{:S(2)}) copy-start(f32[16,1024]{1,0:T(8,128)S(1)} %get-tuple-element.741) | copy-start | bytes 196612 | tf_op jit(solution)/shard_map/while
  1195.4 35.4 %copy-start.45 = (f32[16,1024]{1,0:T(8,128)}, f32[16,1024]{1,0:T(8,128)S(1)}, u32[]{:S(2)}) copy-start(f32[16,1024]{1,0:T(8,128)S(1)} %get-tuple-element.739) | copy-start | bytes 196612 | tf_op jit(solution)/shard_map/while
  1283.9 35.3 %copy-start.36 = (f32[16,1024]{1,0:T(8,128)}, f32[16,1024]{1,0:T(8,128)S(1)}, u32[]{:S(2)}) copy-start(f32[16,1024]{1,0:T(8,128)S(1)} %get-tuple-element.741) | copy-start | bytes 196612 | tf_op jit(solution)/shard_map/while
  1283.9 35.3 %copy-start.45 = (f32[16,1024]{1,0:T(8,128)}, f32[16,1024]{1,0:T(8,128)S(1)}, u32[]{:S(2)}) copy-start(f32[16,1024]{1,0:T(8,128)S(1)} %get-tuple-element.739) | copy-start | bytes 196612 | tf_op jit(solution)/shard_map/while
  1372.1 35.2 %copy-start.36 = (f32[16,1024]{1,0:T(8,128)}, f32[16,1024]{1,0:T(8,128)S(1)}, u32[]{:S(2)}) copy-start(f32[16,1024]{1,0:T(8,128)S(1)} %get-tuple-element.741) | copy-start | bytes 196612 | tf_op jit(solution)/shard_map/while
  1372.1 35.2 %copy-start.45 = (f32[16,1024]{1,0:T(8,128)}, f32[16,1024]{1,0:T(8,128)S(1)}, u32[]{:S(2)}) copy-start(f32[16,1024]{1,0:T(8,128)S(1)} %get-tuple-element.739) | copy-start | bytes 196612 | tf_op jit(solution)/shard_map/while
  1466.4 12.5 collective-permute-start.1
  (86 other events, 595.7 us)
Sparse Core Ops, SparseCore 0:
  9.6 19.4 all-gather.12
  48.4 11.8 all-gather.14
  415.9 18.2 all-gather.16
  487.4 17.9 reduce-scatter.7
  812.7 18.2 all-gather.18
  897.1 17.9 reduce-scatter.9
  971.9 179.9 reduce-scatter.15
  1154.8 147.1 reduce-scatter.13
  1497.2 173.8 reduce-scatter.11
where the time goes:
time: 1690 us; the launch traced here: 1680 us
  matrix products  609 us (36%)
  blocking collectives  294 us (17%)
  local copies, waits for them, and re-layouts  287 us (17%)
  waiting for transfers between devices  255 us (15%)
  other arithmetic  192 us (11%)
  starting transfers between devices  20 us (1%)
    unnamed x161, local copies, waits for them, and re-layouts  122 us
    all_to_all x1, blocking collectives, body(): lax.all_to_all(dispatch(d_expert_value), 'expert', split_axis=0, concat_a...  114 us
    all_to_all x1, blocking collectives, body(): lax.all_to_all(dispatch(mixed_low), 'expert', split_axis=0, concat_axis=1...  101 us
    dot_general x4, matrix products, backward_block(): jnp.einsum('qhd,khd->hqk', d_context_heads, value_heads, preferred_elemen...  82.9 us
    all_to_all x1, waiting for transfers between devices, body(): lax.all_to_all(d_rows, 'expert', split_axis=1, concat_axis=0, tiled=True)  78.2 us
    all_to_all x1, waiting for transfers between devices, body(): lax.all_to_all(expert_rows, 'expert', split_axis=1, concat_axis=0, tiled=...  77.5 us
    dot_general x4, matrix products, forward_block(): jnp.einsum('hqk,khd->hqd', weights.astype(jnp.bfloat16), value_heads, pre...  67.7 us
    dot_general x4, matrix products, backward_block(): jnp.einsum('hqk,qhd->khd', probs_part.astype(jnp.bfloat16), d_context_hea...  62 us
  transfers between devices with their start and end apart: 13, of which 8 were waited for; matrix products, arithmetic and copies ran while one was open for 46% of the time, Pallas kernels for 0%

commit v1 on v0

v1 whole, which is shorter than its diff:
```python
from functools import partial

import jax
import jax.numpy as jnp
from jax import lax
from jax.experimental import pallas as pl
from jax.experimental.pallas import tpu as pltpu
from jax.sharding import PartitionSpec as P

HEAD_DIM = 64
NORM_EPSILON = 1e-05
MASK_FILL = -1e30
LOG2E = 1.4426950408889634
GELU_A = 0.7978845608028654
GELU_B = 0.044715
CHUNKS = 2
LANES = 128
BF16 = jnp.bfloat16
F32 = jnp.float32
VMEM_LIMIT = 56 << 20


def nn(left, right):
    return lax.dot_general(left, right, (((1,), (0,)), ((), ())), preferred_element_type=F32)


def nt(left, right):
    return lax.dot_general(left, right, (((1,), (1,)), ((), ())), preferred_element_type=F32)


def tn(left, right):
    return lax.dot_general(left, right, (((0,), (0,)), ((), ())), preferred_element_type=F32)


def lane_index(rows):
    return lax.broadcasted_iota(jnp.int32, (rows, LANES), 1)


def split_queries(queries):
    scaled = queries.astype(F32) * LOG2E
    high = scaled.astype(BF16).astype(F32)
    low = scaled - high
    first = lane_index(queries.shape[0]) < HEAD_DIM
    head_a = jnp.where(first, high, pltpu.roll(low, HEAD_DIM, 1)).astype(BF16)
    head_b = jnp.where(first, pltpu.roll(high, HEAD_DIM, 1), low).astype(BF16)
    return head_a, head_b


def twice(keys):
    wide = keys.astype(F32)
    rolled = pltpu.roll(wide, HEAD_DIM, 1)
    first = lane_index(keys.shape[0]) < HEAD_DIM
    return jnp.where(first, wide, rolled).astype(BF16), jnp.where(first, rolled, wide).astype(BF16)


def in_three(values):
    high = values.astype(BF16).astype(F32)
    rest = values - high
    middle = rest.astype(BF16).astype(F32)
    return high, middle, rest - middle


def three_columns(values, place):
    high, middle, low = in_three(values)
    return jnp.where(
        place == 0, high, jnp.where(place == 1, middle, jnp.where(place == 2, low, 0.0))
    )


def forward_kernel(
    block_q,
    block_k,
    scalars,
    q_ref,
    prev_k_ref,
    prev_v_ref,
    own_k_ref,
    own_v_ref,
    out_ref,
    lse_ref,
    key_aug,
    value_aug,
    query_aug,
    total,
    top,
):
    rows = q_ref.shape[0]
    has_prev, own_prefix = scalars[0], scalars[1]
    lane = lane_index(rows)
    first = lane < HEAD_DIM
    ones = jnp.where((lane & (HEAD_DIM - 1)) < 3, 1.0, 0.0).astype(BF16)
    head_a, head_b = split_queries(q_ref[...])
    query_aug[0, :, :LANES] = head_a
    query_aug[1, :, :LANES] = head_b

    def prepare(k_ref, v_ref, at):
        keys_a, keys_b = twice(k_ref[...])
        values = v_ref[...]
        one = jnp.ones_like(values)
        where = pl.ds(at, rows)
        key_aug[0, where, :LANES] = keys_a
        key_aug[1, where, :LANES] = keys_b
        key_aug[0, where, LANES:] = ones
        key_aug[1, where, LANES:] = ones
        value_aug[0, where] = jnp.where(first, values, one)
        value_aug[1, where] = jnp.where(first, one, values)

    @pl.when(has_prev > 0)
    def _():
        prepare(prev_k_ref, prev_v_ref, 0)

    prepare(own_k_ref, own_v_ref, rows)
    block_lane = lane_index(block_q)
    block_first = block_lane < HEAD_DIM
    place = block_lane & (HEAD_DIM - 1)
    key_blocks = rows // block_k
    for i in range(rows // block_q):
        here = slice(i * block_q, (i + 1) * block_q)
        seen = jnp.minimum(
            jnp.maximum(-(-(i + 1) * block_q // block_k), (own_prefix + block_k - 1) // block_k),
            key_blocks,
        )
        whole = jnp.minimum(jnp.maximum(i * block_q // block_k, own_prefix // block_k), seen)

        def over_keys(block):
            @pl.when(has_prev > 0)
            def _():
                for j in range(key_blocks):
                    block(j * block_k, False)

            def unmasked(j, carried):
                block(rows + j * block_k, False)
                return carried

            def masked(j, carried):
                block(rows + j * block_k, True)
                return carried

            lax.fori_loop(0, whole, unmasked, 0)
            lax.fori_loop(whole, seen, masked, 0)

        def allowed(at):
            key_pos = at - rows + lax.broadcasted_iota(jnp.int32, (block_q, block_k), 1)
            query_pos = i * block_q + lax.broadcasted_iota(jnp.int32, (block_q, block_k), 0)
            return key_pos <= jnp.maximum(query_pos, own_prefix - 1)

        top[...] = jnp.full_like(top, MASK_FILL)

        def find_top(at, masked):
            at = pl.multiple_of(at, block_k)
            visible = allowed(at) if masked else None
            for h in range(2):
                scores = nt(query_aug[h, here, :LANES], key_aug[h, pl.ds(at, block_k), :LANES])
                if masked:
                    scores = jnp.where(visible, scores, MASK_FILL)
                largest = top[h]
                for t in range(block_k // LANES):
                    largest = jnp.maximum(largest, scores[:, t * LANES : (t + 1) * LANES])
                top[h] = largest

        over_keys(find_top)
        maxima = []
        for h in range(2):
            maximum = jnp.max(top[h], axis=1, keepdims=True)
            maxima.append(maximum)
            columns = three_columns(jnp.broadcast_to(-maximum, (block_q, LANES)), place)
            mine = block_first if h == 0 else jnp.logical_not(block_first)
            query_aug[h, here, LANES:] = jnp.where(mine, columns, 0.0).astype(BF16)
        total[...] = jnp.zeros_like(total)

        def add_up(at, masked):
            at = pl.multiple_of(at, block_k)
            visible = allowed(at) if masked else None
            for h in range(2):
                scores = nt(query_aug[h, here, :], key_aug[h, pl.ds(at, block_k), :])
                if masked:
                    scores = jnp.where(visible, scores, MASK_FILL)
                total[h] += nn(jnp.exp2(scores).astype(BF16), value_aug[h, pl.ds(at, block_k), :])

        over_keys(add_up)
        sum_a, sum_b = total[0], total[1]
        weight = jnp.where(
            block_first, pltpu.roll(sum_a, HEAD_DIM, 1), pltpu.roll(sum_b, HEAD_DIM, 1)
        )
        out_ref[here, :] = (jnp.where(block_first, sum_a, sum_b) / weight).astype(BF16)
        lse_ref[here, :] = jnp.where(block_first, maxima[0], maxima[1]) + jnp.log2(weight)


def attention_forward(scalars, queries, prev, own, block_q=1024, block_k=512):
    rows, width = queries.shape
    pairs = width // LANES

    def spec(offset):
        return pl.BlockSpec((rows, LANES), lambda h, scalars: (0, h + offset))

    return pl.pallas_call(
        partial(forward_kernel, block_q, block_k),
        grid_spec=pltpu.PrefetchScalarGridSpec(
            num_scalar_prefetch=1,
            grid=(pairs,),
            in_specs=[spec(0), spec(0), spec(pairs), spec(0), spec(pairs)],
            out_specs=[spec(0), spec(0)],
            scratch_shapes=[
                pltpu.VMEM((2, 2 * rows, 2 * LANES), BF16),
                pltpu.VMEM((2, 2 * rows, LANES), BF16),
                pltpu.VMEM((2, rows, 2 * LANES), BF16),
                pltpu.VMEM((2, block_q, LANES), F32),
                pltpu.VMEM((2, block_q, LANES), F32),
            ],
        ),
        out_shape=[
            jax.ShapeDtypeStruct((rows, width), BF16),
            jax.ShapeDtypeStruct((rows, width), F32),
        ],
        compiler_params=pltpu.CompilerParams(vmem_limit_bytes=VMEM_LIMIT),
        cost_estimate=pl.CostEstimate(
            flops=40 * rows * rows * width,
            bytes_accessed=16 * rows * width,
            transcendentals=2 * rows * rows * width // HEAD_DIM,
        ),
        name="attention_forward",
    )(scalars, queries, prev, prev, own, own)


def backward_kernel(
    block_q,
    block_k,
    scalars,
    q_ref,
    prev_k_ref,
    prev_v_ref,
    own_k_ref,
    own_v_ref,
    out_ref,
    lse_ref,
    grad_ref,
    dq_ref,
    prev_grad_ref,
    own_grad_ref,
    key_aug,
    key_zero,
    value_aug,
    query_aug,
    query_zero,
    grad_aug,
    grad_zero,
    dq_total,
    dk_total,
    dv_total,
):
    rows = q_ref.shape[0]
    has_prev, own_prefix = scalars[0], scalars[1]
    lane = lane_index(rows)
    first = lane < HEAD_DIM
    place = lane & (HEAD_DIM - 1)
    zero = jnp.zeros((rows, LANES), BF16)
    ones = jnp.where(place < 3, 1.0, 0.0).astype(BF16)
    queries = q_ref[...]
    head_a, head_b = split_queries(queries)
    columns = three_columns(-lse_ref[...], place)
    query_aug[0, :, :LANES] = head_a
    query_aug[1, :, :LANES] = head_b
    query_aug[0, :, LANES:] = jnp.where(first, columns, 0.0).astype(BF16)
    query_aug[1, :, LANES:] = jnp.where(first, 0.0, columns).astype(BF16)
    query_zero[0] = jnp.where(first, queries, zero)
    query_zero[1] = jnp.where(first, zero, queries)
    grads = grad_ref[...]
    grad_zero[0] = jnp.where(first, grads, zero)
    grad_zero[1] = jnp.where(first, zero, grads)
    products = grads.astype(F32) * out_ref[...].astype(F32)
    delta_a = jnp.sum(jnp.where(first, products, 0.0), axis=1, keepdims=True)
    delta_b = jnp.sum(jnp.where(first, 0.0, products), axis=1, keepdims=True)
    columns = three_columns(jnp.where(first, -delta_b, -delta_a), place).astype(BF16)
    grad_aug[0] = jnp.where(first, grads, columns)
    grad_aug[1] = jnp.where(first, columns, grads)

    def prepare(k_ref, v_ref, at):
        keys, values = k_ref[...], v_ref[...]
        keys_a, keys_b = twice(keys)
        where = pl.ds(at, rows)
        key_aug[0, where, :LANES] = keys_a
        key_aug[1, where, :LANES] = keys_b
        key_aug[0, where, LANES:] = ones
        key_aug[1, where, LANES:] = ones
        key_zero[0, where] = jnp.where(first, keys, zero)
        key_zero[1, where] = jnp.where(first, zero, keys)
        value_aug[0, where] = jnp.where(first, values, ones)
        value_aug[1, where] = jnp.where(first, ones, values)

    @pl.when(has_prev > 0)
    def _():
        prepare(prev_k_ref, prev_v_ref, 0)

    prepare(own_k_ref, own_v_ref, rows)
    dq_total[...] = jnp.zeros_like(dq_total)

    def block(at, i, masked):
        keys_at = pl.ds(pl.multiple_of(at, block_k), block_k)
        start = pl.multiple_of(i * block_q, block_q)
        queries_at = pl.ds(start, block_q)
        if masked:
            key_pos = at - rows + lax.broadcasted_iota(jnp.int32, (block_k, block_q), 0)
            query_pos = start + lax.broadcasted_iota(jnp.int32, (block_k, block_q), 1)
            visible = key_pos <= jnp.maximum(query_pos, own_prefix - 1)
        probs, d_scores = [], []
        for h in range(2):
            scores = nt(key_aug[h, keys_at, :], query_aug[h, queries_at, :])
            if masked:
                scores = jnp.where(visible, scores, MASK_FILL)
            part = jnp.exp2(scores)
            centered = nt(value_aug[h, keys_at, :], grad_aug[h, queries_at, :])
            d_scores.append((part * centered).astype(BF16))
            probs.append(part.astype(BF16))
        dv_total[...] += nn(probs[0], grad_zero[0, queries_at, :]) + nn(
            probs[1], grad_zero[1, queries_at, :]
        )
        dk_total[...] += nn(d_scores[0], query_zero[0, queries_at, :]) + nn(
            d_scores[1], query_zero[1, queries_at, :]
        )
        dq_total[queries_at, :] += tn(d_scores[0], key_zero[0, keys_at, :]) + tn(
            d_scores[1], key_zero[1, keys_at, :]
        )

    query_blocks = rows // block_q

    def clear():
        dk_total[...] = jnp.zeros_like(dk_total)
        dv_total[...] = jnp.zeros_like(dv_total)

    def put(ref, j):
        here = slice(j * block_k, (j + 1) * block_k)
        ref[0, here, :] = dk_total[...].astype(BF16)
        ref[1, here, :] = dv_total[...].astype(BF16)

    @pl.when(has_prev > 0)
    def _():
        for j in range(rows // block_k):
            clear()

            def step(i, carried):
                block(j * block_k, i, False)
                return carried

            lax.fori_loop(0, query_blocks, step, 0)
            put(prev_grad_ref, j)

    @pl.when(has_prev == 0)
    def _():
        prev_grad_ref[0] = zero
        prev_grad_ref[1] = zero

    for j in range(rows // block_k):
        clear()
        inside = own_prefix >= (j + 1) * block_k
        reached = own_prefix > j * block_k
        first_whole = jnp.where(inside, 0, min(query_blocks, -(-((j + 1) * block_k - 1) // block_q)))
        first_seen = jnp.where(reached, 0, min(query_blocks, j * block_k // block_q))

        def masked(i, carried):
            block(rows + j * block_k, i, True)
            return carried

        def unmasked(i, carried):
            block(rows + j * block_k, i, False)
            return carried

        lax.fori_loop(first_seen, first_whole, masked, 0)
        lax.fori_loop(first_whole, query_blocks, unmasked, 0)
        put(own_grad_ref, j)
    dq_ref[...] = (dq_total[...] * (HEAD_DIM**-0.5)).astype(BF16)


def attention_backward(scalars, queries, prev, own, out, lse, grads, block_q=512, block_k=512):
    rows, width = queries.shape
    pairs = width // LANES

    def spec(offset):
        return pl.BlockSpec((rows, LANES), lambda h, scalars: (0, h + offset))

    both = pl.BlockSpec((2, rows, LANES), lambda h, scalars: (0, 0, h))
    return pl.pallas_call(
        partial(backward_kernel, block_q, block_k),
        grid_spec=pltpu.PrefetchScalarGridSpec(
            num_scalar_prefetch=1,
            grid=(pairs,),
            in_specs=[spec(0), spec(0), spec(pairs), spec(0), spec(pairs)] + [spec(0)] * 3,
            out_specs=[spec(0), both, both],
            scratch_shapes=[
                pltpu.VMEM((2, 2 * rows, 2 * LANES), BF16),
                pltpu.VMEM((2, 2 * rows, LANES), BF16),
                pltpu.VMEM((2, 2 * rows, LANES), BF16),
                pltpu.VMEM((2, rows, 2 * LANES), BF16),
                pltpu.VMEM((2, rows, LANES), BF16),
                pltpu.VMEM((2, rows, LANES), BF16),
                pltpu.VMEM((2, rows, LANES), BF16),
                pltpu.VMEM((rows, LANES), F32),
                pltpu.VMEM((block_k, LANES), F32),
                pltpu.VMEM((block_k, LANES), F32),
            ],
        ),
        out_shape=[
            jax.ShapeDtypeStruct((rows, width), BF16),
            jax.ShapeDtypeStruct((2, rows, width), BF16),
            jax.ShapeDtypeStruct((2, rows, width), BF16),
        ],
        compiler_params=pltpu.CompilerParams(vmem_limit_bytes=VMEM_LIMIT),
        cost_estimate=pl.CostEstimate(
            flops=60 * rows * rows * width,
            bytes_accessed=26 * rows * width,
            transcendentals=2 * rows * rows * width // HEAD_DIM,
        ),
        name="attention_backward",
    )(scalars, queries, prev, prev, own, own, out, lse, grads)


def expert_kernel(
    experts,
    block_r,
    scalars,
    rows_ref,
    cot_ref,
    w_in_ref,
    w_down_ref,
    router_ref,
    y_ref,
    dm_ref,
    act_ref,
    du_ref,
    dy_ref,
    dz_ref,
    y_total,
    dm_total,
    probs,
):
    step = pl.program_id(0)
    blocks = rows_ref.shape[0] // block_r
    lane = lane_index(block_r)
    is_mine = lane == scalars[0]

    def over_rows(work):
        def one(b, carried):
            work(pl.ds(pl.multiple_of(b * block_r, block_r), block_r))
            return carried

        lax.fori_loop(0, blocks, one, 0)

    @pl.when(step == 0)
    def _():
        def gate(here):
            logits = nt(rows_ref[here, :], router_ref[...])
            logits = jnp.where(lane < experts, logits, MASK_FILL)
            spread = jnp.exp(logits - jnp.max(logits, axis=1, keepdims=True))
            part = spread / jnp.sum(spread, axis=1, keepdims=True)
            probs[here, :] = part
            mine = jnp.sum(jnp.where(is_mine, part, 0.0), axis=1, keepdims=True)
            dy_ref[here, :] = (mine * cot_ref[here, :].astype(F32)).astype(BF16)
            y_total[here, :] = jnp.zeros((block_r, y_total.shape[1]), F32)
            dm_total[here, :] = jnp.zeros((block_r, dm_total.shape[1]), F32)

        over_rows(gate)

    def hidden_block(here):
        u = nn(rows_ref[here, :], w_in_ref[...])
        d_act = nt(dy_ref[here, :], w_down_ref[...])
        square = u * u
        bend = jnp.tanh(u * (GELU_A + (GELU_A * GELU_B) * square))
        half = 0.5 + 0.5 * bend
        act = (u * half).astype(BF16)
        slope = half + (0.5 * u) * (1.0 - bend * bend) * (
            GELU_A + (3.0 * GELU_A * GELU_B) * square
        )
        du = (d_act * slope).astype(BF16)
        act_ref[here, :] = act
        du_ref[here, :] = du
        y_total[here, :] += nn(act, w_down_ref[...])
        dm_total[here, :] += nt(du, w_in_ref[...])

    over_rows(hidden_block)

    @pl.when(step == pl.num_programs(0) - 1)
    def _():
        def finish(here):
            y = y_total[here, :].astype(BF16)
            y_ref[here, :] = y
            d_gate = jnp.sum(cot_ref[here, :].astype(F32) * y.astype(F32), axis=1, keepdims=True)
            part = probs[here, :]
            mine = jnp.sum(jnp.where(is_mine, part, 0.0), axis=1, keepdims=True)
            dz = ((d_gate * mine) * (jnp.where(is_mine, 1.0, 0.0) - part)).astype(BF16)
            dz = jnp.where(lane < experts, dz, jnp.zeros_like(dz))
            dz_ref[here, :] = dz
            dm_ref[here, :] = (dm_total[here, :] + nn(dz, router_ref[...])).astype(BF16)

        over_rows(finish)


def run_expert(scalars, rows_in, cots, w_in, w_down, router, experts, block_h=512, block_r=256):
    rows, width = rows_in.shape
    half = w_in.shape[2]
    per_half = half // block_h
    whole = pl.BlockSpec((rows, width), lambda j, s: (0, 0))
    hidden = pl.BlockSpec((rows, block_h), lambda j, s: (0, j))

    def which(j, s):
        return lax.rem(j // per_half + s[1], 2)

    return pl.pallas_call(
        partial(expert_kernel, experts, block_r),
        grid_spec=pltpu.PrefetchScalarGridSpec(
            num_scalar_prefetch=1,
            grid=(2 * per_half,),
            in_specs=[
                whole,
                whole,
                pl.BlockSpec(
                    (None, width, block_h), lambda j, s: (which(j, s), 0, lax.rem(j, per_half))
                ),
                pl.BlockSpec(
                    (None, block_h, width), lambda j, s: (which(j, s), lax.rem(j, per_half), 0)
                ),
                pl.BlockSpec((LANES, width), lambda j, s: (0, 0)),
            ],
            out_specs=[
                whole,
                whole,
                hidden,
                hidden,
                whole,
                pl.BlockSpec((rows, LANES), lambda j, s: (0, 0)),
            ],
            scratch_shapes=[
                pltpu.VMEM((rows, width), F32),
                pltpu.VMEM((rows, width), F32),
                pltpu.VMEM((rows, LANES), F32),
            ],
        ),
        out_shape=[
            jax.ShapeDtypeStruct((rows, width), BF16),
            jax.ShapeDtypeStruct((rows, width), BF16),
            jax.ShapeDtypeStruct((rows, 2 * half), BF16),
            jax.ShapeDtypeStruct((rows, 2 * half), BF16),
            jax.ShapeDtypeStruct((rows, width), BF16),
            jax.ShapeDtypeStruct((rows, LANES), BF16),
        ],
        compiler_params=pltpu.CompilerParams(vmem_limit_bytes=VMEM_LIMIT),
        cost_estimate=pl.CostEstimate(
            flops=16 * rows * width * half,
            bytes_accessed=8 * width * half + 12 * rows * width + 8 * rows * half,
            transcendentals=2 * rows * half,
        ),
        name="expert_rows",
    )(scalars, rows_in, cots, w_in, w_down, router)


def layer_norm(values, norm_gain, norm_bias):
    center = values - jnp.mean(values, axis=-1, keepdims=True)
    inv_std = lax.rsqrt(jnp.mean(center * center, axis=-1, keepdims=True) + NORM_EPSILON)
    normed = center * inv_std
    return (normed * norm_gain + norm_bias, normed, inv_std)


def norm_backward(grad_out, normed, inv_std, norm_gain):
    scaled = grad_out * norm_gain
    return inv_std * (
        scaled
        - jnp.mean(scaled, axis=-1, keepdims=True)
        - normed * jnp.mean(scaled * normed, axis=-1, keepdims=True)
    )


def swapped(array):
    return lax.ppermute(array, "fsdp", [(0, 1), (1, 0)])


def exchanged(array):
    return lax.all_to_all(array, "expert", split_axis=0, concat_axis=0, tiled=True)


def body(
    tokens,
    out_grad,
    routes,
    prefix,
    ln1_gain,
    ln1_bias,
    w_qkv,
    q_bias,
    v_bias,
    attention_output_weight,
    attention_output_bias,
    ln2_gain,
    ln2_bias,
    w_router,
    moe_bias,
    w_in,
    w_down,
):
    experts = lax.axis_size("expert")
    my_expert = lax.axis_index("expert")
    my_half = lax.axis_index("fsdp")
    is_first = my_half == 0
    rows, width = tokens.shape[1], tokens.shape[2]
    half_width = width // 2
    slots = max(2, 2 * rows // experts) // CHUNKS
    chunk_rows = experts * slots

    def in_order(own, other, axis):
        return jnp.where(
            is_first,
            jnp.concatenate([own, other], axis=axis),
            jnp.concatenate([other, own], axis=axis),
        )

    small = jnp.concatenate(
        [
            jnp.stack(
                [
                    ln1_gain,
                    ln1_bias,
                    q_bias,
                    v_bias,
                    attention_output_bias,
                    ln2_gain,
                    ln2_bias,
                    moe_bias,
                ]
            ),
            w_router.T,
        ],
        axis=0,
    )
    small = in_order(small, swapped(small), 1)
    vectors = small[:8].astype(F32)
    norm1_gain, norm1_bias, query_bias, value_bias = (vectors[i] for i in range(4))
    output_bias, norm2_gain, norm2_bias, expert_bias = (vectors[i] for i in range(4, 8))
    router_t = small[8:]
    qkv_weight = in_order(w_qkv, swapped(w_qkv), 0)
    out_weight = lax.all_gather(attention_output_weight, "fsdp", axis=0, tiled=True)
    w_in_both = lax.all_gather(w_in[0], "fsdp", axis=0, tiled=False)
    w_down_both = lax.all_gather(w_down[0], "fsdp", axis=0, tiled=False)

    token_route = routes[0, :, 0]
    one_hot = token_route[:, None] == jnp.arange(experts, dtype=jnp.int32)[None, :]
    row_ids = jnp.arange(rows, dtype=jnp.int32)
    earlier_same = nn(
        (row_ids[None, :] < row_ids[:, None]).astype(BF16), one_hot.astype(BF16)
    )
    slot_index = jnp.sum(jnp.where(one_hot, earlier_same, 0.0), axis=-1).astype(jnp.int32)
    chunk_of = slot_index // slots
    place_in = token_route * slots + slot_index % slots
    buffer_ids = jnp.arange(chunk_rows, dtype=jnp.int32)

    def dispatch(row_values, chunk):
        place = jnp.where(chunk_of == chunk, place_in, -1)
        picked = nn((buffer_ids[:, None] == place[None, :]).astype(BF16), row_values)
        return exchanged(picked.astype(BF16).reshape(experts, slots, width)).reshape(
            chunk_rows, width
        )

    def give_back(buffers):
        got = [exchanged(b.reshape(experts, slots, width)).reshape(chunk_rows, width) for b in buffers]
        total = None
        for chunk in range(CHUNKS):
            place = jnp.where(chunk_of == chunk, place_in, -1)
            part = nn((place[:, None] == buffer_ids[None, :]).astype(BF16), got[chunk])
            total = part if total is None else total + part
        return total

    cot_rows = [dispatch(out_grad[0], chunk) for chunk in range(CHUNKS)]

    residual = tokens[0].astype(F32)
    norm1_out, normed1, inv_std1 = layer_norm(residual, norm1_gain, norm1_bias)
    attn_in = norm1_out.astype(BF16)
    key_value = (
        nn(attn_in, qkv_weight[:, width:])
        + jnp.concatenate([jnp.zeros_like(value_bias), value_bias])
    ).astype(BF16)
    prev_key_value = lax.ppermute(key_value, "fsdp", [(0, 1)])
    queries = ((nn(attn_in, qkv_weight[:, :width]) + query_bias) * (HEAD_DIM**-0.5)).astype(BF16)
    scalars = jnp.stack([my_half, prefix[0] - my_half * rows]).astype(jnp.int32)
    context, lse = attention_forward(scalars, queries, prev_key_value, key_value)
    hidden = residual + (nn(context, out_weight) + output_bias)
    norm2_out, normed2, inv_std2 = layer_norm(hidden, norm2_gain, norm2_bias)
    mixed = norm2_out.astype(BF16)

    mixed_rows = [dispatch(mixed, chunk) for chunk in range(CHUNKS)]
    router_pad = jnp.pad(router_t, ((0, LANES - experts), (0, 0)))
    expert_scalars = jnp.stack([my_expert, my_half]).astype(jnp.int32)
    done = [
        run_expert(
            expert_scalars, mixed_rows[c], cot_rows[c], w_in_both, w_down_both, router_pad, experts
        )
        for c in range(CHUNKS)
    ]
    d_mixed = give_back([d[1] for d in done])

    hidden_half = w_in.shape[2]

    def both_chunks(pick_left, pick_right):
        total = None
        for c in range(CHUNKS):
            part = tn(pick_left(c), pick_right(c))
            total = part if total is None else total + part
        return total

    own, other = slice(0, hidden_half), slice(hidden_half, 2 * hidden_half)
    d_in_other = both_chunks(lambda c: mixed_rows[c], lambda c: done[c][3][:, other])
    d_down_other = both_chunks(lambda c: done[c][2][:, other], lambda c: done[c][4])
    d_in_got = swapped(d_in_other.astype(BF16))
    d_down_got = swapped(d_down_other.astype(BF16))
    d_w_in = both_chunks(lambda c: mixed_rows[c], lambda c: done[c][3][:, own]) + d_in_got
    d_w_down = both_chunks(lambda c: done[c][2][:, own], lambda c: done[c][4]) + d_down_got
    d_router = both_chunks(lambda c: mixed_rows[c], lambda c: done[c][5])

    out_cot = out_grad[0].astype(F32)
    d_expert_bias = jnp.sum(out_cot, axis=0)
    d_norm2_gain = jnp.sum(d_mixed * normed2, axis=0)
    d_norm2_bias = jnp.sum(d_mixed, axis=0)
    d_hidden = out_cot + norm_backward(d_mixed, normed2, inv_std2, norm2_gain)
    d_attn = d_hidden.astype(BF16)
    d_output_bias = jnp.sum(d_attn.astype(F32), axis=0)
    d_context = nt(d_attn, out_weight).astype(BF16)

    logits = nt(mixed, router_t)
    router_probs = jax.nn.softmax(logits, axis=-1)
    gate_value = jnp.sum(jnp.where(one_hot, router_probs, 0.0), axis=-1)
    expert_value = give_back([d[0] for d in done])
    output = hidden + gate_value[:, None] * expert_value + expert_bias

    def halves(columns):
        left, right = columns[:, :half_width], columns[:, half_width:]
        return jnp.where(is_first, left, right), jnp.where(is_first, right, left)

    def row_halves(matrix):
        top, bottom = matrix[:half_width], matrix[half_width:]
        return jnp.where(is_first, top, bottom), jnp.where(is_first, bottom, top)

    def scattered(own_part, other_part):
        pair = own_part + swapped(other_part.astype(BF16)).astype(F32)
        blocks = pair.astype(BF16).reshape(experts, half_width // experts, pair.shape[1])
        return jnp.sum(exchanged(blocks).astype(F32), axis=0)

    def as_columns(pieces):
        packed = jnp.concatenate(pieces, axis=1)
        return jnp.pad(packed, ((0, 0), (0, -packed.shape[1] % LANES)))

    context_own, context_other = halves(context)
    extra_own, extra_other = row_halves(
        as_columns(
            [
                d_router[:, :experts],
                jnp.stack([d_expert_bias, d_norm2_gain, d_norm2_bias, d_output_bias], axis=1),
            ]
        )
    )
    sum_out = scattered(
        jnp.concatenate([tn(context_own, d_attn), extra_own], axis=1),
        jnp.concatenate([tn(context_other, d_attn), extra_other], axis=1),
    )

    d_query, prev_grad, own_grad = attention_backward(
        scalars, queries, prev_key_value, key_value, context, lse, d_context
    )
    returned = lax.ppermute(prev_grad, "fsdp", [(1, 0)])
    in_own, in_other = halves(attn_in)
    sum_query = scattered(tn(in_own, d_query), tn(in_other, d_query))
    d_key_value = (own_grad.astype(F32) + returned.astype(F32)).astype(BF16)
    d_key, d_value = d_key_value[0], d_key_value[1]
    sum_key = scattered(tn(in_own, d_key), tn(in_other, d_key))
    sum_value = scattered(tn(in_own, d_value), tn(in_other, d_value))
    d_norm1_out = (
        nt(d_query, qkv_weight[:, :width])
        + nt(d_key, qkv_weight[:, width : 2 * width])
        + nt(d_value, qkv_weight[:, 2 * width :])
    )
    d_tokens = (d_hidden + norm_backward(d_norm1_out, normed1, inv_std1, norm1_gain)).astype(BF16)
    last_own, last_other = row_halves(
        as_columns(
            [
                jnp.stack(
                    [
                        jnp.sum(d_query.astype(F32), axis=0),
                        jnp.sum(d_value.astype(F32), axis=0),
                        jnp.sum(d_norm1_out * normed1, axis=0),
                        jnp.sum(d_norm1_out, axis=0),
                    ],
                    axis=1,
                )
            ]
        )
    )
    sum_last = scattered(last_own, last_other)
    return (
        output.astype(BF16)[None],
        d_tokens[None],
        sum_last[:, 2],
        sum_last[:, 3],
        jnp.concatenate([sum_query, sum_key, sum_value], axis=1),
        sum_last[:, 0],
        sum_last[:, 1],
        sum_out[:, :width],
        sum_out[:, width + experts + 3],
        sum_out[:, width + experts + 1],
        sum_out[:, width + experts + 2],
        sum_out[:, width : width + experts],
        sum_out[:, width + experts],
        d_w_in[None],
        d_w_down[None],
    )


def solution(mesh):
    vector = P(("fsdp", "expert"))
    matrix = P(("fsdp", "expert"), None)
    tokens = P("expert", "fsdp", None)
    return jax.shard_map(
        body,
        mesh=mesh,
        in_specs=(
            tokens,
            tokens,
            tokens,
            P("expert"),
            P("fsdp"),
            P("fsdp"),
            P("fsdp", None),
            P("fsdp"),
            P("fsdp"),
            P("fsdp", None),
            P("fsdp"),
            P("fsdp"),
            P("fsdp"),
            P("fsdp", None),
            P("fsdp"),
            P("expert", None, "fsdp"),
            P("expert", "fsdp", None),
        ),
        out_specs=(
            tokens,
            tokens,
            vector,
            vector,
            matrix,
            vector,
            vector,
            matrix,
            vector,
            vector,
            vector,
            matrix,
            vector,
            P("expert", None, "fsdp"),
            P("expert", "fsdp", None),
        ),
        check_vma=False,
    )
```

time: 1690 us -> 770 us (0.46)
  matrix products: 609 us -> 191 us
  blocking collectives: 294 us -> 0 us
  local copies, waits for them, and re-layouts: 287 us -> 11 us
  Pallas kernels: 0 us -> 230 us
  waiting for transfers between devices: 255 us -> 84.2 us
  starting transfers between devices: 20 us -> 190 us
  other arithmetic: 192 us -> 40 us
    dot_general x42 -> x35, matrix products: 607 us -> 191 us  [the longest x18 105 us: tn(): lax.dot_general(left, right, (((0,), (0,)), ((), ())), preferred_element_...]
    pallas_call x0 -> x4, Pallas kernels: none -> 230 us  [the longest x2 114 us: run_expert(): pl.pallas_call(partial(expert_kernel, experts, block_r), grid_spec=pltpu....]
    all_to_all x2 -> x0, blocking collectives: 215 us -> none  [the longest x1 114 us: body(): lax.all_to_all(dispatch(d_expert_value), 'expert', split_axis=0, concat_a...]
    unnamed x161 -> x113, local copies, waits for them, and re-layouts: 122 us -> 6.18 us
    ppermute x2 -> x11, starting transfers between devices: 5.7 us -> 97.4 us  [the longest x9 92.1 us: swapped(): return lax.ppermute(array, 'fsdp', [(0, 1), (1, 0)])]
    all_to_all x2 -> x13, starting transfers between devices: 14 us -> 92.3 us  [exchanged(): lax.all_to_all(array, 'expert', split_axis=0, concat_axis=0, tiled=True)]
    all_to_all x2 -> x13, waiting for transfers between devices: 156 us -> 79.3 us  [exchanged(): lax.all_to_all(array, 'expert', split_axis=0, concat_axis=0, tiled=True)]
    reduce_sum x12 -> x9, other arithmetic: 71.7 us -> 8.72 us  [the longest x5 3.88 us: scattered(): return jnp.sum(exchanged(blocks).astype(F32), axis=0)]
  transfers between devices with their start and end apart: 13 -> 27, of which waited for: 8 -> 8; matrix products, arithmetic and copies ran while one was open for 46% -> 31% of each run, Pallas kernels for 0% -> 30%
where the time goes in v1:
time: 770 us; the launch traced here: 762 us
  Pallas kernels  230 us (30%)
  matrix products  191 us (25%)
  starting transfers between devices  190 us (25%)
  waiting for transfers between devices  84.2 us (11%)
  other arithmetic  40 us (5%)
  between operations  15.8 us (2%)
  local copies, waits for them, and re-layouts  11 us (1%)
    pallas_call x2, Pallas kernels, run_expert(): pl.pallas_call(partial(expert_kernel, experts, block_r), grid_spec=pltpu....  114 us
    dot_general x18, matrix products, tn(): lax.dot_general(left, right, (((0,), (0,)), ((), ())), preferred_element_...  105 us
    all_to_all x13, starting transfers between devices, exchanged(): lax.all_to_all(array, 'expert', split_axis=0, concat_axis=0, tiled=True)  92.3 us
    ppermute x9, starting transfers between devices, swapped(): return lax.ppermute(array, 'fsdp', [(0, 1), (1, 0)])  92.1 us
    all_to_all x13, waiting for transfers between devices, exchanged(): lax.all_to_all(array, 'expert', split_axis=0, concat_axis=0, tiled=True)  79.3 us
    pallas_call x1, Pallas kernels, attention_backward(): pl.pallas_call(partial(backward_kernel, block_q, block_k), grid_spec=pltp...  68.1 us
    dot_general x12, matrix products, nn(): lax.dot_general(left, right, (((1,), (0,)), ((), ())), preferred_element_...  58.7 us
    pallas_call x1, Pallas kernels, attention_forward(): pl.pallas_call(partial(forward_kernel, block_q, block_k), grid_spec=pltpu...  47.9 us
  transfers between devices with their start and end apart: 27, of which 8 were waited for; matrix products, arithmetic and copies ran while one was open for 31% of the time, Pallas kernels for 30%

profile of v1, /device:TPU:0, one launch (start us, length us, event | category | flops | bytes accessed | tf_op | source)
XLA Modules:
  0.0 761.8 jit_solution(10318319990860488169)
XLA Ops:
  16.0 6.3 maximum_select_fusion
  36.2 8.3 %all-to-all-start.1 = ((bf16[16,64,1024]{2,1,0:T(8,128)(2,1)}), bf16[16,64,1024]{2,1,0:T(8,128)(2,1)}, u32[]{:S(2)}, u32[]{:S(2)}) async-start(bf16[16,64,1024]{2,1,0:T(8,128)(2,1)} %bitcast.173), calls=%async_computation.1 | async-start | bytes 4194304 | tf_op jit(solution)/shard_map/all_to_all | solution.py:575
  57.1 28.3 %all-to-all-done.1 = bf16[16,64,1024]{2,1,0:T(8,128)(2,1)} async-done(((bf16[16,64,1024]{2,1,0:T(8,128)(2,1)}), bf16[16,64,1024]{2,1,0:T(8,128)(2,1)}, u32[]{:S(2)}, u32[]{:S(2)}) %all-to-all-start.1) | async-done | bytes 2097184 | tf_op jit(solution)/shard_map/all_to_all | solution.py:575
  85.4 9.8 %all-to-all-start.4 = ((bf16[16,64,1024]{2,1,0:T(8,128)(2,1)}), bf16[16,64,1024]{2,1,0:T(8,128)(2,1)}, u32[]{:S(2)}, u32[]{:S(2)}) async-start(bf16[16,64,1024]{2,1,0:T(8,128)(2,1)} %bitcast.171), calls=%async_computation.4 | async-start | bytes 4194304 | tf_op jit(solution)/shard_map/all_to_all | solution.py:575
  95.2 47.9 %attention_forward.1 = (bf16[1024,1024]{1,0:T(8,128)(2,1)}, f32[1024,1024]{1,0:T(8,128)}) custom-call(s32[2]{0:T(128)} %pad_add_fusion.scalars, bf16[1024,1024]{1,0:T(8,128)(2,1)} %multiply_convert_fusion.q_ref, bf16[1024,2048]{1,0:T(8,128)(2,1)} %collective-permute-done.2.prev_k_ref.prev_v_ref, ...), custom_call_target="tpu_custom_call" | custom-call | flops 42949672960 | bytes 16777216 | tf_op jit(solution)/shard_map/attention_forward/pallas_call | solution.py:196
  154.8 6.8 all-to-all-start.3
  171.0 16.3 %all-to-all-done.3 = bf16[16,64,1024]{2,1,0:T(8,128)(2,1)S(1)} async-done(((bf16[16,64,1024]{2,1,0:T(8,128)(2,1)}), bf16[16,64,1024]{2,1,0:T(8,128)(2,1)S(1)}, u32[]{:S(2)}, u32[]{:S(2)}) %all-to-all-start.3) | async-done | bytes 2097184 | tf_op jit(solution)/shard_map/all_to_all | solution.py:575
  188.6 7.2 all-to-all-start
  195.9 57.2 %expert_rows.3 = (bf16[1024,1024]{1,0:T(8,128)(2,1)}, bf16[1024,1024]{1,0:T(8,128)(2,1)}, bf16[1024,4096]{1,0:T(8,128)(2,1)}, bf16[1024,4096]{1,0:T(8,128)(2,1)}...) custom-call(s32[2]{0:T(128)} %pad_add_fusion.1.scalars, bf16[1024,1024]{1,0:T(8,128)(2,1)} %bitcast.162, ...), custom_call_target="tpu_custom_call" | custom-call | flops 34359738368 | bytes 46137344 | tf_op jit(solution)/shard_map/expert_rows/pallas_call | solution.py:506
  253.1 9.0 %fusion.27 = f32[1024,2048]{1,0:T(8,128)} fusion(bf16[1024,1024]{1,0:T(8,128)(2,1)S(1)} %bitcast.163, bf16[1024,4096]{1,0:T(8,128)(2,1)} %get-tuple-element.44), kind=kOutput, calls=%fused_computation.38 | convolution fusion | flops 4294967296 | bytes 14680064 | tf_op jit(solution)/shard_map/dot_general | solution.py:32
  262.1 7.1 all-to-all-start.7
  269.2 56.5 %expert_rows.2 = (bf16[1024,1024]{1,0:T(8,128)(2,1)}, bf16[1024,1024]{1,0:T(8,128)(2,1)}, bf16[1024,4096]{1,0:T(8,128)(2,1)}, bf16[1024,4096]{1,0:T(8,128)(2,1)}...) custom-call(s32[2]{0:T(128)} %pad_add_fusion.1.scalars, bf16[1024,1024]{1,0:T(8,128)(2,1)} %bitcast.158, ...), custom_call_target="tpu_custom_call" | custom-call | flops 34359738368 | bytes 46137344 | tf_op jit(solution)/shard_map/expert_rows/pallas_call | solution.py:506
  325.7 11.8 %add_convert_fusion.1 = bf16[1024,2048]{1,0:T(8,128)(2,1)} fusion(f32[1024,2048]{1,0:T(8,128)} %fusion.27, bf16[1024,1024]{1,0:T(8,128)(2,1)} %bitcast.159, bf16[1024,4096]{1,0:T(8,128)(2,1)} %get-tuple-element.43), kind=kOutput, calls=%fused_computation.3 | convolution fusion | flops 4299161600 | bytes 18874368 | tf_op jit(solution)/shard_map/dot_general | solution.py:32
  337.6 49.2 %collective-permute-start.9 = (bf16[1024,2048]{1,0:T(8,128)(2,1)}, bf16[1024,2048]{1,0:T(8,128)(2,1)}, u32[]{:S(2)}, u32[]{:S(2)}) collective-permute-start(bf16[1024,2048]{1,0:T(8,128)(2,1)} %add_convert_fusion.1), channel_id=1, source_target_pairs={{0,16},{16,0},{1,17},{17,1},{2,18},{18,2},{3,19},{19,3},{4,20},{20... | collective-permute-start | bytes 12582920 | tf_op jit(solution)/shard_map/ppermute | solution.py:571
  386.7 7.3 all-to-all-start.6
  396.1 9.3 %fusion.31 = f32[1024,2048]{1,0:T(8,128)} fusion(bf16[1024,1024]{1,0:T(8,128)(2,1)S(1)} %bitcast.165, bf16[1024,4096]{1,0:T(8,128)(2,1)} %get-tuple-element.44), kind=kOutput, calls=%fused_computation.42 | convolution fusion | flops 4294967296 | bytes 14680064 | tf_op jit(solution)/shard_map/dot_general | solution.py:32
  405.4 6.9 fusion.19
  412.3 6.9 fusion.23
  425.2 12.0 %all-to-all-done.6 = bf16[16,64,1024]{2,1,0:T(8,128)(2,1)} async-done(((bf16[16,64,1024]{2,1,0:T(8,128)(2,1)}), bf16[16,64,1024]{2,1,0:T(8,128)(2,1)}, u32[]{:S(2)}, u32[]{:S(2)}) %all-to-all-start.6) | async-done | bytes 2097184 | tf_op jit(solution)/shard_map/all_to_all | solution.py:575
  437.2 10.1 %all-to-all-start.5 = ((bf16[16,64,1024]{2,1,0:T(8,128)(2,1)}), bf16[16,64,1024]{2,1,0:T(8,128)(2,1)}, u32[]{:S(2)}, u32[]{:S(2)}) async-start(bf16[16,64,1024]{2,1,0:T(8,128)(2,1)} %bitcast.25), calls=%async_computation.5 | async-start | bytes 4194304 | tf_op jit(solution)/shard_map/all_to_all | solution.py:575
  447.3 7.0 multiply_reduce_fusion
  461.6 68.1 %attention_backward.1 = (bf16[1024,1024]{1,0:T(8,128)(2,1)}, bf16[2,1024,1024]{2,1,0:T(8,128)(2,1)}, bf16[2,1024,1024]{2,1,0:T(8,128)(2,1)}) custom-call(s32[2]{0:T(128)} %pad_add_fusion.scalars, bf16[1024,1024]{1,0:T(8,128)(2,1)} %multiply_convert_fusion.q_ref, bf16[1024,2048]{1,0:T(8,128)(2,1)} %collective-permute-done.2.prev_k_ref.prev_v_ref, ...), custom_call_target="tpu_custom_call" | custom-call | flops 64424509440 | bytes 27262976 | tf_op jit(solution)/shard_map/attention_backward/pallas_call | solution.py:381
  530.9 7.1 all-to-all-start.2
  538.1 11.9 %add_convert_fusion = bf16[2048,1024]{1,0:T(8,128)(2,1)} fusion(f32[2048,1024]{1,0:T(8,128)} %fusion.19, bf16[1024,1024]{1,0:T(8,128)(2,1)} %get-tuple-element.46, bf16[1024,4096]{1,0:T(8,128)(2,1)} %get-tuple-element.45), kind=kOutput, calls=%fused_computation.1 | convolution fusion | flops 4299161600 | bytes 18874368 | tf_op jit(solution)/shard_map/dot_general | solution.py:32
  550.0 41.5 %collective-permute-start.10 = (bf16[2048,1024]{1,0:T(8,128)(2,1)}, bf16[2048,1024]{1,0:T(8,128)(2,1)}, u32[]{:S(2)}, u32[]{:S(2)}) collective-permute-start(bf16[2048,1024]{1,0:T(8,128)(2,1)} %add_convert_fusion), channel_id=1, source_target_pairs={{0,16},{16,0},{1,17},{17,1},{2,18},{18,2},{3,19},{19,3},{4,20},{20... | collective-permute-start | bytes 12582920 | tf_op jit(solution)/shard_map/ppermute | solution.py:571
  616.0 6.6 all-to-all-start.9
  632.2 6.1 fusion.59
  638.3 8.9 %all-to-all-done.9 = bf16[16,32,1024]{2,1,0:T(8,128)(2,1)S(1)} async-done(((bf16[16,32,1024]{2,1,0:T(8,128)(2,1)}), bf16[16,32,1024]{2,1,0:T(8,128)(2,1)S(1)}, u32[]{:S(2)}, u32[]{:S(2)}) %all-to-all-start.9) | async-done | bytes 1048608 | tf_op jit(solution)/shard_map/all_to_all | solution.py:575
  654.3 10.6 %fusion.15 = (f32[1024]{0:T(1024)S(1)}, f32[1024]{0:T(1024)}, f32[1024]{0:T(1024)}, f32[1024]{0:T(1024)S(1)}, f32[1024,1024]{1,0:T(8,128)}) fusion(bf16[1,1024,1024]{2,1,0:T(8,128)(2,1)S(1)} %copy-done.3, f32[1024]{0:T(1024)S(1)} %copy-done.39, f32[1024]{0:T(1024)S(1)} %copy-done.35, f32[1024]{0:T(1024)S(1)} %bitcast.182, ...), kind=kOutput, calls=%fused_computation.26 | convolution fusion | flops 2160062464 | bytes 18903040 | tf_op jit(solution)/shard_map/dot_general | solution.py:28
  667.5 6.9 fusion.55
  701.6 11.2 %add_bitcast_fusion.1 = f32[1,1024,2048]{2,1,0:T(8,128)} fusion(bf16[1024,2048]{1,0:T(8,128)(2,1)} %collective-permute-done.9, f32[1024,2048]{1,0:T(8,128)} %fusion.31, bf16[1024,1024]{1,0:T(8,128)(2,1)S(1)} %bitcast.161, bf16[1024,4096]{1,0:T(8,128)(2,1)} %get-tuple-element.43), kind=kOutput, calls=%fused_computation.2 | convolution fusion | flops 4301258752 | bytes 27262976 | tf_op jit(solution)/shard_map/dot_general | solution.py:32
  726.3 14.6 %add_bitcast_fusion = f32[1,2048,1024]{2,1,0:T(8,128)} fusion(bf16[2048,1024]{1,0:T(8,128)(2,1)} %collective-permute-done.10, f32[2048,1024]{1,0:T(8,128)} %fusion.23, bf16[1024,1024]{1,0:T(8,128)(2,1)} %get-tuple-element.46, bf16[1024,4096]{1,0:T(8,128)(2,1)} %get-tuple-element.45), kind=kOutput, calls=%fused_computation | convolution fusion | flops 4301258752 | bytes 27262976 | tf_op jit(solution)/shard_map/dot_general | solution.py:32
  (238 shorter events, 171.5 us)
Async XLA Ops:
  7.3 135.9 %all-gather.4.cloned.1.call-start = ((), (), s32[]{:S(2)}) async-start(), calls=%async_computation.13 | async-start | bytes 3145728 | tf_op jit(solution)/shard_map/all_gather | solution.py:637
  8.0 187.8 %all-gather.6.cloned.1.call-start = ((), (), s32[]{:S(2)}) async-start(), calls=%async_computation.14 | async-start | bytes 12582912 | tf_op jit(solution)/shard_map/all_gather | solution.py:638
  8.8 7.2 collective-permute-start.1
  9.5 5.0 collective-permute-start
  28.5 66.7 %collective-permute-start.2 = (bf16[1024,2048]{1,0:T(8,128)(2,1)}, bf16[1024,2048]{1,0:T(8,128)(2,1)}, u32[]{:S(2)}, u32[]{:S(2)}) collective-permute-start(bf16[1024,2048]{1,0:T(8,128)(2,1)} %add_convert_fusion.3.own_k_ref.own_v_ref), channel_id=1, source_target_pairs={{0,16},{1,17},{2,18},{3,19},{4,20},{5,21},{6,22},{7,23},{8,24},{9,... | collective-permute-start | bytes 12582920 | tf_op jit(solution)/shard_map/ppermute | solution.py:677
  36.2 49.2 %all-to-all-start.1 = ((bf16[16,64,1024]{2,1,0:T(8,128)(2,1)}), bf16[16,64,1024]{2,1,0:T(8,128)(2,1)}, u32[]{:S(2)}, u32[]{:S(2)}) async-start(bf16[16,64,1024]{2,1,0:T(8,128)(2,1)} %bitcast.173), calls=%async_computation.1 | async-start | bytes 4194304 | tf_op jit(solution)/shard_map/all_to_all | solution.py:575
  44.5 151.4 %all-gather.8.cloned.1.call-start = ((), (), s32[]{:S(2)}) async-start(), calls=%async_computation.15 | async-start | bytes 12582912 | tf_op jit(solution)/shard_map/all_gather | solution.py:639
  85.4 69.4 %all-to-all-start.4 = ((bf16[16,64,1024]{2,1,0:T(8,128)(2,1)}), bf16[16,64,1024]{2,1,0:T(8,128)(2,1)}, u32[]{:S(2)}, u32[]{:S(2)}) async-start(bf16[16,64,1024]{2,1,0:T(8,128)(2,1)} %bitcast.171), calls=%async_computation.4 | async-start | bytes 4194304 | tf_op jit(solution)/shard_map/all_to_all | solution.py:575
  154.8 32.5 %all-to-all-start.3 = ((bf16[16,64,1024]{2,1,0:T(8,128)(2,1)}), bf16[16,64,1024]{2,1,0:T(8,128)(2,1)S(1)}, u32[]{:S(2)}, u32[]{:S(2)}) async-start(bf16[16,64,1024]{2,1,0:T(8,128)(2,1)} %bitcast.169), calls=%async_computation.3 | async-start | bytes 4194304 | tf_op jit(solution)/shard_map/all_to_all | solution.py:575
  188.6 73.5 %all-to-all-start = ((bf16[16,64,1024]{2,1,0:T(8,128)(2,1)}), bf16[16,64,1024]{2,1,0:T(8,128)(2,1)S(1)}, u32[]{:S(2)}, u32[]{:S(2)}) async-start(bf16[16,64,1024]{2,1,0:T(8,128)(2,1)} %bitcast.172), calls=%async_computation | async-start | bytes 4194304 | tf_op jit(solution)/shard_map/all_to_all | solution.py:575
  195.9 57.2 %copy-start.8 = (bf16[16,64,1024]{2,1,0:T(8,128)(2,1)S(1)}, bf16[16,64,1024]{2,1,0:T(8,128)(2,1)}, u32[]{:S(2)}) copy-start(bf16[16,64,1024]{2,1,0:T(8,128)(2,1)} %copy-done.7) | copy-start | bytes 6291460
  262.1 124.6 %all-to-all-start.7 = ((bf16[16,64,1024]{2,1,0:T(8,128)(2,1)}), bf16[16,64,1024]{2,1,0:T(8,128)(2,1)}, u32[]{:S(2)}, u32[]{:S(2)}) async-start(bf16[16,64,1024]{2,1,0:T(8,128)(2,1)} %bitcast.170), calls=%async_computation.7 | async-start | bytes 4194304 | tf_op jit(solution)/shard_map/all_to_all | solution.py:575
  337.6 56.4 %copy-start.5 = (bf16[16,64,1024]{2,1,0:T(8,128)(2,1)S(1)}, bf16[16,64,1024]{2,1,0:T(8,128)(2,1)}, u32[]{:S(2)}) copy-start(bf16[16,64,1024]{2,1,0:T(8,128)(2,1)} %copy-done.4) | copy-start | bytes 6291460
  337.6 56.5 %copy-start.33 = (bf16[1024,128]{1,0:T(8,128)(2,1)S(1)}, bf16[1024,128]{1,0:T(8,128)(2,1)}, u32[]{:S(2)}) copy-start(bf16[1024,128]{1,0:T(8,128)(2,1)} %get-tuple-element.41) | copy-start | bytes 786436
  337.6 364.1 %collective-permute-start.9 = (bf16[1024,2048]{1,0:T(8,128)(2,1)}, bf16[1024,2048]{1,0:T(8,128)(2,1)}, u32[]{:S(2)}, u32[]{:S(2)}) collective-permute-start(bf16[1024,2048]{1,0:T(8,128)(2,1)} %add_convert_fusion.1), channel_id=1, source_target_pairs={{0,16},{16,0},{1,17},{17,1},{2,18},{18,2},{3,19},{19,3},{4,20},{20... | collective-permute-start | bytes 12582920 | tf_op jit(solution)/shard_map/ppermute | solution.py:571
  386.7 50.5 %all-to-all-start.6 = ((bf16[16,64,1024]{2,1,0:T(8,128)(2,1)}), bf16[16,64,1024]{2,1,0:T(8,128)(2,1)}, u32[]{:S(2)}, u32[]{:S(2)}) async-start(bf16[16,64,1024]{2,1,0:T(8,128)(2,1)} %bitcast.168), calls=%async_computation.6 | async-start | bytes 4194304 | tf_op jit(solution)/shard_map/all_to_all | solution.py:575
  437.2 93.7 %all-to-all-start.5 = ((bf16[16,64,1024]{2,1,0:T(8,128)(2,1)}), bf16[16,64,1024]{2,1,0:T(8,128)(2,1)}, u32[]{:S(2)}, u32[]{:S(2)}) async-start(bf16[16,64,1024]{2,1,0:T(8,128)(2,1)} %bitcast.25), calls=%async_computation.5 | async-start | bytes 4194304 | tf_op jit(solution)/shard_map/all_to_all | solution.py:575
  529.6 95.7 %collective-permute-start.3 = (bf16[2,1024,1024]{2,1,0:T(8,128)(2,1)}, bf16[2,1024,1024]{2,1,0:T(8,128)(2,1)}, u32[]{:S(2)}, u32[]{:S(2)}) collective-permute-start(bf16[2,1024,1024]{2,1,0:T(8,128)(2,1)} %get-tuple-element.40), channel_id=1, source_target_pairs={{16,0},{17,1},{18,2},{19,3},{20,4},{21,5},{22,6},{23,7},{24,8},{25... | collective-permute-start | bytes 12582920 | tf_op jit(solution)/shard_map/ppermute | solution.py:763
  530.9 85.1 %all-to-all-start.2 = ((bf16[16,64,1024]{2,1,0:T(8,128)(2,1)}), bf16[16,64,1024]{2,1,0:T(8,128)(2,1)}, u32[]{:S(2)}, u32[]{:S(2)}) async-start(bf16[16,64,1024]{2,1,0:T(8,128)(2,1)} %bitcast.167), calls=%async_computation.2 | async-start | bytes 4194304 | tf_op jit(solution)/shard_map/all_to_all | solution.py:575
  550.0 176.3 %collective-permute-start.10 = (bf16[2048,1024]{1,0:T(8,128)(2,1)}, bf16[2048,1024]{1,0:T(8,128)(2,1)}, u32[]{:S(2)}, u32[]{:S(2)}) collective-permute-start(bf16[2048,1024]{1,0:T(8,128)(2,1)} %add_convert_fusion), channel_id=1, source_target_pairs={{0,16},{16,0},{1,17},{17,1},{2,18},{18,2},{3,19},{19,3},{4,20},{20... | collective-permute-start | bytes 12582920 | tf_op jit(solution)/shard_map/ppermute | solution.py:571
  595.1 18.2 %collective-permute-start.5 = (bf16[512,1024]{1,0:T(8,128)(2,1)S(1)}, bf16[512,1024]{1,0:T(8,128)(2,1)S(1)}, u32[]{:S(2)}, u32[]{:S(2)}) collective-permute-start(bf16[512,1024]{1,0:T(8,128)(2,1)S(1)} %convolution_convert_fusion.3), channel_id=1, source_target_pairs={{0,16},{16,0},{1,17},{17,1},{2,18},{18,2},{3,19},{19,3},{4,20},{20... | collective-permute-start | bytes 3145736 | tf_op jit(solution)/shard_map/ppermute | solution.py:571
  597.7 24.9 %collective-permute-start.8 = (bf16[512,1152]{1,0:T(8,128)(2,1)}, bf16[512,1152]{1,0:T(8,128)(2,1)}, u32[]{:S(2)}, u32[]{:S(2)}) collective-permute-start(bf16[512,1152]{1,0:T(8,128)(2,1)} %pad_maximum_fusion), channel_id=1, source_target_pairs={{0,16},{16,0},{1,17},{17,1},{2,18},{18,2},{3,19},{19,3},{4,20},{20... | collective-permute-start | bytes 3538952 | tf_op jit(solution)/shard_map/ppermute | solution.py:571
  616.0 31.1 %all-to-all-start.9 = ((bf16[16,32,1024]{2,1,0:T(8,128)(2,1)}), bf16[16,32,1024]{2,1,0:T(8,128)(2,1)S(1)}, u32[]{:S(2)}, u32[]{:S(2)}) async-start(bf16[16,32,1024]{2,1,0:T(8,128)(2,1)} %bitcast.175), calls=%async_computation.9 | async-start | bytes 2097152 | tf_op jit(solution)/shard_map/all_to_all | solution.py:575
  632.1 22.2 %copy-start.37 = (f32[1,1024]{1,0:T(1,128)S(1)}, f32[1,1024]{1,0:T(1,128)}, u32[]{:S(2)}) copy-start(f32[1,1024]{1,0:T(1,128)} %copy-done.36) | copy-start | bytes 12292
  632.1 22.2 %copy-start.39 = (f32[1024]{0:T(1024)S(1)}, f32[1024]{0:T(1024)}, u32[]{:S(2)}) copy-start(f32[1024]{0:T(1024)} %copy-done.38) | copy-start | bytes 12292
  632.1 54.0 %collective-permute-start.6 = (bf16[512,1024]{1,0:T(8,128)(2,1)}, bf16[512,1024]{1,0:T(8,128)(2,1)}, u32[]{:S(2)}, u32[]{:S(2)}) collective-permute-start(bf16[512,1024]{1,0:T(8,128)(2,1)} %fusion.87), channel_id=1, source_target_pairs={{0,16},{16,0},{1,17},{17,1},{2,18},{18,2},{3,19},{19,3},{4,20},{20... | collective-permute-start | bytes 3145736 | tf_op jit(solution)/shard_map/ppermute | solution.py:571
  648.1 31.8 %all-to-all-start.12 = ((bf16[16,32,1152]{2,1,0:T(8,128)(2,1)}), bf16[16,32,1152]{2,1,0:T(8,128)(2,1)S(1)}, u32[]{:S(2)}, u32[]{:S(2)}) async-start(bf16[16,32,1152]{2,1,0:T(8,128)(2,1)} %bitcast.166), calls=%async_computation.12 | async-start | bytes 2359296 | tf_op jit(solution)/shard_map/all_to_all | solution.py:575
  667.4 7.0 collective-permute-start.4
  679.9 13.9 %all-to-all-start.8 = ((bf16[16,32,128]{2,1,0:T(8,128)(2,1)}), bf16[16,32,128]{2,1,0:T(8,128)(2,1)S(1)}, u32[]{:S(2)}, u32[]{:S(2)}) async-start(bf16[16,32,128]{2,1,0:T(8,128)(2,1)} %bitcast.40), calls=%async_computation.8 | async-start | bytes 262144 | tf_op jit(solution)/shard_map/all_to_all | solution.py:575
  693.8 26.9 %all-to-all-start.10 = ((bf16[16,32,1024]{2,1,0:T(8,128)(2,1)}), bf16[16,32,1024]{2,1,0:T(8,128)(2,1)}, u32[]{:S(2)}, u32[]{:S(2)}) async-start(bf16[16,32,1024]{2,1,0:T(8,128)(2,1)} %bitcast.176), calls=%async_computation.10 | async-start | bytes 2097152 | tf_op jit(solution)/shard_map/all_to_all | solution.py:575
  701.5 11.3 %collective-permute-start.7 = (bf16[512,1024]{1,0:T(8,128)(2,1)S(1)}, bf16[512,1024]{1,0:T(8,128)(2,1)S(1)}, u32[]{:S(2)}, u32[]{:S(2)}) collective-permute-start(bf16[512,1024]{1,0:T(8,128)(2,1)S(1)} %convolution_convert_fusion.2), channel_id=1, source_target_pairs={{0,16},{16,0},{1,17},{17,1},{2,18},{18,2},{3,19},{19,3},{4,20},{20... | collective-permute-start | bytes 3145736 | tf_op jit(solution)/shard_map/ppermute | solution.py:571
  720.8 32.1 %all-to-all-start.11 = ((bf16[16,32,1024]{2,1,0:T(8,128)(2,1)}), bf16[16,32,1024]{2,1,0:T(8,128)(2,1)}, u32[]{:S(2)}, u32[]{:S(2)}) async-start(bf16[16,32,1024]{2,1,0:T(8,128)(2,1)} %bitcast.174), calls=%async_computation.11 | async-start | bytes 2097152 | tf_op jit(solution)/shard_map/all_to_all | solution.py:575
  (51 other events, 328.9 us)
Sparse Core Ops, SparseCore 0:
  9.7 13.2 all-gather.3
  24.5 21.0 all-gather.5
  47.1 21.0 all-gather.7

commit v2 on v1

--- a/solution.py
+++ b/solution.py
@@ -14,6 +14,7 @@
 GELU_A = 0.7978845608028654
 GELU_B = 0.044715
 CHUNKS = 2
+FIRST_PAIRS = 5
 LANES = 128
 BF16 = jnp.bfloat16
 F32 = jnp.float32
@@ -123,21 +124,18 @@
         whole = jnp.minimum(jnp.maximum(i * block_q // block_k, own_prefix // block_k), seen)
 
         def over_keys(block):
-            @pl.when(has_prev > 0)
-            def _():
-                for j in range(key_blocks):
-                    block(j * block_k, False)
-
             def unmasked(j, carried):
-                block(rows + j * block_k, False)
+                block(j * block_k, False)
                 return carried
 
             def masked(j, carried):
-                block(rows + j * block_k, True)
+                block(j * block_k, True)
                 return carried
 
-            lax.fori_loop(0, whole, unmasked, 0)
-            lax.fori_loop(whole, seen, masked, 0)
+            lax.fori_loop(
+                jnp.where(has_prev > 0, 0, key_blocks), key_blocks + whole, unmasked, 0
+            )
+            lax.fori_loop(key_blocks + whole, key_blocks + seen, masked, 0)
 
         def allowed(at):
             key_pos = at - rows + lax.broadcasted_iota(jnp.int32, (block_q, block_k), 1)
@@ -322,69 +320,74 @@
         )
 
     query_blocks = rows // block_q
-
-    def clear():
-        dk_total[...] = jnp.zeros_like(dk_total)
-        dv_total[...] = jnp.zeros_like(dv_total)
-
-    def put(ref, j):
-        here = slice(j * block_k, (j + 1) * block_k)
-        ref[0, here, :] = dk_total[...].astype(BF16)
-        ref[1, here, :] = dv_total[...].astype(BF16)
-
-    @pl.when(has_prev > 0)
-    def _():
-        for j in range(rows // block_k):
-            clear()
-
-            def step(i, carried):
-                block(j * block_k, i, False)
-                return carried
-
-            lax.fori_loop(0, query_blocks, step, 0)
-            put(prev_grad_ref, j)
+    key_blocks = rows // block_k
 
     @pl.when(has_prev == 0)
     def _():
         prev_grad_ref[0] = zero
         prev_grad_ref[1] = zero
 
-    for j in range(rows // block_k):
-        clear()
-        inside = own_prefix >= (j + 1) * block_k
-        reached = own_prefix > j * block_k
-        first_whole = jnp.where(inside, 0, min(query_blocks, -(-((j + 1) * block_k - 1) // block_q)))
-        first_seen = jnp.where(reached, 0, min(query_blocks, j * block_k // block_q))
+    def one_key_block(j, carried):
+        at = j * block_k
+        own_at = at - rows
+        dk_total[...] = jnp.zeros_like(dk_total)
+        dv_total[...] = jnp.zeros_like(dv_total)
+        first_whole = jnp.where(
+            own_prefix >= own_at + block_k,
+            0,
+            jnp.clip((own_at + block_k - 1 + block_q - 1) // block_q, 0, query_blocks),
+        )
+        first_seen = jnp.where(own_prefix > own_at, 0, jnp.clip(own_at // block_q, 0, query_blocks))
+        first_whole = jnp.where(own_at < 0, 0, first_whole)
+        first_seen = jnp.where(own_at < 0, 0, first_seen)
 
         def masked(i, carried):
-            block(rows + j * block_k, i, True)
+            block(at, i, True)
             return carried
 
         def unmasked(i, carried):
-            block(rows + j * block_k, i, False)
+            block(at, i, False)
             return carried
 
         lax.fori_loop(first_seen, first_whole, masked, 0)
         lax.fori_loop(first_whole, query_blocks, unmasked, 0)
-        put(own_grad_ref, j)
+
+        @pl.when(own_at < 0)
+        def _():
+            here = pl.ds(pl.multiple_of(at, block_k), block_k)
+            prev_grad_ref[0, here, :] = dk_total[...].astype(BF16)
+            prev_grad_ref[1, here, :] = dv_total[...].astype(BF16)
+
+        @pl.when(own_at >= 0)
+        def _():
+            here = pl.ds(pl.multiple_of(own_at, block_k), block_k)
+            own_grad_ref[0, here, :] = dk_total[...].astype(BF16)
+            own_grad_ref[1, here, :] = dv_total[...].astype(BF16)
+
+        return carried
+
+    lax.fori_loop(jnp.where(has_prev > 0, 0, key_blocks), 2 * key_blocks, one_key_block, 0)
     dq_ref[...] = (dq_total[...] * (HEAD_DIM**-0.5)).astype(BF16)
 
 
-def attention_backward(scalars, queries, prev, own, out, lse, grads, block_q=512, block_k=512):
+def attention_backward(
+    scalars, queries, prev, own, out, lse, grads, begin, count, block_q=512, block_k=512
+):
     rows, width = queries.shape
     pairs = width // LANES
 
     def spec(offset):
-        return pl.BlockSpec((rows, LANES), lambda h, scalars: (0, h + offset))
+        return pl.BlockSpec((rows, LANES), lambda h, scalars: (0, h + begin + offset))
 
     both = pl.BlockSpec((2, rows, LANES), lambda h, scalars: (0, 0, h))
+    share = count * LANES
     return pl.pallas_call(
         partial(backward_kernel, block_q, block_k),
         grid_spec=pltpu.PrefetchScalarGridSpec(
             num_scalar_prefetch=1,
-            grid=(pairs,),
+            grid=(count,),
             in_specs=[spec(0), spec(0), spec(pairs), spec(0), spec(pairs)] + [spec(0)] * 3,
-            out_specs=[spec(0), both, both],
+            out_specs=[pl.BlockSpec((rows, LANES), lambda h, scalars: (0, h)), both, both],
             scratch_shapes=[
                 pltpu.VMEM((2, 2 * rows, 2 * LANES), BF16),
                 pltpu.VMEM((2, 2 * rows, LANES), BF16),
@@ -399,15 +402,15 @@
             ],
         ),
         out_shape=[
-            jax.ShapeDtypeStruct((rows, width), BF16),
-            jax.ShapeDtypeStruct((2, rows, width), BF16),
-            jax.ShapeDtypeStruct((2, rows, width), BF16),
+            jax.ShapeDtypeStruct((rows, share), BF16),
+            jax.ShapeDtypeStruct((2, rows, share), BF16),
+            jax.ShapeDtypeStruct((2, rows, share), BF16),
         ],
         compiler_params=pltpu.CompilerParams(vmem_limit_bytes=VMEM_LIMIT),
         cost_estimate=pl.CostEstimate(
-            flops=60 * rows * rows * width,
-            bytes_accessed=26 * rows * width,
-            transcendentals=2 * rows * rows * width // HEAD_DIM,
+            flops=60 * rows * rows * share,
+            bytes_accessed=26 * rows * share,
+            transcendentals=2 * rows * rows * share // HEAD_DIM,
         ),
         name="attention_backward",
     )(scalars, queries, prev, prev, own, own, out, lse, grads)
@@ -422,6 +425,7 @@
     w_in_ref,
     w_down_ref,
     router_ref,
+    y_before_ref,
     y_ref,
     dm_ref,
     act_ref,
@@ -433,33 +437,34 @@
     probs,
 ):
     step = pl.program_id(0)
-    blocks = rows_ref.shape[0] // block_r
+    slots, width = cot_ref.shape[1], cot_ref.shape[2]
+    sources = block_r // slots
     lane = lane_index(block_r)
     is_mine = lane == scalars[0]
 
     def over_rows(work):
-        def one(b, carried):
-            work(pl.ds(pl.multiple_of(b * block_r, block_r), block_r))
-            return carried
-
-        lax.fori_loop(0, blocks, one, 0)
+        for b in range(rows_ref.shape[0] // block_r):
+            work(slice(b * block_r, (b + 1) * block_r), slice(b * sources, (b + 1) * sources))
+
+    def cots(source):
+        return cot_ref[source].reshape(block_r, width).astype(F32)
 
     @pl.when(step == 0)
     def _():
-        def gate(here):
+        def gate(here, source):
             logits = nt(rows_ref[here, :], router_ref[...])
             logits = jnp.where(lane < experts, logits, MASK_FILL)
             spread = jnp.exp(logits - jnp.max(logits, axis=1, keepdims=True))
             part = spread / jnp.sum(spread, axis=1, keepdims=True)
             probs[here, :] = part
             mine = jnp.sum(jnp.where(is_mine, part, 0.0), axis=1, keepdims=True)
-            dy_ref[here, :] = (mine * cot_ref[here, :].astype(F32)).astype(BF16)
+            dy_ref[here, :] = (mine * cots(source)).astype(BF16)
             y_total[here, :] = jnp.zeros((block_r, y_total.shape[1]), F32)
             dm_total[here, :] = jnp.zeros((block_r, dm_total.shape[1]), F32)
 
         over_rows(gate)
 
-    def hidden_block(here):
+    def hidden_block(here, source):
         u = nn(rows_ref[here, :], w_in_ref[...])
         d_act = nt(dy_ref[here, :], w_down_ref[...])
         square = u * u
@@ -479,10 +484,10 @@
 
     @pl.when(step == pl.num_programs(0) - 1)
     def _():
-        def finish(here):
+        def finish(here, source):
             y = y_total[here, :].astype(BF16)
-            y_ref[here, :] = y
-            d_gate = jnp.sum(cot_ref[here, :].astype(F32) * y.astype(F32), axis=1, keepdims=True)
+            y_ref[source] = y.reshape(sources, slots, width)
+            d_gate = jnp.sum(cots(source) * y.astype(F32), axis=1, keepdims=True)
             part = probs[here, :]
             mine = jnp.sum(jnp.where(is_mine, part, 0.0), axis=1, keepdims=True)
             dz = ((d_gate * mine) * (jnp.where(is_mine, 1.0, 0.0) - part)).astype(BF16)
@@ -493,16 +498,22 @@
         over_rows(finish)
 
 
-def run_expert(scalars, rows_in, cots, w_in, w_down, router, experts, block_h=512, block_r=256):
+def run_expert(
+    scalars, rows_in, cots, w_in, w_down, router, y_before, chunk, experts, block_h=512, block_r=1024
+):
     rows, width = rows_in.shape
     half = w_in.shape[2]
     per_half = half // block_h
     whole = pl.BlockSpec((rows, width), lambda j, s: (0, 0))
     hidden = pl.BlockSpec((rows, block_h), lambda j, s: (0, j))
+    mine = pl.BlockSpec(
+        (cots.shape[0], None, cots.shape[2], width), lambda j, s: (0, chunk, 0, 0)
+    )
 
     def which(j, s):
         return lax.rem(j // per_half + s[1], 2)
 
+    first = y_before is None
     return pl.pallas_call(
         partial(expert_kernel, experts, block_r),
         grid_spec=pltpu.PrefetchScalarGridSpec(
@@ -510,7 +521,7 @@
             grid=(2 * per_half,),
             in_specs=[
                 whole,
-                whole,
+                mine,
                 pl.BlockSpec(
                     (None, width, block_h), lambda j, s: (which(j, s), 0, lax.rem(j, per_half))
                 ),
@@ -518,9 +529,10 @@
                     (None, block_h, width), lambda j, s: (which(j, s), lax.rem(j, per_half), 0)
                 ),
                 pl.BlockSpec((LANES, width), lambda j, s: (0, 0)),
+                pl.BlockSpec(memory_space=pl.ANY),
             ],
             out_specs=[
-                whole,
+                mine,
                 whole,
                 hidden,
                 hidden,
@@ -534,13 +546,14 @@
             ],
         ),
         out_shape=[
-            jax.ShapeDtypeStruct((rows, width), BF16),
+            jax.ShapeDtypeStruct(cots.shape, BF16),
             jax.ShapeDtypeStruct((rows, width), BF16),
             jax.ShapeDtypeStruct((rows, 2 * half), BF16),
             jax.ShapeDtypeStruct((rows, 2 * half), BF16),
             jax.ShapeDtypeStruct((rows, width), BF16),
             jax.ShapeDtypeStruct((rows, LANES), BF16),
         ],
+        input_output_aliases={} if first else {6: 0},
         compiler_params=pltpu.CompilerParams(vmem_limit_bytes=VMEM_LIMIT),
         cost_estimate=pl.CostEstimate(
             flops=16 * rows * width * half,
@@ -548,7 +561,199 @@
             transcendentals=2 * rows * half,
         ),
         name="expert_rows",
-    )(scalars, rows_in, cots, w_in, w_down, router)
+    )(scalars, rows_in, cots, w_in, w_down, router, scalars if first else y_before)
+
+
+def expert_weights_kernel(chunks, add, *refs):
+    rows_refs, dy_refs, act_refs, du_refs = (
+        refs[i * chunks : (i + 1) * chunks] for i in range(4)
+    )
+    rest = refs[4 * chunks :]
+    d_in_ref, d_down_ref, turned = rest[-3:]
+    rows = rows_refs[0].shape[0]
+
+    @pl.when(pl.program_id(0) == 0)
+    def _():
+        for c in range(chunks):
+            turned[:, c * rows : (c + 1) * rows] = rows_refs[c][...].T
+
+    d_in, d_down = None, None
+    for c in range(chunks):
+        part = nn(turned[:, c * rows : (c + 1) * rows], du_refs[c][...])
+        d_in = part if d_in is None else d_in + part
+        part = tn(act_refs[c][...], dy_refs[c][...])
+        d_down = part if d_down is None else d_down + part
+    if add:
+        d_in = d_in + rest[0][...].astype(F32)
+        d_down = d_down + rest[1][...].astype(F32)
+    d_in_ref[...] = d_in.astype(d_in_ref.dtype)
+    d_down_ref[...] = d_down.astype(d_down_ref.dtype)
+
+
+def expert_weights(rows_in, dy, act, du, half_index, got, block_h=512):
+    chunks = len(rows_in)
+    rows, width = rows_in[0].shape
+    half = du[0].shape[1] // 2
+    steps = half // block_h
+    whole = pl.BlockSpec((rows, width), lambda j: (0, 0))
+    hidden = pl.BlockSpec((rows, block_h), lambda j: (0, j + half_index * steps))
+    columns = pl.BlockSpec((width, block_h), lambda j: (0, j))
+    lines = pl.BlockSpec((block_h, width), lambda j: (j, 0))
+    dtype = BF16 if got is None else F32
+    extra = () if got is None else tuple(got)
+    return pl.pallas_call(
+        partial(expert_weights_kernel, chunks, got is not None),
+        grid=(steps,),
+        in_specs=[whole] * (2 * chunks) + [hidden] * (2 * chunks) + [columns, lines][: len(extra)],
+        out_specs=[columns, lines],
+        out_shape=[
+            jax.ShapeDtypeStruct((width, half), dtype),
+            jax.ShapeDtypeStruct((half, width), dtype),
+        ],
+        scratch_shapes=[pltpu.VMEM((width, chunks * rows), BF16)],
+        compiler_params=pltpu.CompilerParams(vmem_limit_bytes=VMEM_LIMIT),
+        cost_estimate=pl.CostEstimate(
+            flops=4 * chunks * rows * width * half,
+            bytes_accessed=4 * chunks * rows * (width + half) + 8 * width * half,
+            transcendentals=0,
+        ),
+        name="expert_weights",
+    )(*rows_in, *dy, *act, *du, *extra)
+
+
+def pair_weights_kernel(groups, add, scalars, *refs):
+    out_ref = refs[-1]
+    at, column = 0, 0
+    got = refs[-4:-1] if add else None
+    for rights in groups:
+        turned = refs[at][...].T
+        at += 1
+        for stacked in rights:
+            for i in range(max(1, stacked)):
+                grads = refs[at][i] if stacked else refs[at][...]
+                part = nn(turned, grads)
+                here = slice(column, column + part.shape[1])
+                column += part.shape[1]
+                if add:
+                    part = part + got[0][:, here].astype(F32)
+                out_ref[:, here] = part.astype(BF16)
+            at += 1
+    if add:
+        out_ref[:, column:] = (got[1][...] + got[2][...].astype(F32)).astype(BF16)
+
+
+def pair_weights(half_index, products, got=None):
+    more = () if got is None else tuple(got)
+    arrays, specs, groups, columns, flops = [], [], [], 0, 0
+
+    def full(shape):
+        return pl.BlockSpec(shape, lambda i, s: (0,) * len(shape))
+
+    for left, rights in products:
+        rows, half = left.shape[0], left.shape[1] // 2
+        arrays.append(left)
+        specs.append(pl.BlockSpec((rows, half), lambda i, s: (0, s[0])))
+        groups.append(tuple(r.shape[0] if r.ndim == 3 else 0 for r in rights))
+        for right in rights:
+            arrays.append(right)
+            specs.append(full(right.shape))
+            columns += right.size // rows
+    flops = 2 * rows * half * columns
+    if got is not None:
+        columns += got[1].shape[1]
+    return pl.pallas_call(
+        partial(pair_weights_kernel, tuple(groups), got is not None),
+        grid_spec=pltpu.PrefetchScalarGridSpec(
+            num_scalar_prefetch=1,
+            grid=(1,),
+            in_specs=specs + [full(m.shape) for m in more],
+            out_specs=full((half, columns)),
+        ),
+        out_shape=jax.ShapeDtypeStruct((half, columns), BF16),
+        compiler_params=pltpu.CompilerParams(vmem_limit_bytes=VMEM_LIMIT),
+        cost_estimate=pl.CostEstimate(
+            flops=flops, bytes_accessed=4 * (rows + half) * columns, transcendentals=0
+        ),
+        name="pair_weights",
+    )(half_index, *arrays, *more)
+
+
+def first_norm_kernel(shares, tokens_ref, dh_ref, gain_ref, w_ref, *refs):
+    parts = len(shares)
+    out_ref, sums_ref = refs[2 * parts], refs[2 * parts + 1]
+    width = tokens_ref.shape[1]
+    d_norm = None
+    query_sums, value_sums = [], []
+    begin = 0
+    for p, share in enumerate(shares):
+        dq, dkv = refs[2 * p], refs[2 * p + 1]
+        for i in range(3):
+            grads = dq[...] if i == 0 else dkv[i - 1]
+            at = i * width + begin
+            part = nt(grads, w_ref[:, at : at + share])
+            d_norm = part if d_norm is None else d_norm + part
+        query_sums.append(jnp.sum(dq[...].astype(F32), axis=0, keepdims=True))
+        value_sums.append(jnp.sum(dkv[1].astype(F32), axis=0, keepdims=True))
+        begin += share
+    values = tokens_ref[...].astype(F32)
+    center = values - jnp.mean(values, axis=1, keepdims=True)
+    inv_std = lax.rsqrt(jnp.mean(center * center, axis=1, keepdims=True) + NORM_EPSILON)
+    normed = center * inv_std
+    scaled = d_norm * gain_ref[...]
+    back = inv_std * (
+        scaled
+        - jnp.mean(scaled, axis=1, keepdims=True)
+        - normed * jnp.mean(scaled * normed, axis=1, keepdims=True)
+    )
+    out_ref[...] = (dh_ref[...] + back).astype(BF16)
+    sums = jnp.concatenate(
+        [
+            jnp.sum(d_norm * normed, axis=0, keepdims=True),
+            jnp.sum(d_norm, axis=0, keepdims=True),
+            jnp.concatenate(query_sums, axis=1),
+            jnp.concatenate(value_sums, axis=1),
+            jnp.zeros((4, width), F32),
+        ],
+        axis=0,
+    )
+    started = pl.program_id(0) > 0
+    sums_ref[...] = jnp.where(started, sums_ref[...], 0.0) + sums
+
+
+def first_norm(tokens, d_hidden, gain, weight, grads, block_r=256):
+    rows, width = tokens.shape
+    shares = tuple(g[0].shape[1] for g in grads)
+    lines = pl.BlockSpec((block_r, width), lambda i: (i, 0))
+    specs, arrays = [], []
+    for (d_query, d_key_value), share in zip(grads, shares):
+        specs += [
+            pl.BlockSpec((block_r, share), lambda i: (i, 0)),
+            pl.BlockSpec((2, block_r, share), lambda i: (0, i, 0)),
+        ]
+        arrays += [d_query, d_key_value]
+    return pl.pallas_call(
+        partial(first_norm_kernel, shares),
+        grid=(rows // block_r,),
+        in_specs=[
+            lines,
+            lines,
+            pl.BlockSpec((1, width), lambda i: (0, 0)),
+            pl.BlockSpec((width, 3 * width), lambda i: (0, 0)),
+        ]
+        + specs,
+        out_specs=[lines, pl.BlockSpec((8, width), lambda i: (0, 0))],
+        out_shape=[
+            jax.ShapeDtypeStruct((rows, width), BF16),
+            jax.ShapeDtypeStruct((8, width), F32),
+        ],
+        compiler_params=pltpu.CompilerParams(vmem_limit_bytes=VMEM_LIMIT),
+        cost_estimate=pl.CostEstimate(
+            flops=6 * rows * width * width,
+            bytes_accessed=14 * rows * width + 6 * width * width,
+            transcendentals=rows,
+        ),
+        name="first_norm",
+    )(tokens, d_hidden, gain[None, :], weight, *arrays)
 
 
 def layer_norm(values, norm_gain, norm_bias):
@@ -649,23 +854,31 @@
     place_in = token_route * slots + slot_index % slots
     buffer_ids = jnp.arange(chunk_rows, dtype=jnp.int32)
 
+    def place_of(chunk):
+        return jnp.where(chunk_of == chunk, place_in, -1)
+
     def dispatch(row_values, chunk):
-        place = jnp.where(chunk_of == chunk, place_in, -1)
-        picked = nn((buffer_ids[:, None] == place[None, :]).astype(BF16), row_values)
+        picked = nn((buffer_ids[:, None] == place_of(chunk)[None, :]).astype(BF16), row_values)
         return exchanged(picked.astype(BF16).reshape(experts, slots, width)).reshape(
             chunk_rows, width
         )
 
-    def give_back(buffers):
-        got = [exchanged(b.reshape(experts, slots, width)).reshape(chunk_rows, width) for b in buffers]
+    def sent_back(buffer):
+        return exchanged(buffer.reshape(experts, slots, width)).reshape(chunk_rows, width)
+
+    def picked_up(got):
         total = None
         for chunk in range(CHUNKS):
-            place = jnp.where(chunk_of == chunk, place_in, -1)
-            part = nn((place[:, None] == buffer_ids[None, :]).astype(BF16), got[chunk])
+            part = nn((place_of(chunk)[:, None] == buffer_ids[None, :]).astype(BF16), got[chunk])
             total = part if total is None else total + part
         return total
 
-    cot_rows = [dispatch(out_grad[0], chunk) for chunk in range(CHUNKS)]
+    full_place = token_route * (CHUNKS * slots) + slot_index
+    full_ids = jnp.arange(CHUNKS * chunk_rows, dtype=jnp.int32)
+    cot_rows = nn((full_ids[:, None] == full_place[None, :]).astype(BF16), out_grad[0])
+    cot_rows = exchanged(cot_rows.astype(BF16).reshape(experts, CHUNKS * slots, width)).reshape(
+        experts, CHUNKS, slots, width
+    )
 
     residual = tokens[0].astype(F32)
     norm1_out, normed1, inv_std1 = layer_norm(residual, norm1_gain, norm1_bias)
@@ -685,31 +898,30 @@
     mixed_rows = [dispatch(mixed, chunk) for chunk in range(CHUNKS)]
     router_pad = jnp.pad(router_t, ((0, LANES - experts), (0, 0)))
     expert_scalars = jnp.stack([my_expert, my_half]).astype(jnp.int32)
-    done = [
-        run_expert(
-            expert_scalars, mixed_rows[c], cot_rows[c], w_in_both, w_down_both, router_pad, experts
-        )
-        for c in range(CHUNKS)
-    ]
-    d_mixed = give_back([d[1] for d in done])
-
-    hidden_half = w_in.shape[2]
-
-    def both_chunks(pick_left, pick_right):
-        total = None
-        for c in range(CHUNKS):
-            part = tn(pick_left(c), pick_right(c))
-            total = part if total is None else total + part
-        return total
-
-    own, other = slice(0, hidden_half), slice(hidden_half, 2 * hidden_half)
-    d_in_other = both_chunks(lambda c: mixed_rows[c], lambda c: done[c][3][:, other])
-    d_down_other = both_chunks(lambda c: done[c][2][:, other], lambda c: done[c][4])
-    d_in_got = swapped(d_in_other.astype(BF16))
-    d_down_got = swapped(d_down_other.astype(BF16))
-    d_w_in = both_chunks(lambda c: mixed_rows[c], lambda c: done[c][3][:, own]) + d_in_got
-    d_w_down = both_chunks(lambda c: done[c][2][:, own], lambda c: done[c][4]) + d_down_got
-    d_router = both_chunks(lambda c: mixed_rows[c], lambda c: done[c][5])
+    done, y_rows = [], None
+    for c in range(CHUNKS):
+        y_rows, *rest = run_expert(
+            expert_scalars,
+            mixed_rows[c],
+            cot_rows,
+            w_in_both,
+            w_down_both,
+            router_pad,
+            y_rows,
+            c,
+            experts,
+        )
+        done.append(rest)
+    d_mixed_chunks, act, du, dy, dz = ([d[i] for d in done] for i in range(5))
+    back = [sent_back(d) for d in d_mixed_chunks]
+    others = expert_weights(mixed_rows, dy, act, du, 1, None)
+    back[-1], others = lax.optimization_barrier((back[-1], others))
+    d_mixed = picked_up(back)
+    got = [swapped(o) for o in others]
+    d_router = None
+    for c in range(CHUNKS):
+        part = tn(mixed_rows[c], dz[c])
+        d_router = part if d_router is None else d_router + part
 
     out_cot = out_grad[0].astype(F32)
     d_expert_bias = jnp.sum(out_cot, axis=0)
@@ -723,28 +935,19 @@
     logits = nt(mixed, router_t)
     router_probs = jax.nn.softmax(logits, axis=-1)
     gate_value = jnp.sum(jnp.where(one_hot, router_probs, 0.0), axis=-1)
-    expert_value = give_back([d[0] for d in done])
-    output = hidden + gate_value[:, None] * expert_value + expert_bias
-
-    def halves(columns):
-        left, right = columns[:, :half_width], columns[:, half_width:]
-        return jnp.where(is_first, left, right), jnp.where(is_first, right, left)
-
-    def row_halves(matrix):
-        top, bottom = matrix[:half_width], matrix[half_width:]
-        return jnp.where(is_first, top, bottom), jnp.where(is_first, bottom, top)
-
-    def scattered(own_part, other_part):
-        pair = own_part + swapped(other_part.astype(BF16)).astype(F32)
-        blocks = pair.astype(BF16).reshape(experts, half_width // experts, pair.shape[1])
-        return jnp.sum(exchanged(blocks).astype(F32), axis=0)
-
+    y_back = exchanged(y_rows.reshape(experts, CHUNKS * slots, width)).reshape(-1, width)
     def as_columns(pieces):
         packed = jnp.concatenate(pieces, axis=1)
         return jnp.pad(packed, ((0, 0), (0, -packed.shape[1] % LANES)))
 
-    context_own, context_other = halves(context)
-    extra_own, extra_other = row_halves(
+    def split_columns(columns):
+        top, bottom = columns[:half_width], columns[half_width:]
+        return (
+            jnp.where(is_first, top, bottom),
+            swapped(jnp.where(is_first, bottom, top).astype(BF16)),
+        )
+
+    early = split_columns(
         as_columns(
             [
                 d_router[:, :experts],
@@ -752,51 +955,58 @@
             ]
         )
     )
-    sum_out = scattered(
-        jnp.concatenate([tn(context_own, d_attn), extra_own], axis=1),
-        jnp.concatenate([tn(context_other, d_attn), extra_other], axis=1),
-    )
-
-    d_query, prev_grad, own_grad = attention_backward(
-        scalars, queries, prev_key_value, key_value, context, lse, d_context
-    )
-    returned = lax.ppermute(prev_grad, "fsdp", [(1, 0)])
-    in_own, in_other = halves(attn_in)
-    sum_query = scattered(tn(in_own, d_query), tn(in_other, d_query))
-    d_key_value = (own_grad.astype(F32) + returned.astype(F32)).astype(BF16)
-    d_key, d_value = d_key_value[0], d_key_value[1]
-    sum_key = scattered(tn(in_own, d_key), tn(in_other, d_key))
-    sum_value = scattered(tn(in_own, d_value), tn(in_other, d_value))
-    d_norm1_out = (
-        nt(d_query, qkv_weight[:, :width])
-        + nt(d_key, qkv_weight[:, width : 2 * width])
-        + nt(d_value, qkv_weight[:, 2 * width :])
-    )
-    d_tokens = (d_hidden + norm_backward(d_norm1_out, normed1, inv_std1, norm1_gain)).astype(BF16)
-    last_own, last_other = row_halves(
-        as_columns(
-            [
-                jnp.stack(
-                    [
-                        jnp.sum(d_query.astype(F32), axis=0),
-                        jnp.sum(d_value.astype(F32), axis=0),
-                        jnp.sum(d_norm1_out * normed1, axis=0),
-                        jnp.sum(d_norm1_out, axis=0),
-                    ],
-                    axis=1,
-                )
-            ]
-        )
-    )
-    sum_last = scattered(last_own, last_other)
+
+    own_index = my_half[None].astype(jnp.int32)
+    other_index = 1 - own_index
+    pairs = width // LANES
+    groups = ((0, FIRST_PAIRS), (FIRST_PAIRS, pairs - FIRST_PAIRS))
+    grads, sums = [], []
+    for number, (begin, count) in enumerate(groups):
+        d_query, prev_grad, own_grad = attention_backward(
+            scalars, queries, prev_key_value, key_value, context, lse, d_context, begin, count
+        )
+        returned = lax.ppermute(prev_grad, "fsdp", [(1, 0)])
+        d_key_value = (own_grad.astype(F32) + returned.astype(F32)).astype(BF16)
+        grads.append((d_query, d_key_value))
+        if number == 0:
+            d_key_value, y_back = lax.optimization_barrier((d_key_value, y_back))
+        products = [(attn_in, [d_query, d_key_value])]
+        if number == 0:
+            products.append((context, [d_attn]))
+        other_part = swapped(pair_weights(other_index, products))
+        if number == 0:
+            extra = early
+        else:
+            d_tokens, norm_sums = first_norm(tokens[0], d_hidden, norm1_gain, qkv_weight, grads)
+            norm_sums, sums[0] = lax.optimization_barrier((norm_sums, sums[0]))
+            extra = split_columns(as_columns([norm_sums.T]))
+        own_part = pair_weights(own_index, products, (other_part,) + extra)
+        blocks = own_part.reshape(experts, half_width // experts, own_part.shape[1])
+        if number < len(groups) - 1:
+            d_context, blocks = lax.optimization_barrier((d_context, blocks))
+        sums.append(jnp.sum(exchanged(blocks).astype(F32), axis=0))
+    d_w_in, d_w_down = expert_weights(mixed_rows, dy, act, du, 0, got)
+    expert_value = nn((full_place[:, None] == full_ids[None, :]).astype(BF16), y_back)
+    output = hidden + gate_value[:, None] * expert_value + expert_bias
+
+    sum_qkv = jnp.concatenate(
+        [
+            sums[g][:, i * count * LANES : (i + 1) * count * LANES]
+            for i in range(3)
+            for g, (begin, count) in enumerate(groups)
+        ],
+        axis=1,
+    )
+    sum_out = sums[0][:, 3 * groups[0][1] * LANES :]
+    sum_last = sums[-1][:, 3 * groups[-1][1] * LANES :]
     return (
         output.astype(BF16)[None],
         d_tokens[None],
+        sum_last[:, 0],
+        sum_last[:, 1],
+        sum_qkv,
         sum_last[:, 2],
         sum_last[:, 3],
-        jnp.concatenate([sum_query, sum_key, sum_value], axis=1),
-        sum_last[:, 0],
-        sum_last[:, 1],
         sum_out[:, :width],
         sum_out[:, width + experts + 3],
         sum_out[:, width + experts + 1],

time: 770 us -> 634 us (0.82)
  matrix products: 191 us -> 58.9 us
  starting transfers between devices: 190 us -> 106 us
  Pallas kernels: 230 us -> 312 us
  other arithmetic: 40 us -> 25.7 us
  waiting for transfers between devices: 84.2 us -> 94.3 us
    dot_general x18 -> x2, matrix products: 105 us -> 2.7 us  [tn(): lax.dot_general(left, right, (((0,), (0,)), ((), ())), preferred_element_...]
    pallas_call x0 -> x7, Pallas kernels: none -> 96.1 us  [the longest x2 52 us: expert_weights(): pl.pallas_call(partial(expert_weights_kernel, chunks, got is not None), g...]
    ppermute x9 -> x8, starting transfers between devices: 92.1 us -> 17.6 us  [swapped(): return lax.ppermute(array, 'fsdp', [(0, 1), (1, 0)])]
    ppermute x1 -> x2, waiting for transfers between devices: 0.01 us -> 32.2 us  [body(): returned = lax.ppermute(prev_grad, 'fsdp', [(1, 0)])]
    all_to_all x13 -> x8, waiting for transfers between devices: 79.3 us -> 55.9 us  [exchanged(): lax.all_to_all(array, 'expert', split_axis=0, concat_axis=0, tiled=True)]
    dot_general x5 -> x2, matrix products: 27.2 us -> 4.36 us  [nt(): lax.dot_general(left, right, (((1,), (1,)), ((), ())), preferred_element_...]
    pallas_call x2, Pallas kernels: 114 us -> 95.7 us  [run_expert(): pl.pallas_call(partial(expert_kernel, experts, block_r), grid_spec=pltpu....]
    all_to_all x13 -> x8, starting transfers between devices: 92.3 us -> 80.8 us  [exchanged(): lax.all_to_all(array, 'expert', split_axis=0, concat_axis=0, tiled=True)]
  transfers between devices with their start and end apart: 27 -> 22, of which waited for: 8 -> 7; matrix products, arithmetic and copies ran while one was open for 31% -> 15% of each run, Pallas kernels for 30% -> 47%
where the time goes in v2:
time: 634 us; the launch traced here: 626 us
  Pallas kernels  312 us (49%)
  starting transfers between devices  106 us (17%)
  waiting for transfers between devices  94.3 us (15%)
  matrix products  58.9 us (9%)
  other arithmetic  25.7 us (4%)
  between operations  15.7 us (2%)
  local copies, waits for them, and re-layouts  13.5 us (2%)
    pallas_call x2, Pallas kernels, run_expert(): pl.pallas_call(partial(expert_kernel, experts, block_r), grid_spec=pltpu....  95.7 us
    all_to_all x8, starting transfers between devices, exchanged(): lax.all_to_all(array, 'expert', split_axis=0, concat_axis=0, tiled=True)  80.8 us
    pallas_call x2, Pallas kernels, attention_backward(): pl.pallas_call(partial(backward_kernel, block_q, block_k), grid_spec=pltp...  71.6 us
    all_to_all x8, waiting for transfers between devices, exchanged(): lax.all_to_all(array, 'expert', split_axis=0, concat_axis=0, tiled=True)  55.9 us
    pallas_call x2, Pallas kernels, expert_weights(): pl.pallas_call(partial(expert_weights_kernel, chunks, got is not None), g...  52 us
    dot_general x10, matrix products, nn(): lax.dot_general(left, right, (((1,), (0,)), ((), ())), preferred_element_...  51.8 us
    pallas_call x1, Pallas kernels, attention_forward(): pl.pallas_call(partial(forward_kernel, block_q, block_k), grid_spec=pltpu...  48.3 us
    ppermute x2, waiting for transfers between devices, body(): returned = lax.ppermute(prev_grad, 'fsdp', [(1, 0)])  32.2 us
  transfers between devices with their start and end apart: 22, of which 7 were waited for; matrix products, arithmetic and copies ran while one was open for 15% of the time, Pallas kernels for 47%

profile of v2, /device:TPU:0, one launch (start us, length us, event | category | flops | bytes accessed | tf_op | source)
XLA Modules:
  0.0 625.6 jit_solution(16720750375279752101)
XLA Ops:
  17.6 6.2 maximum_select_fusion.w_ref
  23.9 6.0 add_convert_fusion.own_k_ref.own_v_ref
  34.7 6.2 fusion.17
  40.8 8.3 %all-to-all-start.1 = ((bf16[16,128,1024]{2,1,0:T(8,128)(2,1)}), bf16[16,128,1024]{2,1,0:T(8,128)(2,1)}, u32[]{:S(2)}, u32[]{:S(2)}) async-start(bf16[16,128,1024]{2,1,0:T(8,128)(2,1)} %bitcast.75), calls=%async_computation.1 | async-start | bytes 8388608 | tf_op jit(solution)/shard_map/all_to_all | solution.py:780
  51.1 5.2 multiply_convert_fusion.q_ref
  56.3 48.3 %attention_forward.1 = (bf16[1024,1024]{1,0:T(8,128)(2,1)}, f32[1024,1024]{1,0:T(8,128)}) custom-call(s32[2]{0:T(128)} %pad_add_fusion.scalars, bf16[1024,1024]{1,0:T(8,128)(2,1)} %multiply_convert_fusion.q_ref, bf16[1024,2048]{1,0:T(8,128)(2,1)} %collective-permute-done.2.prev_k_ref.prev_v_ref, ...), custom_call_target="tpu_custom_call" | custom-call | flops 42949672960 | bytes 16777216 | tf_op jit(solution)/shard_map/attention_forward/pallas_call | solution.py:194
  116.5 9.9 %all-to-all-done.1 = bf16[16,128,1024]{2,1,0:T(8,128)(2,1)} async-done(((bf16[16,128,1024]{2,1,0:T(8,128)(2,1)}), bf16[16,128,1024]{2,1,0:T(8,128)(2,1)}, u32[]{:S(2)}, u32[]{:S(2)}) %all-to-all-start.1) | async-done | bytes 4194336 | tf_op jit(solution)/shard_map/all_to_all | solution.py:780
  126.3 18.4 %all-to-all-start = ((bf16[16,64,1024]{2,1,0:T(8,128)(2,1)}), bf16[16,64,1024]{2,1,0:T(8,128)(2,1)S(1)}, u32[]{:S(2)}, u32[]{:S(2)}) async-start(bf16[16,64,1024]{2,1,0:T(8,128)(2,1)} %bitcast.81), calls=%async_computation | async-start | bytes 4194304 | tf_op jit(solution)/shard_map/all_to_all | solution.py:780
  144.7 5.3 fusion.29
  150.0 33.2 %all-to-all-done = bf16[16,64,1024]{2,1,0:T(8,128)(2,1)S(1)} async-done(((bf16[16,64,1024]{2,1,0:T(8,128)(2,1)}), bf16[16,64,1024]{2,1,0:T(8,128)(2,1)S(1)}, u32[]{:S(2)}, u32[]{:S(2)}) %all-to-all-start) | async-done | bytes 2097184 | tf_op jit(solution)/shard_map/all_to_all | solution.py:780
  183.2 12.9 %all-to-all-start.3 = ((bf16[16,64,1024]{2,1,0:T(8,128)(2,1)}), bf16[16,64,1024]{2,1,0:T(8,128)(2,1)}, u32[]{:S(2)}, u32[]{:S(2)}) async-start(bf16[16,64,1024]{2,1,0:T(8,128)(2,1)} %bitcast.77), calls=%async_computation.3 | async-start | bytes 4194304 | tf_op jit(solution)/shard_map/all_to_all | solution.py:780
  197.5 47.8 %expert_rows.2 = (bf16[16,2,64,1024]{3,2,1,0:T(8,128)(2,1)}, bf16[1024,1024]{1,0:T(8,128)(2,1)}, bf16[1024,4096]{1,0:T(8,128)(2,1)}, bf16[1024,4096]{1,0:T(8,128...) custom-call(s32[2]{0:T(128)} %pad_add_fusion.1.scalars.y_before_ref, bf16[1024,1024]{1,0:T(8,128)(2,1)} %bitcast.67, ...), custom_call_target="tpu_custom_call" | custom-call | flops 34359738368 | bytes 46137344 | tf_op jit(solution)/shard_map/expert_rows/pallas_call | solution.py:517
  245.3 7.1 %all-to-all-start.2 = ((bf16[16,64,1024]{2,1,0:T(8,128)(2,1)}), bf16[16,64,1024]{2,1,0:T(8,128)(2,1)S(1)}, u32[]{:S(2)}, u32[]{:S(2)}) async-start(bf16[16,64,1024]{2,1,0:T(8,128)(2,1)} %bitcast.79), calls=%async_computation.2 | async-start | bytes 4194304 | tf_op jit(solution)/shard_map/all_to_all | solution.py:780
  252.4 47.9 %expert_rows.3 = (bf16[16,2,64,1024]{3,2,1,0:T(8,128)(2,1)}, bf16[1024,1024]{1,0:T(8,128)(2,1)}, bf16[1024,4096]{1,0:T(8,128)(2,1)}, bf16[1024,4096]{1,0:T(8,128...) custom-call(s32[2]{0:T(128)} %pad_add_fusion.1.scalars.y_before_ref, ...), custom_call_target="tpu_custom_call", output_to_operand_aliasing={{0}: (6, {})} | custom-call | flops 34359738368 | bytes 46137344 | tf_op jit(solution)/shard_map/expert_rows/pallas_call | solution.py:517
  300.3 7.1 %all-to-all-start.4 = ((bf16[16,64,1024]{2,1,0:T(8,128)(2,1)}), bf16[16,64,1024]{2,1,0:T(8,128)(2,1)}, u32[]{:S(2)}, u32[]{:S(2)}) async-start(bf16[16,64,1024]{2,1,0:T(8,128)(2,1)} %bitcast.80), calls=%async_computation.4 | async-start | bytes 4194304 | tf_op jit(solution)/shard_map/all_to_all | solution.py:780
  307.4 25.3 %expert_weights.2 = (bf16[1024,2048]{1,0:T(8,128)(2,1)}, bf16[2048,1024]{1,0:T(8,128)(2,1)}) custom-call(bf16[1024,1024]{1,0:T(8,128)(2,1)} %bitcast.68, bf16[1024,1024]{1,0:T(8,128)(2,1)} %bitcast.22.rows_ref.refs_1_, bf16[1024,1024]{1,0:T(8,128)(2,1)} %get-tuple-element.55.refs_2_, bf16[1024,1024]{1,0:T(8,128)(2,1)} %get-tuple-element.56.refs_3_, ...), custom_call_target="tpu_custom_call" | custom-call | flops 17179869184 | bytes 41943040 | tf_op jit(solution)/shard_map/expert_weights/pallas_call | solution.py:604
  337.1 12.8 %all-to-all-done.4 = bf16[16,64,1024]{2,1,0:T(8,128)(2,1)} async-done(((bf16[16,64,1024]{2,1,0:T(8,128)(2,1)}), bf16[16,64,1024]{2,1,0:T(8,128)(2,1)}, u32[]{:S(2)}, u32[]{:S(2)}) %all-to-all-start.4) | async-done | bytes 2097184 | tf_op jit(solution)/shard_map/all_to_all | solution.py:780
  349.9 12.4 %all-to-all-start.5 = ((bf16[16,128,1024]{2,1,0:T(8,128)(2,1)}), bf16[16,128,1024]{2,1,0:T(8,128)(2,1)}, u32[]{:S(2)}, u32[]{:S(2)}) async-start(bf16[16,128,1024]{2,1,0:T(8,128)(2,1)} %bitcast.76), calls=%async_computation.5 | async-start | bytes 8388608 | tf_op jit(solution)/shard_map/all_to_all | solution.py:780
  362.4 7.0 %multiply_reduce_fusion = (f32[1024]{0:T(1024)S(1)}, f32[1024]{0:T(1024)S(1)}, f32[1024]{0:T(1024)S(1)}, f32[1024]{0:T(1024)S(1)}, f32[1024,1024]{1,0:T(8,128)S(1)}) fusion(f32[1024,1024]{1,0:T(8,128)} %copy-done.1, f32[1024]{0:T(1024)S(1)} %add_rsqrt_fusion, f32[1024]{0:T(1024)S(1)} %broadcast_multiply_fusion.2, f32[1024]{0:T(1024)S(1)} %bitcast.83, ...), kind=kOutput, calls=%fused_computation.22 | convolution fusion | flops 2159013888 | bytes 14712832 | tf_op jit(solution)/shard_map/dot_general | solution.py:25
  376.6 43.8 %attention_backward.2 = (bf16[1024,640]{1,0:T(8,128)(2,1)}, bf16[2,1024,640]{2,1,0:T(8,128)(2,1)}, bf16[2,1024,640]{2,1,0:T(8,128)(2,1)}) custom-call(s32[2]{0:T(128)} %pad_add_fusion.scalars, bf16[1024,1024]{1,0:T(8,128)(2,1)} %multiply_convert_fusion.q_ref, bf16[1024,2048]{1,0:T(8,128)(2,1)} %collective-permute-done.2.prev_k_ref.prev_v_ref, ...), custom_call_target="tpu_custom_call" | custom-call | flops 40265318400 | bytes 17039360 | tf_op jit(solution)/shard_map/attention_backward/pallas_call | solution.py:384
  421.9 30.3 %collective-permute-done.3 = bf16[2,1024,640]{2,1,0:T(8,128)(2,1)S(1)} collective-permute-done((bf16[2,1024,640]{2,1,0:T(8,128)(2,1)}, bf16[2,1024,640]{2,1,0:T(8,128)(2,1)S(1)}, u32[]{:S(2)}, u32[]{:S(2)}) %collective-permute-start.3) | collective-permute-done | bytes 2621472 | tf_op jit(solution)/shard_map/ppermute | solution.py:968
  456.2 8.8 %pair_weights.4 = bf16[512,2944]{1,0:T(8,128)(2,1)} custom-call(s32[1]{0:T(128)S(6)} %sub.58.scalars, bf16[1024,1024]{1,0:T(8,128)(2,1)} %copy-done, bf16[1024,640]{1,0:T(8,128)(2,1)} %get-tuple-element.68.refs_1_.refs_0_, bf16[2,1024,640]{2,1,0:T(8,128)(2,1)} %add_convert_fusion.1.refs_2_.refs_1_, bf16[1024,1024]{1,0:T(8,128)(2,1)} %get-tuple-element.50.out_ref.refs_3_, ...), custom_call_target="tpu_custom_call" | custom-call | flops 3087007744 | bytes 18087936 | tf_op jit(solution)/shard_map/pair_weights/pallas_call | solution.py:664
  474.1 9.7 %pair_weights.5 = bf16[512,3072]{1,0:T(8,128)(2,1)} custom-call(s32[1]{0:T(128)} %bitcast.1.scalars, bf16[1024,1024]{1,0:T(8,128)(2,1)} %copy-done, bf16[1024,640]{1,0:T(8,128)(2,1)} %get-tuple-element.68.refs_1_.refs_0_, bf16[2,1024,640]{2,1,0:T(8,128)(2,1)} %add_convert_fusion.1.refs_2_.refs_1_, bf16[1024,1024]{1,0:T(8,128)(2,1)} %get-tuple-element.50.out_ref.refs_3_, ...), custom_call_target="tpu_custom_call" | custom-call | flops 3087007744 | bytes 18874368 | tf_op jit(solution)/shard_map/pair_weights/pallas_call | solution.py:664
  483.8 7.6 %all-to-all-start.6 = ((bf16[16,32,3072]{2,1,0:T(8,128)(2,1)}), bf16[16,32,3072]{2,1,0:T(8,128)(2,1)S(1)}, u32[]{:S(2)}, u32[]{:S(2)}) async-start(bf16[16,32,3072]{2,1,0:T(8,128)(2,1)} %bitcast.71), calls=%async_computation.6 | async-start | bytes 6291456 | tf_op jit(solution)/shard_map/all_to_all | solution.py:780
  491.5 27.8 %attention_backward.3 = (bf16[1024,384]{1,0:T(8,128)(2,1)}, bf16[2,1024,384]{2,1,0:T(8,128)(2,1)}, bf16[2,1024,384]{2,1,0:T(8,128)(2,1)}) custom-call(s32[2]{0:T(128)} %pad_add_fusion.scalars, bf16[1024,1024]{1,0:T(8,128)(2,1)} %multiply_convert_fusion.q_ref, bf16[1024,2048]{1,0:T(8,128)(2,1)} %collective-permute-done.2.prev_k_ref.prev_v_ref, ...), custom_call_target="tpu_custom_call" | custom-call | flops 24159191040 | bytes 10223616 | tf_op jit(solution)/shard_map/attention_backward/pallas_call | solution.py:384
  520.9 15.7 %collective-permute-start.9 = (bf16[1024,2048]{1,0:T(8,128)(2,1)}, bf16[1024,2048]{1,0:T(8,128)(2,1)}, u32[]{:S(2)}, u32[]{:S(2)}) collective-permute-start(bf16[1024,2048]{1,0:T(8,128)(2,1)} %get-tuple-element.81), channel_id=1, source_target_pairs={{0,16},{16,0},{1,17},{17,1},{2,18},{18,2},{3,19},{19,3},{4,20},{20... | collective-permute-start | bytes 12582920 | tf_op jit(solution)/shard_map/ppermute | solution.py:776
  542.2 4.8 pair_weights.6
  547.1 15.5 %first_norm.1 = (bf16[1024,1024]{1,0:T(8,128)(2,1)}, f32[8,1024]{1,0:T(8,128)}) custom-call(bf16[1024,1024]{1,0:T(8,128)(2,1)} %bitcast.66, f32[1024,1024]{1,0:T(8,128)} %get-tuple-element.159.dh_ref, f32[1,1024]{1,0:T(1,128)} %copy-done.26, bf16[1024,3072]{1,0:T(8,128)(2,1)} %copy-done.10, bf16[1024,640]{1,0:T(8,128)(2,1)} %get-tuple-element.68.refs_1_.refs_0_, ...), custom_call_target="tpu_custom_call" | custom-call | flops 6442450944 | bytes 20971520 | tf_op jit(solution)/shard_map/first_norm/pallas_call | solution.py:734
  566.9 5.3 pair_weights.7
  572.2 7.0 %all-to-all-start.7 = ((bf16[16,32,1280]{2,1,0:T(8,128)(2,1)}), bf16[16,32,1280]{2,1,0:T(8,128)(2,1)S(1)}, u32[]{:S(2)}, u32[]{:S(2)}) async-start(bf16[16,32,1280]{2,1,0:T(8,128)(2,1)} %bitcast.72), calls=%async_computation.7 | async-start | bytes 2621440 | tf_op jit(solution)/shard_map/all_to_all | solution.py:780
  579.2 8.8 %fusion.20 = bf16[1,1024,1024]{2,1,0:T(8,128)(2,1)} fusion(f32[1024,1024]{1,0:T(8,128)} %copy-done.1, f32[1024]{0:T(1024)S(1)} %bitcast.95, f32[1024]{0:T(1024)S(1)} %select_reduce_fusion, bf16[2048,1024]{1,0:T(8,128)(2,1)} %bitcast.26, s32[1024]{0:T(1024)S(1)} %copy-done.29), kind=kOutput, calls=%fused_computation.45 | convolution fusion | flops 4301258752 | bytes 10498048 | tf_op jit(solution)/shard_map/dot_general | solution.py:25
  588.1 26.6 %expert_weights.3 = (f32[1024,2048]{1,0:T(8,128)}, f32[2048,1024]{1,0:T(8,128)}) custom-call(bf16[1024,1024]{1,0:T(8,128)(2,1)} %bitcast.69, bf16[1024,1024]{1,0:T(8,128)(2,1)} %bitcast.22.rows_ref.refs_1_, bf16[1024,1024]{1,0:T(8,128)(2,1)} %get-tuple-element.55.refs_2_, bf16[1024,1024]{1,0:T(8,128)(2,1)} %get-tuple-element.56.refs_3_, ...), custom_call_target="tpu_custom_call" | custom-call | flops 17179869184 | bytes 41943040 | tf_op jit(solution)/shard_map/expert_weights/pallas_call | solution.py:604
  (174 shorter events, 70.5 us)
Async XLA Ops:
  7.3 97.4 %all-gather.4.cloned.1.call-start = ((), (), s32[]{:S(2)}) async-start(), calls=%async_computation.8 | async-start | bytes 3145728 | tf_op jit(solution)/shard_map/all_gather | solution.py:842
  8.0 189.5 %all-gather.6.cloned.1.call-start = ((), (), s32[]{:S(2)}) async-start(), calls=%async_computation.9 | async-start | bytes 12582912 | tf_op jit(solution)/shard_map/all_gather | solution.py:843
  8.8 8.8 %collective-permute-start.1 = (bf16[512,3072]{1,0:T(8,128)(2,1)}, bf16[512,3072]{1,0:T(8,128)(2,1)}, u32[]{:S(2)}, u32[]{:S(2)}) collective-permute-start(bf16[512,3072]{1,0:T(8,128)(2,1)} %param.23), channel_id=1, source_target_pairs={{0,16},{16,0},{1,17},{17,1},{2,18},{18,2},{3,19},{19,3},{4,20},{20... | collective-permute-start | bytes 9437192 | tf_op jit(solution)/shard_map/ppermute | solution.py:776
  9.5 5.0 collective-permute-start
  14.5 182.2 %copy-start.16 = (bf16[24,1024]{1,0:T(8,128)(2,1)}, bf16[24,1024]{1,0:T(8,128)(2,1)S(1)}, u32[]{:S(2)}) copy-start(bf16[24,1024]{1,0:T(8,128)(2,1)S(1)} %maximum_select_fusion.1) | copy-start | bytes 147460
  17.6 33.5 %copy-start = (bf16[1024,1024]{1,0:T(8,128)(2,1)}, bf16[1024,1024]{1,0:T(8,128)(2,1)S(1)}, u32[]{:S(2)}) copy-start(bf16[1024,1024]{1,0:T(8,128)(2,1)S(1)} %fusion.7.refs_0_) | copy-start | bytes 6291460
  23.9 10.2 %copy-start.24 = (s32[1,1024,1]{1,2,0:T(1,128)S(1)}, s32[1,1024,1]{1,2,0:T(1,128)}, u32[]{:S(2)}) copy-start(s32[1,1024,1]{1,2,0:T(1,128)} %param.19) | copy-start | bytes 12292
  23.9 10.8 %copy-start.13 = (bf16[1,1024,1024]{2,1,0:T(8,128)(2,1)S(1)}, bf16[1,1024,1024]{2,1,0:T(8,128)(2,1)}, u32[]{:S(2)}) copy-start(bf16[1,1024,1024]{2,1,0:T(8,128)(2,1)} %param.18) | copy-start | bytes 6291460
  30.0 26.4 %collective-permute-start.2 = (bf16[1024,2048]{1,0:T(8,128)(2,1)}, bf16[1024,2048]{1,0:T(8,128)(2,1)}, u32[]{:S(2)}, u32[]{:S(2)}) collective-permute-start(bf16[1024,2048]{1,0:T(8,128)(2,1)} %add_convert_fusion.own_k_ref.own_v_ref), channel_id=1, source_target_pairs={{0,16},{1,17},{2,18},{3,19},{4,20},{5,21},{6,22},{7,23},{8,24},{9,... | collective-permute-start | bytes 12582920 | tf_op jit(solution)/shard_map/ppermute | solution.py:890
  40.8 85.5 %all-to-all-start.1 = ((bf16[16,128,1024]{2,1,0:T(8,128)(2,1)}), bf16[16,128,1024]{2,1,0:T(8,128)(2,1)}, u32[]{:S(2)}, u32[]{:S(2)}) async-start(bf16[16,128,1024]{2,1,0:T(8,128)(2,1)} %bitcast.75), calls=%async_computation.1 | async-start | bytes 8388608 | tf_op jit(solution)/shard_map/all_to_all | solution.py:780
  49.1 148.4 %all-gather.8.cloned.1.call-start = ((), (), s32[]{:S(2)}) async-start(), calls=%async_computation.10 | async-start | bytes 12582912 | tf_op jit(solution)/shard_map/all_gather | solution.py:844
  56.3 48.3 %copy-start.5 = (bf16[1,1024,1024]{2,1,0:T(8,128)(2,1)S(1)}, bf16[1,1024,1024]{2,1,0:T(8,128)(2,1)}, u32[]{:S(2)}) copy-start(bf16[1,1024,1024]{2,1,0:T(8,128)(2,1)} %param.17) | copy-start | bytes 6291460
  126.3 56.9 %all-to-all-start = ((bf16[16,64,1024]{2,1,0:T(8,128)(2,1)}), bf16[16,64,1024]{2,1,0:T(8,128)(2,1)S(1)}, u32[]{:S(2)}, u32[]{:S(2)}) async-start(bf16[16,64,1024]{2,1,0:T(8,128)(2,1)} %bitcast.81), calls=%async_computation | async-start | bytes 4194304 | tf_op jit(solution)/shard_map/all_to_all | solution.py:780
  183.2 14.3 %copy-start.6 = (bf16[16,64,1024]{2,1,0:T(8,128)(2,1)}, bf16[16,64,1024]{2,1,0:T(8,128)(2,1)S(1)}, u32[]{:S(2)}) copy-start(bf16[16,64,1024]{2,1,0:T(8,128)(2,1)S(1)} %all-to-all-done) | copy-start | bytes 6291460
  183.2 62.1 %all-to-all-start.3 = ((bf16[16,64,1024]{2,1,0:T(8,128)(2,1)}), bf16[16,64,1024]{2,1,0:T(8,128)(2,1)}, u32[]{:S(2)}, u32[]{:S(2)}) async-start(bf16[16,64,1024]{2,1,0:T(8,128)(2,1)} %bitcast.77), calls=%async_computation.3 | async-start | bytes 4194304 | tf_op jit(solution)/shard_map/all_to_all | solution.py:780
  245.3 55.0 %all-to-all-start.2 = ((bf16[16,64,1024]{2,1,0:T(8,128)(2,1)}), bf16[16,64,1024]{2,1,0:T(8,128)(2,1)S(1)}, u32[]{:S(2)}, u32[]{:S(2)}) async-start(bf16[16,64,1024]{2,1,0:T(8,128)(2,1)} %bitcast.79), calls=%async_computation.2 | async-start | bytes 4194304 | tf_op jit(solution)/shard_map/all_to_all | solution.py:780
  300.3 49.6 %all-to-all-start.4 = ((bf16[16,64,1024]{2,1,0:T(8,128)(2,1)}), bf16[16,64,1024]{2,1,0:T(8,128)(2,1)}, u32[]{:S(2)}, u32[]{:S(2)}) async-start(bf16[16,64,1024]{2,1,0:T(8,128)(2,1)} %bitcast.80), calls=%async_computation.4 | async-start | bytes 4194304 | tf_op jit(solution)/shard_map/all_to_all | solution.py:780
  349.9 106.3 %all-to-all-start.5 = ((bf16[16,128,1024]{2,1,0:T(8,128)(2,1)}), bf16[16,128,1024]{2,1,0:T(8,128)(2,1)}, u32[]{:S(2)}, u32[]{:S(2)}) async-start(bf16[16,128,1024]{2,1,0:T(8,128)(2,1)} %bitcast.76), calls=%async_computation.5 | async-start | bytes 8388608 | tf_op jit(solution)/shard_map/all_to_all | solution.py:780
  420.5 31.8 %collective-permute-start.3 = (bf16[2,1024,640]{2,1,0:T(8,128)(2,1)}, bf16[2,1024,640]{2,1,0:T(8,128)(2,1)S(1)}, u32[]{:S(2)}, u32[]{:S(2)}) collective-permute-start(bf16[2,1024,640]{2,1,0:T(8,128)(2,1)} %get-tuple-element.65), channel_id=1, source_target_pairs={{16,0},{17,1},{18,2},{19,3},{20,4},{21,5},{22,6},{23,7},{24,8},{25... | collective-permute-start | bytes 7864328 | tf_op jit(solution)/shard_map/ppermute | solution.py:968
  465.0 6.8 %collective-permute-start.4 = (bf16[512,2944]{1,0:T(8,128)(2,1)}, bf16[512,2944]{1,0:T(8,128)(2,1)S(1)}, u32[]{:S(2)}, u32[]{:S(2)}) collective-permute-start(bf16[512,2944]{1,0:T(8,128)(2,1)} %pair_weights.4), channel_id=1, source_target_pairs={{0,16},{16,0},{1,17},{17,1},{2,18},{18,2},{3,19},{19,3},{4,20},{20... | collective-permute-start | bytes 9043976 | tf_op jit(solution)/shard_map/ppermute | solution.py:776
  470.3 1.5 collective-permute-start.5
  483.8 78.8 %all-to-all-start.6 = ((bf16[16,32,3072]{2,1,0:T(8,128)(2,1)}), bf16[16,32,3072]{2,1,0:T(8,128)(2,1)S(1)}, u32[]{:S(2)}, u32[]{:S(2)}) async-start(bf16[16,32,3072]{2,1,0:T(8,128)(2,1)} %bitcast.71), calls=%async_computation.6 | async-start | bytes 6291456 | tf_op jit(solution)/shard_map/all_to_all | solution.py:780
  491.5 45.2 %copy-start.9 = (bf16[1024,1024]{1,0:T(8,128)(2,1)S(1)}, bf16[1024,1024]{1,0:T(8,128)(2,1)}, u32[]{:S(2)}) copy-start(bf16[1024,1024]{1,0:T(8,128)(2,1)} %copy-done.8) | copy-start | bytes 6291460
  491.5 45.1 %copy-start.17 = (bf16[24,1024]{1,0:T(8,128)(2,1)S(1)}, bf16[24,1024]{1,0:T(8,128)(2,1)}, u32[]{:S(2)}) copy-start(bf16[24,1024]{1,0:T(8,128)(2,1)} %copy-done.16) | copy-start | bytes 147460
  519.3 19.9 %collective-permute-start.6 = (bf16[2,1024,384]{2,1,0:T(8,128)(2,1)}, bf16[2,1024,384]{2,1,0:T(8,128)(2,1)S(1)}, u32[]{:S(2)}, u32[]{:S(2)}) collective-permute-start(bf16[2,1024,384]{2,1,0:T(8,128)(2,1)} %get-tuple-element.75), channel_id=1, source_target_pairs={{16,0},{17,1},{18,2},{19,3},{20,4},{21,5},{22,6},{23,7},{24,8},{25... | collective-permute-start | bytes 4718600 | tf_op jit(solution)/shard_map/ppermute | solution.py:968
  520.9 67.2 %collective-permute-start.9 = (bf16[1024,2048]{1,0:T(8,128)(2,1)}, bf16[1024,2048]{1,0:T(8,128)(2,1)}, u32[]{:S(2)}, u32[]{:S(2)}) collective-permute-start(bf16[1024,2048]{1,0:T(8,128)(2,1)} %get-tuple-element.81), channel_id=1, source_target_pairs={{0,16},{16,0},{1,17},{17,1},{2,18},{18,2},{3,19},{19,3},{4,20},{20... | collective-permute-start | bytes 12582920 | tf_op jit(solution)/shard_map/ppermute | solution.py:776
  536.5 51.5 %collective-permute-start.10 = (bf16[2048,1024]{1,0:T(8,128)(2,1)}, bf16[2048,1024]{1,0:T(8,128)(2,1)}, u32[]{:S(2)}, u32[]{:S(2)}) collective-permute-start(bf16[2048,1024]{1,0:T(8,128)(2,1)} %get-tuple-element.82), channel_id=1, source_target_pairs={{0,16},{16,0},{1,17},{17,1},{2,18},{18,2},{3,19},{19,3},{4,20},{20... | collective-permute-start | bytes 12582920 | tf_op jit(solution)/shard_map/ppermute | solution.py:776
  547.0 19.3 %collective-permute-start.7 = (bf16[512,1152]{1,0:T(8,128)(2,1)}, bf16[512,1152]{1,0:T(8,128)(2,1)}, u32[]{:S(2)}, u32[]{:S(2)}) collective-permute-start(bf16[512,1152]{1,0:T(8,128)(2,1)} %pair_weights.6), channel_id=1, source_target_pairs={{0,16},{16,0},{1,17},{17,1},{2,18},{18,2},{3,19},{19,3},{4,20},{20... | collective-permute-start | bytes 3538952 | tf_op jit(solution)/shard_map/ppermute | solution.py:776
  564.2 2.0 collective-permute-start.8
  566.2 13.0 %copy-start.27 = (f32[1,1024]{1,0:T(1,128)S(1)}, f32[1,1024]{1,0:T(1,128)}, u32[]{:S(2)}) copy-start(f32[1,1024]{1,0:T(1,128)} %get-tuple-element.162) | copy-start | bytes 12292
  566.3 13.0 %copy-start.29 = (s32[1024]{0:T(1024)S(1)}, s32[1024]{0:T(1024)}, u32[]{:S(2)}) copy-start(s32[1024]{0:T(1024)} %copy-done.28) | copy-start | bytes 12292
  572.2 44.6 %all-to-all-start.7 = ((bf16[16,32,1280]{2,1,0:T(8,128)(2,1)}), bf16[16,32,1280]{2,1,0:T(8,128)(2,1)S(1)}, u32[]{:S(2)}, u32[]{:S(2)}) async-start(bf16[16,32,1280]{2,1,0:T(8,128)(2,1)} %bitcast.72), calls=%async_computation.7 | async-start | bytes 2621440 | tf_op jit(solution)/shard_map/all_to_all | solution.py:780
  (29 other events, 103.3 us)
Sparse Core Ops, SparseCore 0:
  9.7 13.2 all-gather.3
  24.5 21.0 all-gather.5
  51.5 21.0 all-gather.7

commit v3 on v2

v3 whole, which is shorter than its diff:
```python
from functools import partial

import jax
import jax.numpy as jnp
from jax import lax
from jax.experimental import pallas as pl
from jax.experimental.pallas import tpu as pltpu
from jax.sharding import PartitionSpec as P

HEAD_DIM = 64
NORM_EPSILON = 1e-05
MASK_FILL = -1e30
LOG2E = 1.4426950408889634
SAFE_LOG2 = 90.0
GELU_A = 0.7978845608028654
GELU_B = 0.044715
CHUNKS = 2
BWD_Q = 512
BWD_K = 512
FIRST_PAIRS = 4
LANES = 128
BF16 = jnp.bfloat16
F32 = jnp.float32
VMEM_LIMIT = 56 << 20


def nn(left, right):
    return lax.dot_general(left, right, (((1,), (0,)), ((), ())), preferred_element_type=F32)


def nt(left, right):
    return lax.dot_general(left, right, (((1,), (1,)), ((), ())), preferred_element_type=F32)


def tn(left, right):
    return lax.dot_general(left, right, (((0,), (0,)), ((), ())), preferred_element_type=F32)


def lane_index(rows):
    return lax.broadcasted_iota(jnp.int32, (rows, LANES), 1)


def in_three(values):
    high = values.astype(BF16).astype(F32)
    rest = values - high
    middle = rest.astype(BF16).astype(F32)
    return high, middle, rest - middle


def three_columns(values, place):
    high, middle, low = in_three(values)
    return jnp.where(
        place == 0, high, jnp.where(place == 1, middle, jnp.where(place == 2, low, 0.0))
    )


def forward_kernel(
    block,
    scalars,
    q_ref,
    prev_k_ref,
    prev_v_ref,
    own_k_ref,
    own_v_ref,
    out_ref,
    lse_ref,
    values_one,
    query_parts,
    keys_both,
    total,
    top,
):
    rows = q_ref.shape[0]
    has_prev, own_prefix = scalars[0], scalars[1]
    lane = lane_index(rows)
    first = lane < HEAD_DIM
    zero = jnp.zeros((rows, LANES), BF16)
    one = jnp.ones((rows, LANES), BF16)
    own_values, prev_values = own_v_ref[...], prev_v_ref[...]
    values_one[0, 0] = jnp.where(first, prev_values, one)
    values_one[1, 0] = jnp.where(first, one, prev_values)
    values_one[0, 1] = jnp.where(first, own_values, one)
    values_one[1, 1] = jnp.where(first, one, own_values)
    scaled = q_ref[...].astype(F32) * LOG2E
    high = scaled.astype(BF16)
    low = (scaled - high.astype(F32)).astype(BF16)
    query_parts[0, :, :LANES] = jnp.where(first, high, zero)
    query_parts[0, :, LANES:] = jnp.where(first, low, zero)
    query_parts[1, :, :LANES] = jnp.where(first, zero, high)
    query_parts[1, :, LANES:] = jnp.where(first, zero, low)

    same_head = (
        lax.broadcasted_iota(jnp.int32, (LANES, LANES), 0) < HEAD_DIM
    ) == (lax.broadcasted_iota(jnp.int32, (LANES, LANES), 1) < HEAD_DIM)
    same_head = jnp.where(same_head, 1.0, 0.0).astype(BF16)

    def longest(ref):
        values = ref[...].astype(F32)
        return jnp.max(nn((values * values).astype(BF16), same_head), axis=0, keepdims=True)

    keys_longest = jnp.maximum(longest(own_k_ref), longest(prev_k_ref))
    small = jnp.max(longest(q_ref) * keys_longest) < (SAFE_LOG2 / LOG2E) ** 2
    keys_both[0] = prev_k_ref[...]
    keys_both[1] = own_k_ref[...]
    first_part = jnp.where(has_prev > 0, 0, 1)
    total[...] = jnp.zeros_like(total)

    def scores_of(h, keys, queries_at, size_q, part, at, size_k):
        scores = nt(query_parts[h, queries_at, :], keys)
        key_pos = at + (part - 1) * rows + lax.broadcasted_iota(jnp.int32, (1, size_k), 1)
        query_pos = queries_at.start + lax.broadcasted_iota(jnp.int32, (size_q, 1), 0)
        visible = key_pos <= jnp.maximum(query_pos, own_prefix - 1)
        return jnp.where(visible, scores, MASK_FILL)

    def keys_twice(part, at, size):
        keys = keys_both[part, pl.ds(at, size), :]
        return jnp.concatenate([keys, keys], axis=1)

    @pl.when(small)
    def _():
        top[...] = jnp.zeros_like(top)

        def add_up(part, carried):
            keys = keys_twice(part, 0, rows)
            for h in range(2):
                scores = scores_of(h, keys, pl.ds(0, rows), rows, part, 0, rows)
                total[h] += nn(jnp.exp2(scores).astype(BF16), values_one[h, part])
            return carried

        lax.fori_loop(first_part, 2, add_up, 0)

    @pl.when(jnp.logical_not(small))
    def _():
        size = block
        blocks = rows // size
        lane = lane_index(size)
        place = lane & (HEAD_DIM - 1)
        three = jnp.where(place < 3, 1.0, 0.0).astype(BF16)

        def queries_block(i, carried):
            here = pl.ds(pl.multiple_of(i * size, size), size)

            def over_keys(visit):
                def one(n, carried):
                    part = n // blocks
                    visit(part, pl.multiple_of(lax.rem(n, blocks) * size, size))
                    return carried

                lax.fori_loop(first_part * blocks, 2 * blocks, one, 0)

            for h in range(2):
                top[h, here, :] = jnp.full((size, LANES), MASK_FILL, F32)

                def find_top(part, at):
                    keys = keys_twice(part, at, size)
                    scores = scores_of(h, keys, here, size, part, at, size)
                    largest = top[h, here, :]
                    for t in range(size // LANES):
                        largest = jnp.maximum(largest, scores[:, t * LANES : (t + 1) * LANES])
                    top[h, here, :] = largest

                over_keys(find_top)
                maximum = jnp.max(top[h, here, :], axis=1, keepdims=True)
                maximum = jnp.broadcast_to(maximum, (size, LANES))
                top[h, here, :] = maximum
                mine = (lane < HEAD_DIM) == (h == 0)
                less = jnp.where(mine, three_columns(-maximum, place), 0.0).astype(BF16)

                def add_up(part, at):
                    keys = keys_twice(part, at, size)
                    scores = scores_of(h, keys, here, size, part, at, size) + nt(less, three)
                    weights = jnp.exp2(scores).astype(BF16)
                    total[h, here, :] += nn(weights, values_one[h, part, pl.ds(at, size), :])

                over_keys(add_up)
            return carried

        lax.fori_loop(0, blocks, queries_block, 0)

    sum_a, sum_b = total[0], total[1]
    weight = jnp.where(first, pltpu.roll(sum_a, HEAD_DIM, 1), pltpu.roll(sum_b, HEAD_DIM, 1))
    out_ref[...] = (jnp.where(first, sum_a, sum_b) / weight).astype(BF16)
    lse_ref[...] = jnp.where(first, top[0], top[1]) * (1.0 / LOG2E) + jnp.log(weight)


def attention_forward(scalars, queries, prev, own, block=512):
    rows, width = queries.shape
    pairs = width // LANES

    def spec(offset):
        return pl.BlockSpec((rows, LANES), lambda h, scalars: (0, h + offset))

    return pl.pallas_call(
        partial(forward_kernel, block),
        grid_spec=pltpu.PrefetchScalarGridSpec(
            num_scalar_prefetch=1,
            grid=(pairs,),
            in_specs=[spec(0), spec(0), spec(pairs), spec(0), spec(pairs)],
            out_specs=[spec(0), spec(0)],
            scratch_shapes=[
                pltpu.VMEM((2, 2, rows, LANES), BF16),
                pltpu.VMEM((2, rows, 2 * LANES), BF16),
                pltpu.VMEM((2, rows, LANES), BF16),
                pltpu.VMEM((2, rows, LANES), F32),
                pltpu.VMEM((2, rows, LANES), F32),
            ],
        ),
        out_shape=[
            jax.ShapeDtypeStruct((rows, width), BF16),
            jax.ShapeDtypeStruct((rows, width), F32),
        ],
        compiler_params=pltpu.CompilerParams(vmem_limit_bytes=VMEM_LIMIT),
        cost_estimate=pl.CostEstimate(
            flops=4 * rows * rows * width,
            bytes_accessed=16 * rows * width,
            transcendentals=rows * rows,
        ),
        name="attention_forward",
    )(scalars, queries, prev, prev, own, own)


def over_visible(has_prev, own_prefix, rows, block_q, block_k, begin, visit, end):
    query_blocks, key_blocks = rows // block_q, rows // block_k

    def one_block(j, carried):
        line = pl.multiple_of(j * block_k, block_k)
        at = line - rows
        begin()
        seen_by_all = (at < 0) | (own_prefix > at)
        first_seen = jnp.where(seen_by_all, 0, jnp.maximum(at, 0) // block_q)

        def step(i, carried):
            visit(line, pl.multiple_of(i * block_q, block_q))
            return carried

        lax.fori_loop(first_seen, query_blocks, step, 0)
        end(line)
        return carried

    lax.fori_loop(jnp.where(has_prev > 0, 0, key_blocks), 2 * key_blocks, one_block, 0)


def weights_kernel(
    block_q, block_k, scalars, q_ref, prev_k_ref, own_k_ref, lse_ref, weights_ref, query_aug, keys_both
):
    rows = q_ref.shape[0]
    has_prev, own_prefix = scalars[0], scalars[1]
    lane = lane_index(rows)
    first = lane < HEAD_DIM
    zero = jnp.zeros((rows, LANES), BF16)
    queries = q_ref[...]
    less = three_columns(-lse_ref[...], lane & (HEAD_DIM - 1)).astype(BF16)
    query_aug[0, :, :LANES] = jnp.where(first, queries, zero)
    query_aug[0, :, LANES:] = jnp.where(first, less, zero)
    query_aug[1, :, :LANES] = jnp.where(first, zero, queries)
    query_aug[1, :, LANES:] = jnp.where(first, zero, less)
    ones = jnp.where((lane_index(block_k) & (HEAD_DIM - 1)) < 3, 1.0, 0.0).astype(BF16)

    keys_both[:rows] = prev_k_ref[...]
    keys_both[rows:] = own_k_ref[...]

    def visit(line, start):
        keys_aug = jnp.concatenate([keys_both[pl.ds(line, block_k), :], ones], axis=1)
        key_pos = line - rows + lax.broadcasted_iota(jnp.int32, (block_k, 1), 0)
        query_pos = start + lax.broadcasted_iota(jnp.int32, (1, block_q), 1)
        visible = key_pos <= jnp.maximum(query_pos, own_prefix - 1)
        for h in range(2):
            scores = nt(keys_aug, query_aug[h, pl.ds(start, block_q), :]) * LOG2E
            scores = jnp.where(visible, scores, MASK_FILL)
            weights_ref[h, pl.ds(line, block_k), pl.ds(start, block_q)] = jnp.exp2(
                scores
            ).astype(BF16)

    def nothing(*unused):
        return None

    over_visible(has_prev, own_prefix, rows, block_q, block_k, nothing, visit, nothing)


def attention_weights(scalars, queries, prev, own, lse, block_q=1024, block_k=512):
    rows, width = queries.shape
    pairs = width // LANES
    spec = pl.BlockSpec((rows, LANES), lambda h, scalars: (0, h))
    return pl.pallas_call(
        partial(weights_kernel, block_q, block_k),
        grid_spec=pltpu.PrefetchScalarGridSpec(
            num_scalar_prefetch=1,
            grid=(pairs,),
            in_specs=[spec] * 4,
            out_specs=pl.BlockSpec((None, 2, 2 * rows, rows), lambda h, scalars: (h, 0, 0, 0)),
            scratch_shapes=[
                pltpu.VMEM((2, rows, 2 * LANES), BF16),
                pltpu.VMEM((2 * rows, LANES), BF16),
            ],
        ),
        out_shape=jax.ShapeDtypeStruct((pairs, 2, 2 * rows, rows), BF16),
        compiler_params=pltpu.CompilerParams(vmem_limit_bytes=VMEM_LIMIT),
        cost_estimate=pl.CostEstimate(
            flops=8 * rows * rows * width,
            bytes_accessed=4 * pairs * rows * rows * 2 + 10 * rows * width,
            transcendentals=2 * rows * rows * width // HEAD_DIM,
        ),
        name="attention_weights",
    )(scalars, queries, prev, own, lse)


def backward_kernel(
    block_q,
    block_k,
    scalars,
    q_ref,
    prev_k_ref,
    prev_v_ref,
    own_k_ref,
    own_v_ref,
    out_ref,
    grad_ref,
    weights_ref,
    dq_ref,
    prev_grad_ref,
    own_grad_ref,
    grad_aug,
    keys_both,
    values_both,
    dq_total,
    dk_total,
    dv_total,
):
    rows = q_ref.shape[0]
    has_prev, own_prefix = scalars[0], scalars[1]
    lane = lane_index(rows)
    first = lane < HEAD_DIM
    zero = jnp.zeros((rows, LANES), BF16)
    grads = grad_ref[...]
    products = grads.astype(F32) * out_ref[...].astype(F32)
    delta_a = jnp.sum(jnp.where(first, products, 0.0), axis=1, keepdims=True)
    delta_b = jnp.sum(jnp.where(first, 0.0, products), axis=1, keepdims=True)
    less = three_columns(-jnp.where(first, delta_a, delta_b), lane & (HEAD_DIM - 1)).astype(BF16)
    grad_aug[0, :, :LANES] = jnp.where(first, grads, zero)
    grad_aug[0, :, LANES:] = jnp.where(first, less, zero)
    grad_aug[1, :, :LANES] = jnp.where(first, zero, grads)
    grad_aug[1, :, LANES:] = jnp.where(first, zero, less)
    ones = jnp.where((lane_index(block_k) & (HEAD_DIM - 1)) < 3, 1.0, 0.0).astype(BF16)
    keys_first = lane_index(block_k) < HEAD_DIM
    queries_first = lane_index(block_q) < HEAD_DIM
    dq_total[...] = jnp.zeros_like(dq_total)

    keys_both[:rows] = prev_k_ref[...]
    keys_both[rows:] = own_k_ref[...]
    values_both[:rows] = prev_v_ref[...]
    values_both[rows:] = own_v_ref[...]

    def visit(line, start):
        lines, queries_at = pl.ds(line, block_k), pl.ds(start, block_q)
        keys = keys_both[lines, :]
        values_aug = jnp.concatenate([values_both[lines, :], ones], axis=1)
        probs, d_scores = [], []
        for h in range(2):
            part = weights_ref[h, lines, queries_at]
            centered = nt(values_aug, grad_aug[h, queries_at, :])
            d_scores.append((part.astype(F32) * centered).astype(BF16))
            probs.append(part)
        here_grads, here_queries = grad_ref[queries_at, :], q_ref[queries_at, :]
        dv_total[...] += jnp.where(keys_first, nn(probs[0], here_grads), nn(probs[1], here_grads))
        dk_total[...] += jnp.where(
            keys_first, nn(d_scores[0], here_queries), nn(d_scores[1], here_queries)
        )
        dq_total[queries_at, :] += jnp.where(
            queries_first, tn(d_scores[0], keys), tn(d_scores[1], keys)
        )

    @pl.when(has_prev == 0)
    def _():
        prev_grad_ref[0] = zero
        prev_grad_ref[1] = zero

    def clear():
        dk_total[...] = jnp.zeros_like(dk_total)
        dv_total[...] = jnp.zeros_like(dv_total)

    def put(line):
        @pl.when(line < rows)
        def _():
            prev_grad_ref[0, pl.ds(line, block_k), :] = dk_total[...].astype(BF16)
            prev_grad_ref[1, pl.ds(line, block_k), :] = dv_total[...].astype(BF16)

        @pl.when(line >= rows)
        def _():
            at = pl.multiple_of(line - rows, block_k)
            own_grad_ref[0, pl.ds(at, block_k), :] = dk_total[...].astype(BF16)
            own_grad_ref[1, pl.ds(at, block_k), :] = dv_total[...].astype(BF16)

    over_visible(has_prev, own_prefix, rows, block_q, block_k, clear, visit, put)
    dq_ref[...] = (dq_total[...] * (HEAD_DIM**-0.5)).astype(BF16)


def attention_backward(
    scalars, queries, prev, own, out, grads, weights, begin, count, block_q=BWD_Q, block_k=BWD_K
):
    rows, width = queries.shape
    pairs = width // LANES

    def spec(offset):
        return pl.BlockSpec((rows, LANES), lambda h, scalars: (0, h + begin + offset))

    both = pl.BlockSpec((2, rows, LANES), lambda h, scalars: (0, 0, h))
    share = count * LANES
    return pl.pallas_call(
        partial(backward_kernel, block_q, block_k),
        grid_spec=pltpu.PrefetchScalarGridSpec(
            num_scalar_prefetch=1,
            grid=(count,),
            in_specs=[spec(0), spec(0), spec(pairs), spec(0), spec(pairs), spec(0), spec(0)]
            + [pl.BlockSpec((None, 2, 2 * rows, rows), lambda h, scalars: (h + begin, 0, 0, 0))],
            out_specs=[pl.BlockSpec((rows, LANES), lambda h, scalars: (0, h)), both, both],
            scratch_shapes=[
                pltpu.VMEM((2, rows, 2 * LANES), BF16),
                pltpu.VMEM((2 * rows, LANES), BF16),
                pltpu.VMEM((2 * rows, LANES), BF16),
                pltpu.VMEM((rows, LANES), F32),
                pltpu.VMEM((block_k, LANES), F32),
                pltpu.VMEM((block_k, LANES), F32),
            ],
        ),
        out_shape=[
            jax.ShapeDtypeStruct((rows, share), BF16),
            jax.ShapeDtypeStruct((2, rows, share), BF16),
            jax.ShapeDtypeStruct((2, rows, share), BF16),
        ],
        compiler_params=pltpu.CompilerParams(vmem_limit_bytes=VMEM_LIMIT),
        cost_estimate=pl.CostEstimate(
            flops=60 * rows * rows * share,
            bytes_accessed=26 * rows * share,
            transcendentals=2 * rows * rows * share // HEAD_DIM,
        ),
        name="attention_backward",
    )(scalars, queries, prev, prev, own, own, out, grads, weights)


def expert_kernel(
    experts,
    block_r,
    scalars,
    rows_ref,
    cot_ref,
    w_in_ref,
    w_down_ref,
    router_ref,
    y_before_ref,
    y_ref,
    dm_ref,
    act_ref,
    du_ref,
    dy_ref,
    dz_ref,
    y_total,
    dm_total,
    probs,
):
    step = pl.program_id(0)
    slots, width = cot_ref.shape[1], cot_ref.shape[2]
    sources = block_r // slots
    lane = lane_index(block_r)
    is_mine = lane == scalars[0]

    def over_rows(work):
        for b in range(rows_ref.shape[0] // block_r):
            work(slice(b * block_r, (b + 1) * block_r), slice(b * sources, (b + 1) * sources))

    def cots(source):
        return cot_ref[source].reshape(block_r, width).astype(F32)

    @pl.when(step == 0)
    def _():
        def gate(here, source):
            logits = nt(rows_ref[here, :], router_ref[...])
            logits = jnp.where(lane < experts, logits, MASK_FILL)
            spread = jnp.exp(logits - jnp.max(logits, axis=1, keepdims=True))
            part = spread / jnp.sum(spread, axis=1, keepdims=True)
            probs[here, :] = part
            mine = jnp.sum(jnp.where(is_mine, part, 0.0), axis=1, keepdims=True)
            dy_ref[here, :] = (mine * cots(source)).astype(BF16)
            y_total[here, :] = jnp.zeros((block_r, y_total.shape[1]), F32)
            dm_total[here, :] = jnp.zeros((block_r, dm_total.shape[1]), F32)

        over_rows(gate)

    def hidden_block(here, source):
        u = nn(rows_ref[here, :], w_in_ref[...])
        d_act = nt(dy_ref[here, :], w_down_ref[...])
        square = u * u
        bend = jnp.tanh(u * (GELU_A + (GELU_A * GELU_B) * square))
        half = 0.5 + 0.5 * bend
        act = (u * half).astype(BF16)
        slope = half + (0.5 * u) * (1.0 - bend * bend) * (
            GELU_A + (3.0 * GELU_A * GELU_B) * square
        )
        du = (d_act * slope).astype(BF16)
        act_ref[here, :] = act
        du_ref[here, :] = du
        y_total[here, :] += nn(act, w_down_ref[...])
        dm_total[here, :] += nt(du, w_in_ref[...])

    over_rows(hidden_block)

    @pl.when(step == pl.num_programs(0) - 1)
    def _():
        def finish(here, source):
            y = y_total[here, :].astype(BF16)
            y_ref[source] = y.reshape(sources, slots, width)
            d_gate = jnp.sum(cots(source) * y.astype(F32), axis=1, keepdims=True)
            part = probs[here, :]
            mine = jnp.sum(jnp.where(is_mine, part, 0.0), axis=1, keepdims=True)
            dz = ((d_gate * mine) * (jnp.where(is_mine, 1.0, 0.0) - part)).astype(BF16)
            dz = jnp.where(lane < experts, dz, jnp.zeros_like(dz))
            dz_ref[here, :] = dz
            dm_ref[here, :] = (dm_total[here, :] + nn(dz, router_ref[...])).astype(BF16)

        over_rows(finish)


def run_expert(
    scalars, rows_in, cots, w_in, w_down, router, y_before, chunk, experts, block_h=512, block_r=1024
):
    rows, width = rows_in.shape
    half = w_in.shape[2]
    per_half = half // block_h
    whole = pl.BlockSpec((rows, width), lambda j, s: (0, 0))
    hidden = pl.BlockSpec((rows, block_h), lambda j, s: (0, j))
    mine = pl.BlockSpec(
        (cots.shape[0], None, cots.shape[2], width), lambda j, s: (0, chunk, 0, 0)
    )

    def which(j, s):
        return lax.rem(j // per_half + s[1], 2)

    first = y_before is None
    return pl.pallas_call(
        partial(expert_kernel, experts, block_r),
        grid_spec=pltpu.PrefetchScalarGridSpec(
            num_scalar_prefetch=1,
            grid=(2 * per_half,),
            in_specs=[
                whole,
                mine,
                pl.BlockSpec(
                    (None, width, block_h), lambda j, s: (which(j, s), 0, lax.rem(j, per_half))
                ),
                pl.BlockSpec(
                    (None, block_h, width), lambda j, s: (which(j, s), lax.rem(j, per_half), 0)
                ),
                pl.BlockSpec((LANES, width), lambda j, s: (0, 0)),
                pl.BlockSpec(memory_space=pl.ANY),
            ],
            out_specs=[
                mine,
                whole,
                hidden,
                hidden,
                whole,
                pl.BlockSpec((rows, LANES), lambda j, s: (0, 0)),
            ],
            scratch_shapes=[
                pltpu.VMEM((rows, width), F32),
                pltpu.VMEM((rows, width), F32),
                pltpu.VMEM((rows, LANES), F32),
            ],
        ),
        out_shape=[
            jax.ShapeDtypeStruct(cots.shape, BF16),
            jax.ShapeDtypeStruct((rows, width), BF16),
            jax.ShapeDtypeStruct((rows, 2 * half), BF16),
            jax.ShapeDtypeStruct((rows, 2 * half), BF16),
            jax.ShapeDtypeStruct((rows, width), BF16),
            jax.ShapeDtypeStruct((rows, LANES), BF16),
        ],
        input_output_aliases={} if first else {6: 0},
        compiler_params=pltpu.CompilerParams(vmem_limit_bytes=VMEM_LIMIT),
        cost_estimate=pl.CostEstimate(
            flops=16 * rows * width * half,
            bytes_accessed=8 * width * half + 12 * rows * width + 8 * rows * half,
            transcendentals=2 * rows * half,
        ),
        name="expert_rows",
    )(scalars, rows_in, cots, w_in, w_down, router, scalars if first else y_before)


def expert_weights_kernel(chunks, add, *refs):
    rows_refs, dy_refs, act_refs, du_refs = (
        refs[i * chunks : (i + 1) * chunks] for i in range(4)
    )
    rest = refs[4 * chunks :]
    d_in_ref, d_down_ref, turned = rest[-3:]
    rows = rows_refs[0].shape[0]

    @pl.when(pl.program_id(0) == 0)
    def _():
        for c in range(chunks):
            turned[:, c * rows : (c + 1) * rows] = rows_refs[c][...].T

    d_in, d_down = None, None
    for c in range(chunks):
        part = nn(turned[:, c * rows : (c + 1) * rows], du_refs[c][...])
        d_in = part if d_in is None else d_in + part
        part = tn(act_refs[c][...], dy_refs[c][...])
        d_down = part if d_down is None else d_down + part
    if add:
        d_in = d_in + rest[0][...].astype(F32)
        d_down = d_down + rest[1][...].astype(F32)
    d_in_ref[...] = d_in.astype(d_in_ref.dtype)
    d_down_ref[...] = d_down.astype(d_down_ref.dtype)


def expert_weights(rows_in, dy, act, du, half_index, got, block_h=512):
    chunks = len(rows_in)
    rows, width = rows_in[0].shape
    half = du[0].shape[1] // 2
    steps = half // block_h
    whole = pl.BlockSpec((rows, width), lambda j: (0, 0))
    hidden = pl.BlockSpec((rows, block_h), lambda j: (0, j + half_index * steps))
    columns = pl.BlockSpec((width, block_h), lambda j: (0, j))
    lines = pl.BlockSpec((block_h, width), lambda j: (j, 0))
    dtype = BF16 if got is None else F32
    extra = () if got is None else tuple(got)
    return pl.pallas_call(
        partial(expert_weights_kernel, chunks, got is not None),
        grid=(steps,),
        in_specs=[whole] * (2 * chunks) + [hidden] * (2 * chunks) + [columns, lines][: len(extra)],
        out_specs=[columns, lines],
        out_shape=[
            jax.ShapeDtypeStruct((width, half), dtype),
            jax.ShapeDtypeStruct((half, width), dtype),
        ],
        scratch_shapes=[pltpu.VMEM((width, chunks * rows), BF16)],
        compiler_params=pltpu.CompilerParams(vmem_limit_bytes=VMEM_LIMIT),
        cost_estimate=pl.CostEstimate(
            flops=4 * chunks * rows * width * half,
            bytes_accessed=4 * chunks * rows * (width + half) + 8 * width * half,
            transcendentals=0,
        ),
        name="expert_weights",
    )(*rows_in, *dy, *act, *du, *extra)


def both_sums(own_ref, back_ref, i):
    return (own_ref[i].astype(F32) + back_ref[i].astype(F32)).astype(BF16)


def pair_weights_kernel(with_context, scalars, *refs):
    in_ref, dq_ref, own_ref, back_ref, vectors_ref = refs[:5]
    outs = refs[-2:]
    is_first = scalars[0] == 0
    half = outs[0].shape[0]
    column = 0

    def put(top, bottom):
        nonlocal column
        here = slice(column, column + top.shape[1])
        column += top.shape[1]
        top, bottom = top.astype(BF16), bottom.astype(BF16)
        outs[0][:, here] = jnp.where(is_first, top, bottom)
        outs[1][:, here] = jnp.where(is_first, bottom, top)

    def products(left, rights):
        turned = left[...].T
        for right in rights:
            put(nn(turned[:half], right), nn(turned[half:], right))

    products(in_ref, [dq_ref[...]] + [both_sums(own_ref, back_ref, i) for i in range(2)])
    if with_context:
        products(refs[5], [refs[6][...]])
    turned = vectors_ref[...].T
    put(turned[:half], turned[half:])


def pair_weights(half_index, attn_in, grads, vectors, context_side=()):
    d_query, own_grad, back_grad = grads
    rows, width = attn_in.shape
    columns = 3 * d_query.shape[1] + vectors.shape[0]
    if context_side:
        columns += context_side[1].shape[1]

    def full(shape):
        return pl.BlockSpec(shape, lambda i, s: (0,) * len(shape))

    arrays = [attn_in, d_query, own_grad, back_grad, vectors] + list(context_side)
    out = full((width // 2, columns))
    return pl.pallas_call(
        partial(pair_weights_kernel, bool(context_side)),
        grid_spec=pltpu.PrefetchScalarGridSpec(
            num_scalar_prefetch=1,
            grid=(1,),
            in_specs=[full(x.shape) for x in arrays],
            out_specs=[out, out],
        ),
        out_shape=[jax.ShapeDtypeStruct((width // 2, columns), BF16)] * 2,
        compiler_params=pltpu.CompilerParams(vmem_limit_bytes=VMEM_LIMIT),
        cost_estimate=pl.CostEstimate(
            flops=2 * rows * width * columns,
            bytes_accessed=4 * (rows + width) * columns,
            transcendentals=0,
        ),
        name="pair_weights",
    )(half_index, *arrays)


def normalized(values):
    center = values - jnp.mean(values, axis=1, keepdims=True)
    inv_std = lax.rsqrt(jnp.mean(center * center, axis=1, keepdims=True) + NORM_EPSILON)
    return center * inv_std, inv_std


def rows_in_order(is_first, own_ref, other_ref):
    own, other = own_ref[...], other_ref[...]
    return jnp.concatenate(
        [jnp.where(is_first, own, other), jnp.where(is_first, other, own)], axis=0
    )


def key_value_kernel(scalars, tokens_ref, norm_ref, own_ref, other_ref, add_ref, out_ref, in_ref):
    @pl.when(pl.program_id(0) == 0)
    def _():
        normed, inv_std = normalized(tokens_ref[...].astype(F32))
        in_ref[...] = (normed * norm_ref[0:1, :] + norm_ref[1:2, :]).astype(BF16)

    weight = rows_in_order(scalars[0] == 0, own_ref, other_ref)
    out_ref[...] = (nn(in_ref[...], weight) + add_ref[...]).astype(BF16)


def query_kernel(scalars, in_ref, own_ref, other_ref, add_ref, out_ref):
    weight = rows_in_order(scalars[0] == 0, own_ref, other_ref)
    out_ref[...] = ((nn(in_ref[...], weight) + add_ref[...]) * (HEAD_DIM**-0.5)).astype(BF16)


def project(half_index, rows_in, w_own, w_other, bias, norm=None, block_n=512):
    rows, width = rows_in.shape
    columns = bias.shape[0]
    begin = 0 if norm is None else width // block_n
    half = pl.BlockSpec((width // 2, block_n), lambda j, s: (0, begin + j))
    whole = pl.BlockSpec((rows, width), lambda j, s: (0, 0))
    line = pl.BlockSpec((1, block_n), lambda j, s: (0, j))
    block = pl.BlockSpec((rows, block_n), lambda j, s: (0, j))
    shape = jax.ShapeDtypeStruct((rows, columns), BF16)
    if norm is None:
        in_specs, out_specs, out_shape = [whole, half, half, line], block, shape
        arrays = (rows_in, w_own, w_other, bias[None, :])
    else:
        in_specs = [whole, pl.BlockSpec((2, width), lambda j, s: (0, 0)), half, half, line]
        out_specs = [block, whole]
        out_shape = [shape, jax.ShapeDtypeStruct((rows, width), BF16)]
        arrays = (rows_in, norm, w_own, w_other, bias[None, :])
    return pl.pallas_call(
        query_kernel if norm is None else key_value_kernel,
        grid_spec=pltpu.PrefetchScalarGridSpec(
            num_scalar_prefetch=1,
            grid=(columns // block_n,),
            in_specs=in_specs,
            out_specs=out_specs,
        ),
        out_shape=out_shape,
        compiler_params=pltpu.CompilerParams(vmem_limit_bytes=VMEM_LIMIT),
        cost_estimate=pl.CostEstimate(
            flops=2 * rows * width * columns,
            bytes_accessed=2 * (rows * width + width * columns + rows * columns),
            transcendentals=0,
        ),
        name="project",
    )(half_index, *arrays)


def first_norm_kernel(
    shares, scalars, tokens_ref, dh_ref, gain_ref, w_own_ref, w_other_ref, *refs
):
    parts = len(shares)
    out_ref, sums_ref = refs[3 * parts], refs[3 * parts + 1]
    width = tokens_ref.shape[1]
    d_own, d_other = None, None
    query_sums, value_sums = [], []
    begin = 0
    for p, share in enumerate(shares):
        dq, own_grad, back_grad = refs[3 * p : 3 * p + 3]
        for i in range(3):
            grads = dq[...] if i == 0 else both_sums(own_grad, back_grad, i - 1)
            at = i * width + begin
            part = nt(grads, w_own_ref[:, at : at + share])
            d_own = part if d_own is None else d_own + part
            part = nt(grads, w_other_ref[:, at : at + share])
            d_other = part if d_other is None else d_other + part
            if i != 1:
                sums = jnp.sum(grads.astype(F32), axis=0, keepdims=True)
                (query_sums if i == 0 else value_sums).append(sums)
        begin += share
    is_first = scalars[0] == 0
    d_norm = jnp.concatenate(
        [jnp.where(is_first, d_own, d_other), jnp.where(is_first, d_other, d_own)], axis=1
    )
    normed, inv_std = normalized(tokens_ref[...].astype(F32))
    scaled = d_norm * gain_ref[...]
    back = inv_std * (
        scaled
        - jnp.mean(scaled, axis=1, keepdims=True)
        - normed * jnp.mean(scaled * normed, axis=1, keepdims=True)
    )
    out_ref[...] = (dh_ref[...] + back).astype(BF16)
    sums = jnp.concatenate(
        [
            jnp.sum(d_norm * normed, axis=0, keepdims=True),
            jnp.sum(d_norm, axis=0, keepdims=True),
            jnp.concatenate(query_sums, axis=1),
            jnp.concatenate(value_sums, axis=1),
        ],
        axis=0,
    )

    @pl.when(pl.program_id(0) == 0)
    def _():
        sums_ref[...] = jnp.zeros_like(sums_ref)

    sums_ref[0:4, :] += sums


def first_norm(half_index, tokens, d_hidden, gain, w_own, w_other, grads, block_r=256):
    rows, width = tokens.shape
    shares = tuple(g[0].shape[1] for g in grads)
    lines = pl.BlockSpec((block_r, width), lambda i, s: (i, 0))
    weight = pl.BlockSpec((width // 2, 3 * width), lambda i, s: (0, 0))
    specs, arrays = [], []
    for three, share in zip(grads, shares):
        both = pl.BlockSpec((2, block_r, share), lambda i, s: (0, i, 0))
        specs += [pl.BlockSpec((block_r, share), lambda i, s: (i, 0)), both, both]
        arrays += list(three)
    return pl.pallas_call(
        partial(first_norm_kernel, shares),
        grid_spec=pltpu.PrefetchScalarGridSpec(
            num_scalar_prefetch=1,
            grid=(rows // block_r,),
            in_specs=[lines, lines, pl.BlockSpec((1, width), lambda i, s: (0, 0)), weight, weight]
            + specs,
            out_specs=[lines, pl.BlockSpec((LANES, width), lambda i, s: (0, 0))],
        ),
        out_shape=[
            jax.ShapeDtypeStruct((rows, width), BF16),
            jax.ShapeDtypeStruct((LANES, width), F32),
        ],
        compiler_params=pltpu.CompilerParams(vmem_limit_bytes=VMEM_LIMIT),
        cost_estimate=pl.CostEstimate(
            flops=6 * rows * width * width,
            bytes_accessed=14 * rows * width + 6 * width * width,
            transcendentals=rows,
        ),
        name="first_norm",
    )(half_index, tokens, d_hidden, gain[None, :], w_own, w_other, *arrays)


def layer_norm(values, norm_gain, norm_bias):
    center = values - jnp.mean(values, axis=-1, keepdims=True)
    inv_std = lax.rsqrt(jnp.mean(center * center, axis=-1, keepdims=True) + NORM_EPSILON)
    normed = center * inv_std
    return (normed * norm_gain + norm_bias, normed, inv_std)


def norm_backward(grad_out, normed, inv_std, norm_gain):
    scaled = grad_out * norm_gain
    return inv_std * (
        scaled
        - jnp.mean(scaled, axis=-1, keepdims=True)
        - normed * jnp.mean(scaled * normed, axis=-1, keepdims=True)
    )


def swapped(array):
    return lax.ppermute(array, "fsdp", [(0, 1), (1, 0)])


def exchanged(array):
    return lax.all_to_all(array, "expert", split_axis=0, concat_axis=0, tiled=True)


def body(
    tokens,
    out_grad,
    routes,
    prefix,
    ln1_gain,
    ln1_bias,
    w_qkv,
    q_bias,
    v_bias,
    attention_output_weight,
    attention_output_bias,
    ln2_gain,
    ln2_bias,
    w_router,
    moe_bias,
    w_in,
    w_down,
):
    experts = lax.axis_size("expert")
    my_expert = lax.axis_index("expert")
    my_half = lax.axis_index("fsdp")
    is_first = my_half == 0
    rows, width = tokens.shape[1], tokens.shape[2]
    half_width = width // 2
    slots = max(2, 2 * rows // experts) // CHUNKS
    chunk_rows = experts * slots

    def in_order(own, other, axis):
        return jnp.where(
            is_first,
            jnp.concatenate([own, other], axis=axis),
            jnp.concatenate([other, own], axis=axis),
        )

    small = jnp.concatenate(
        [
            jnp.stack(
                [
                    ln1_gain,
                    ln1_bias,
                    q_bias,
                    v_bias,
                    attention_output_bias,
                    ln2_gain,
                    ln2_bias,
                    moe_bias,
                ]
            ),
            w_router.T,
        ],
        axis=0,
    )
    small = in_order(small, swapped(small), 1)
    vectors = small[:8].astype(F32)
    norm1_gain, norm1_bias, query_bias, value_bias = (vectors[i] for i in range(4))
    output_bias, norm2_gain, norm2_bias, expert_bias = (vectors[i] for i in range(4, 8))
    router_t = small[8:]
    w_qkv_other = swapped(w_qkv)
    own_index = my_half[None].astype(jnp.int32)
    out_weight = lax.all_gather(attention_output_weight, "fsdp", axis=0, tiled=True)
    w_in_both = lax.all_gather(w_in[0], "fsdp", axis=0, tiled=False)
    w_down_both = lax.all_gather(w_down[0], "fsdp", axis=0, tiled=False)

    token_route = routes[0, :, 0]
    one_hot = token_route[:, None] == jnp.arange(experts, dtype=jnp.int32)[None, :]
    row_ids = jnp.arange(rows, dtype=jnp.int32)
    earlier_same = nn(
        (row_ids[None, :] < row_ids[:, None]).astype(BF16), one_hot.astype(BF16)
    )
    slot_index = jnp.sum(jnp.where(one_hot, earlier_same, 0.0), axis=-1).astype(jnp.int32)
    chunk_of = slot_index // slots
    place_in = token_route * slots + slot_index % slots
    buffer_ids = jnp.arange(chunk_rows, dtype=jnp.int32)

    def place_of(chunk):
        return jnp.where(chunk_of == chunk, place_in, -1)

    def picked(row_values, chunk):
        return nn(
            (buffer_ids[:, None] == place_of(chunk)[None, :]).astype(BF16), row_values
        ).astype(BF16)

    def sent(buffer):
        return exchanged(buffer.reshape(experts, slots, width)).reshape(chunk_rows, width)

    def picked_up(got):
        total = None
        for chunk in range(CHUNKS):
            part = nn((place_of(chunk)[:, None] == buffer_ids[None, :]).astype(BF16), got[chunk])
            total = part if total is None else total + part
        return total

    full_place = token_route * (CHUNKS * slots) + slot_index
    full_ids = jnp.arange(CHUNKS * chunk_rows, dtype=jnp.int32)
    cot_rows = nn((full_ids[:, None] == full_place[None, :]).astype(BF16), out_grad[0])
    cot_rows, tokens_in = lax.optimization_barrier((cot_rows.astype(BF16), tokens[0]))
    cot_rows = exchanged(cot_rows.reshape(experts, CHUNKS * slots, width)).reshape(
        experts, CHUNKS, slots, width
    )

    key_value, attn_in = project(
        own_index,
        tokens_in,
        w_qkv,
        w_qkv_other,
        jnp.concatenate([jnp.zeros_like(value_bias), value_bias]),
        vectors[0:2],
    )
    prev_key_value = lax.ppermute(key_value, "fsdp", [(0, 1)])
    queries = project(own_index, attn_in, w_qkv, w_qkv_other, query_bias)
    residual = tokens[0].astype(F32)
    scalars = jnp.stack([my_half, prefix[0] - my_half * rows]).astype(jnp.int32)
    context, lse = attention_forward(scalars, queries, prev_key_value, key_value)
    hidden = residual + (nn(context, out_weight) + output_bias)
    norm2_out, normed2, inv_std2 = layer_norm(hidden, norm2_gain, norm2_bias)
    mixed = norm2_out.astype(BF16)

    leaving = [picked(mixed, chunk) for chunk in range(CHUNKS)]
    weights = attention_weights(scalars, queries, prev_key_value, key_value, lse)
    leaving[-1], weights = lax.optimization_barrier((leaving[-1], weights))
    mixed_rows = [sent(rows_out) for rows_out in leaving]
    router_pad = jnp.pad(router_t, ((0, LANES - experts), (0, 0)))
    expert_scalars = jnp.stack([my_expert, my_half]).astype(jnp.int32)
    done, y_rows = [], None
    for c in range(CHUNKS):
        y_rows, *rest = run_expert(
            expert_scalars,
            mixed_rows[c],
            cot_rows,
            w_in_both,
            w_down_both,
            router_pad,
            y_rows,
            c,
            experts,
        )
        done.append(rest)
    d_mixed_chunks, act, du, dy, dz = ([d[i] for d in done] for i in range(5))
    back = [sent(d) for d in d_mixed_chunks]
    others = expert_weights(mixed_rows, dy, act, du, 1, None)
    back[-1], others = lax.optimization_barrier((back[-1], others))
    d_mixed = picked_up(back)
    got = [swapped(o) for o in others]
    d_router_t = None
    for c in range(CHUNKS):
        part = tn(dz[c], mixed_rows[c])
        d_router_t = part if d_router_t is None else d_router_t + part

    out_cot = out_grad[0].astype(F32)
    d_expert_bias = jnp.sum(out_cot, axis=0)
    d_norm2_gain = jnp.sum(d_mixed * normed2, axis=0)
    d_norm2_bias = jnp.sum(d_mixed, axis=0)
    d_hidden = out_cot + norm_backward(d_mixed, normed2, inv_std2, norm2_gain)
    d_attn = d_hidden.astype(BF16)
    d_output_bias = jnp.sum(d_attn.astype(F32), axis=0)
    d_context = nt(d_attn, out_weight).astype(BF16)

    logits = nt(mixed, router_t)
    router_probs = jax.nn.softmax(logits, axis=-1)
    gate_value = jnp.sum(jnp.where(one_hot, router_probs, 0.0), axis=-1)
    y_back = exchanged(y_rows.reshape(experts, CHUNKS * slots, width)).reshape(-1, width)
    early, line = d_router_t, jnp.arange(LANES, dtype=jnp.int32)[:, None]
    for i, vector in enumerate([d_expert_bias, d_norm2_gain, d_norm2_bias, d_output_bias]):
        early = early + jnp.where(line == experts + i, vector[None, :], 0.0)

    pairs = width // LANES
    groups = ((0, FIRST_PAIRS), (FIRST_PAIRS, pairs - FIRST_PAIRS))
    grads, sums = [], []
    for number, (begin, count) in enumerate(groups):
        d_query, prev_grad, own_grad = attention_backward(
            scalars,
            queries,
            prev_key_value,
            key_value,
            context,
            d_context,
            weights,
            begin,
            count,
        )
        returned = lax.ppermute(prev_grad, "fsdp", [(1, 0)])
        group = (d_query, own_grad, returned)
        grads.append(group)
        if number == 0:
            vectors_in, context_side = early, (context, d_attn)
        else:
            d_tokens, norm_sums = first_norm(
                own_index, tokens[0], d_hidden, norm1_gain, w_qkv, w_qkv_other, grads
            )
            norm_sums, sums[0] = lax.optimization_barrier((norm_sums, sums[0]))
            vectors_in, context_side = norm_sums, ()
        own_part, other_part = pair_weights(own_index, attn_in, group, vectors_in, context_side)
        own_part = (own_part.astype(F32) + swapped(other_part).astype(F32)).astype(BF16)
        blocks = own_part.reshape(experts, half_width // experts, own_part.shape[1])
        if number < len(groups) - 1:
            d_context, blocks, y_back = lax.optimization_barrier((d_context, blocks, y_back))
        sums.append(jnp.sum(exchanged(blocks).astype(F32), axis=0))
    d_w_in, d_w_down = expert_weights(mixed_rows, dy, act, du, 0, got)
    expert_value = nn((full_place[:, None] == full_ids[None, :]).astype(BF16), y_back)
    output = hidden + gate_value[:, None] * expert_value + expert_bias

    sum_qkv = jnp.concatenate(
        [
            sums[g][:, i * count * LANES : (i + 1) * count * LANES]
            for i in range(3)
            for g, (begin, count) in enumerate(groups)
        ],
        axis=1,
    )
    sum_out = sums[0][:, 3 * groups[0][1] * LANES :]
    sum_last = sums[-1][:, 3 * groups[-1][1] * LANES :]
    return (
        output.astype(BF16)[None],
        d_tokens[None],
        sum_last[:, 0],
        sum_last[:, 1],
        sum_qkv,
        sum_last[:, 2],
        sum_last[:, 3],
        sum_out[:, :width],
        sum_out[:, width + experts + 3],
        sum_out[:, width + experts + 1],
        sum_out[:, width + experts + 2],
        sum_out[:, width : width + experts],
        sum_out[:, width + experts],
        d_w_in[None],
        d_w_down[None],
    )


def solution(mesh):
    vector = P(("fsdp", "expert"))
    matrix = P(("fsdp", "expert"), None)
    tokens = P("expert", "fsdp", None)
    return jax.shard_map(
        body,
        mesh=mesh,
        in_specs=(
            tokens,
            tokens,
            tokens,
            P("expert"),
            P("fsdp"),
            P("fsdp"),
            P("fsdp", None),
            P("fsdp"),
            P("fsdp"),
            P("fsdp", None),
            P("fsdp"),
            P("fsdp"),
            P("fsdp"),
            P("fsdp", None),
            P("fsdp"),
            P("expert", None, "fsdp"),
            P("expert", "fsdp", None),
        ),
        out_specs=(
            tokens,
            tokens,
            vector,
            vector,
            matrix,
            vector,
            vector,
            matrix,
            vector,
            vector,
            vector,
            matrix,
            vector,
            P("expert", None, "fsdp"),
            P("expert", "fsdp", None),
        ),
        check_vma=False,
    )
```

time: 634 us -> 582 us (0.918)
  waiting for transfers between devices: 94.3 us -> 65 us
  other arithmetic: 25.7 us -> 13.7 us
  matrix products: 58.9 us -> 48.4 us
    all_to_all x8, waiting for transfers between devices: 55.9 us -> 30.1 us  [exchanged(): lax.all_to_all(array, 'expert', split_axis=0, concat_axis=0, tiled=True)]
    pallas_call x6 -> x7, Pallas kernels: 92.4 us -> 115 us  [the longest x1 35.4 us: attention_forward(): pl.pallas_call(partial(forward_kernel, block), grid_spec=pltpu.PrefetchSc...]
    pallas_call x2, Pallas kernels: 71.6 us -> 49 us  [attention_backward(): pl.pallas_call(partial(backward_kernel, block_q, block_k), grid_spec=pltp...]
    dot_general x10 -> x8, matrix products: 51.8 us -> 40.7 us  [nn(): lax.dot_general(left, right, (((1,), (0,)), ((), ())), preferred_element_...]
    ppermute x2, waiting for transfers between devices: 32.2 us -> 23.2 us  [body(): returned = lax.ppermute(prev_grad, 'fsdp', [(1, 0)])]
    ppermute x8 -> x6, starting transfers between devices: 17.6 us -> 21.1 us  [swapped(): return lax.ppermute(array, 'fsdp', [(0, 1), (1, 0)])]
  transfers between devices with their start and end apart: 22 -> 20, of which waited for: 7 -> 8; matrix products, arithmetic and copies ran while one was open for 15% -> 12% of each run, Pallas kernels for 47% -> 54%
where the time goes in v3:
time: 582 us; the launch traced here: 575 us
  Pallas kernels  312 us (54%)
  starting transfers between devices  110 us (19%)
  waiting for transfers between devices  65 us (11%)
  matrix products  48.4 us (8%)
  between operations  15.7 us (3%)
  other arithmetic  13.7 us (2%)
  local copies, waits for them, and re-layouts  9.97 us (2%)
    pallas_call x2, Pallas kernels, run_expert(): pl.pallas_call(partial(expert_kernel, experts, block_r), grid_spec=pltpu....  95.6 us
    all_to_all x8, starting transfers between devices, exchanged(): lax.all_to_all(array, 'expert', split_axis=0, concat_axis=0, tiled=True)  81.5 us
    pallas_call x2, Pallas kernels, expert_weights(): pl.pallas_call(partial(expert_weights_kernel, chunks, got is not None), g...  52.1 us
    pallas_call x2, Pallas kernels, attention_backward(): pl.pallas_call(partial(backward_kernel, block_q, block_k), grid_spec=pltp...  49 us
    dot_general x8, matrix products, nn(): lax.dot_general(left, right, (((1,), (0,)), ((), ())), preferred_element_...  40.7 us
    pallas_call x1, Pallas kernels, attention_forward(): pl.pallas_call(partial(forward_kernel, block), grid_spec=pltpu.PrefetchSc...  35.4 us
    all_to_all x8, waiting for transfers between devices, exchanged(): lax.all_to_all(array, 'expert', split_axis=0, concat_axis=0, tiled=True)  30.1 us
    pallas_call x1, Pallas kernels, attention_weights(): pl.pallas_call(partial(weights_kernel, block_q, block_k), grid_spec=pltpu...  27.9 us
  transfers between devices with their start and end apart: 20, of which 8 were waited for; matrix products, arithmetic and copies ran while one was open for 12% of the time, Pallas kernels for 54%

profile of v3, /device:TPU:0, one launch (start us, length us, event | category | flops | bytes accessed | tf_op | source)
XLA Modules:
  0.0 574.6 jit_solution(18144278772938247340)
XLA Ops:
  10.4 7.6 %fusion.9 = bf16[2048,1024]{1,0:T(8,128)(2,1)} fusion(s32[1024]{0:T(1024)S(1)} %get-tuple-element.173, bf16[1,1024,1024]{2,1,0:T(8,128)(2,1)} %param.18), kind=kOutput, calls=%fused_computation.28 | convolution fusion | flops 4299161600 | bytes 6295552 | tf_op jit(solution)/shard_map/dot_general | solution.py:28
  18.0 8.4 %all-to-all-start.1 = ((bf16[16,128,1024]{2,1,0:T(8,128)(2,1)}), bf16[16,128,1024]{2,1,0:T(8,128)(2,1)}, u32[]{:S(2)}, u32[]{:S(2)}) async-start(bf16[16,128,1024]{2,1,0:T(8,128)(2,1)} %bitcast.58), calls=%async_computation.1 | async-start | bytes 8388608 | tf_op jit(solution)/shard_map/all_to_all | solution.py:876
  28.3 10.3 %project.2 = (bf16[1024,2048]{1,0:T(8,128)(2,1)}, bf16[1024,1024]{1,0:T(8,128)(2,1)}) custom-call(s32[1]{0:T(128)} %bitcast.1.scalars, bf16[1024,1024]{1,0:T(8,128)(2,1)} %bitcast.77, f32[2,1024]{1,0:T(2,128)} %slice.117.norm_ref, bf16[512,3072]{1,0:T(8,128)(2,1)} %w_own_ref.1, bf16[512,3072]{1,0:T(8,128)(2,1)} %collective-permute-done.1.other_ref.w_other_ref, ...), custom_call_target="tpu_custom_call" | custom-call | flops 4294967296 | bytes 10485760 | tf_op jit(solution)/shard_map/project/pallas_call | solution.py:752
  43.7 5.8 %project.3.q_ref = bf16[1024,1024]{1,0:T(8,128)(2,1)} custom-call(s32[1]{0:T(128)} %bitcast.1.scalars, bf16[1024,1024]{1,0:T(8,128)(2,1)} %get-tuple-element.60.in_ref.refs_0_, bf16[512,3072]{1,0:T(8,128)(2,1)} %w_own_ref.1, bf16[512,3072]{1,0:T(8,128)(2,1)} %collective-permute-done.1.other_ref.w_other_ref, f32[1,1024]{1,0:T(1,128)} %get-tuple-element.169.add_ref), custom_call_target="tpu_custom_call" | custom-call | flops 2147483648 | bytes 6291456 | tf_op jit(solution)/shard_map/project/pallas_call | solution.py:752
  51.6 35.4 %attention_forward.1 = (bf16[1024,1024]{1,0:T(8,128)(2,1)}, f32[1024,1024]{1,0:T(8,128)}) custom-call(s32[2]{0:T(128)} %pad_add_fusion.scalars, bf16[1024,1024]{1,0:T(8,128)(2,1)} %project.3.q_ref, bf16[1024,2048]{1,0:T(8,128)(2,1)} %collective-permute-done.2.prev_k_ref.prev_v_ref, bf16[1024,2048]{1,0:T(8,128)(2,1)} %collective-permute-done.2.prev_k_ref.prev_v_ref, ...), custom_call_target="tpu_custom_call" | custom-call | flops 4294967296 | bytes 16777216 | tf_op jit(solution)/shard_map/attention_forward/pallas_call | solution.py:193
  87.0 4.7 fusion.33
  97.3 9.1 %all-to-all-done.1 = bf16[16,128,1024]{2,1,0:T(8,128)(2,1)} async-done(((bf16[16,128,1024]{2,1,0:T(8,128)(2,1)}), bf16[16,128,1024]{2,1,0:T(8,128)(2,1)}, u32[]{:S(2)}, u32[]{:S(2)}) %all-to-all-start.1) | async-done | bytes 4194336 | tf_op jit(solution)/shard_map/all_to_all | solution.py:876
  106.5 20.5 %all-to-all-start = ((bf16[16,64,1024]{2,1,0:T(8,128)(2,1)}), bf16[16,64,1024]{2,1,0:T(8,128)(2,1)}, u32[]{:S(2)}, u32[]{:S(2)}) async-start(bf16[16,64,1024]{2,1,0:T(8,128)(2,1)} %bitcast.64), calls=%async_computation | async-start | bytes 4194304 | tf_op jit(solution)/shard_map/all_to_all | solution.py:876
  130.7 27.9 %attention_weights.1.weights_ref = bf16[8,2,2048,1024]{3,2,1,0:T(8,128)(2,1)} custom-call(s32[2]{0:T(128)} %pad_add_fusion.scalars, bf16[1024,1024]{1,0:T(8,128)(2,1)} %project.3.q_ref, bf16[1024,2048]{1,0:T(8,128)(2,1)} %collective-permute-done.2.prev_k_ref.prev_v_ref, bf16[1024,2048]{1,0:T(8,128)(2,1)} %get-tuple-element.61.own_k_ref.own_v_ref, ...), custom_call_target="tpu_custom_call" | custom-call | flops 8589934592 | bytes 77594624 | tf_op jit(solution)/shard_map/attention_weights/pallas_call | solution.py:284
  158.6 10.9 %all-to-all-done = bf16[16,64,1024]{2,1,0:T(8,128)(2,1)} async-done(((bf16[16,64,1024]{2,1,0:T(8,128)(2,1)}), bf16[16,64,1024]{2,1,0:T(8,128)(2,1)}, u32[]{:S(2)}, u32[]{:S(2)}) %all-to-all-start) | async-done | bytes 2097184 | tf_op jit(solution)/shard_map/all_to_all | solution.py:876
  169.5 9.7 %all-to-all-start.3 = ((bf16[16,64,1024]{2,1,0:T(8,128)(2,1)}), bf16[16,64,1024]{2,1,0:T(8,128)(2,1)S(1)}, u32[]{:S(2)}, u32[]{:S(2)}) async-start(bf16[16,64,1024]{2,1,0:T(8,128)(2,1)} %bitcast.60), calls=%async_computation.3 | async-start | bytes 4194304 | tf_op jit(solution)/shard_map/all_to_all | solution.py:876
  180.6 47.8 %expert_rows.2 = (bf16[16,2,64,1024]{3,2,1,0:T(8,128)(2,1)}, bf16[1024,1024]{1,0:T(8,128)(2,1)}, bf16[1024,4096]{1,0:T(8,128)(2,1)}, bf16[1024,4096]{1,0:T(8,128...) custom-call(s32[2]{0:T(128)} %pad_add_fusion.1.scalars.y_before_ref, ...), custom_call_target="tpu_custom_call" | custom-call | flops 34359738368 | bytes 46137344 | tf_op jit(solution)/shard_map/expert_rows/pallas_call | solution.py:538
  228.4 7.4 %all-to-all-start.2 = ((bf16[16,64,1024]{2,1,0:T(8,128)(2,1)}), bf16[16,64,1024]{2,1,0:T(8,128)(2,1)}, u32[]{:S(2)}, u32[]{:S(2)}) async-start(bf16[16,64,1024]{2,1,0:T(8,128)(2,1)} %bitcast.61), calls=%async_computation.2 | async-start | bytes 4194304 | tf_op jit(solution)/shard_map/all_to_all | solution.py:876
  235.9 47.8 %expert_rows.3 = (bf16[16,2,64,1024]{3,2,1,0:T(8,128)(2,1)}, bf16[1024,1024]{1,0:T(8,128)(2,1)}, bf16[1024,4096]{1,0:T(8,128)(2,1)}, bf16[1024,4096]{1,0:T(8,128...) custom-call(s32[2]{0:T(128)} %pad_add_fusion.1.scalars.y_before_ref, ...), custom_call_target="tpu_custom_call", output_to_operand_aliasing={{0}: (6, {})} | custom-call | flops 34359738368 | bytes 46137344 | tf_op jit(solution)/shard_map/expert_rows/pallas_call | solution.py:538
  283.7 7.2 %all-to-all-start.4 = ((bf16[16,64,1024]{2,1,0:T(8,128)(2,1)}), bf16[16,64,1024]{2,1,0:T(8,128)(2,1)S(1)}, u32[]{:S(2)}, u32[]{:S(2)}) async-start(bf16[16,64,1024]{2,1,0:T(8,128)(2,1)} %bitcast.62), calls=%async_computation.4 | async-start | bytes 4194304 | tf_op jit(solution)/shard_map/all_to_all | solution.py:876
  290.9 25.4 %expert_weights.2 = (bf16[1024,2048]{1,0:T(8,128)(2,1)}, bf16[2048,1024]{1,0:T(8,128)(2,1)}) custom-call(bf16[1024,1024]{1,0:T(8,128)(2,1)} %bitcast.14.rows_ref.refs_0_, bf16[1024,1024]{1,0:T(8,128)(2,1)} %bitcast.55, bf16[1024,1024]{1,0:T(8,128)(2,1)} %get-tuple-element.69.refs_2_, bf16[1024,1024]{1,0:T(8,128)(2,1)} %get-tuple-element.70.refs_3_, ...), custom_call_target="tpu_custom_call" | custom-call | flops 17179869184 | bytes 41943040 | tf_op jit(solution)/shard_map/expert_weights/pallas_call | solution.py:625
  316.3 5.9 %fusion.4 = f32[1024,1024]{1,0:T(8,128)} fusion(bf16[1024,1024]{1,0:T(8,128)(2,1)} %bitcast.18, s32[1024]{0:T(1024)S(1)} %get-tuple-element.172), kind=kOutput, calls=%fused_computation.22 | convolution fusion | flops 2148532224 | bytes 6295552 | tf_op jit(solution)/shard_map/dot_general | solution.py:28
  322.2 10.0 %all-to-all-done.4 = bf16[16,64,1024]{2,1,0:T(8,128)(2,1)S(1)} async-done(((bf16[16,64,1024]{2,1,0:T(8,128)(2,1)}), bf16[16,64,1024]{2,1,0:T(8,128)(2,1)S(1)}, u32[]{:S(2)}, u32[]{:S(2)}) %all-to-all-start.4) | async-done | bytes 2097184 | tf_op jit(solution)/shard_map/all_to_all | solution.py:876
  332.2 10.2 %all-to-all-start.5 = ((bf16[16,128,1024]{2,1,0:T(8,128)(2,1)}), bf16[16,128,1024]{2,1,0:T(8,128)(2,1)}, u32[]{:S(2)}, u32[]{:S(2)}) async-start(bf16[16,128,1024]{2,1,0:T(8,128)(2,1)} %bitcast.59), calls=%async_computation.5 | async-start | bytes 8388608 | tf_op jit(solution)/shard_map/all_to_all | solution.py:876
  342.4 6.4 %multiply_reduce_fusion = (f32[1024]{0:T(1024)S(1)}, f32[1024]{0:T(1024)S(1)}, f32[1024]{0:T(1024)S(1)}, f32[1024]{0:T(1024)S(1)}, f32[1024,1024]{1,0:T(8,128)S(1)}) fusion(f32[1024,1024]{1,0:T(8,128)} %copy-done, f32[1024]{0:T(1024)S(1)} %add_rsqrt_fusion, f32[1024]{0:T(1024)S(1)} %broadcast_multiply_fusion.2, f32[1024]{0:T(1024)S(1)} %bitcast.66, ...), kind=kOutput, calls=%fused_computation.10 | convolution fusion | flops 2159013888 | bytes 14712832 | tf_op jit(solution)/shard_map/dot_general | solution.py:28
  355.9 24.6 %attention_backward.2 = (bf16[1024,512]{1,0:T(8,128)(2,1)}, bf16[2,1024,512]{2,1,0:T(8,128)(2,1)}, bf16[2,1024,512]{2,1,0:T(8,128)(2,1)}) custom-call(s32[2]{0:T(128)} %pad_add_fusion.scalars, bf16[1024,1024]{1,0:T(8,128)(2,1)} %project.3.q_ref, bf16[1024,2048]{1,0:T(8,128)(2,1)} %collective-permute-done.2.prev_k_ref.prev_v_ref, ...), custom_call_target="tpu_custom_call" | custom-call | flops 32212254720 | bytes 13631488 | tf_op jit(solution)/shard_map/attention_backward/pallas_call | solution.py:408
  385.6 20.0 %collective-permute-done.3.refs_3_.refs_2_ = bf16[2,1024,512]{2,1,0:T(8,128)(2,1)S(1)} collective-permute-done((bf16[2,1024,512]{2,1,0:T(8,128)(2,1)}, bf16[2,1024,512]{2,1,0:T(8,128)(2,1)S(1)}, u32[]{:S(2)}, u32[]{:S(2)}) %collective-permute-start.3) | collective-permute-done | bytes 2097184 | tf_op jit(solution)/shard_map/ppermute | solution.py:1060
  406.9 12.5 %pair_weights.2 = (bf16[512,2688]{1,0:T(8,128)(2,1)}, bf16[512,2688]{1,0:T(8,128)(2,1)}) custom-call(s32[1]{0:T(128)} %bitcast.1.scalars, bf16[1024,1024]{1,0:T(8,128)(2,1)} %get-tuple-element.60.in_ref.refs_0_, bf16[1024,512]{1,0:T(8,128)(2,1)} %get-tuple-element.79.refs_1_.refs_0_, bf16[2,1024,512]{2,1,0:T(8,128)(2,1)} %get-tuple-element.80.refs_2_.refs_1_, ...), custom_call_target="tpu_custom_call" | custom-call | flops 5637144576 | bytes 22020096 | tf_op jit(solution)/shard_map/pair_weights/pallas_call | solution.py:688
  419.6 5.2 collective-permute-done.4
  428.7 11.1 %all-to-all-start.6 = ((bf16[16,32,2688]{2,1,0:T(8,128)(2,1)}), bf16[16,32,2688]{2,1,0:T(8,128)(2,1)S(1)}, u32[]{:S(2)}, u32[]{:S(2)}) async-start(bf16[16,32,2688]{2,1,0:T(8,128)(2,1)} %bitcast.23), calls=%async_computation.6 | async-start | bytes 5505024 | tf_op jit(solution)/shard_map/all_to_all | solution.py:876
  439.8 24.4 %attention_backward.3 = (bf16[1024,512]{1,0:T(8,128)(2,1)}, bf16[2,1024,512]{2,1,0:T(8,128)(2,1)}, bf16[2,1024,512]{2,1,0:T(8,128)(2,1)}) custom-call(s32[2]{0:T(128)} %pad_add_fusion.scalars, bf16[1024,1024]{1,0:T(8,128)(2,1)} %project.3.q_ref, bf16[1024,2048]{1,0:T(8,128)(2,1)} %collective-permute-done.2.prev_k_ref.prev_v_ref, ...), custom_call_target="tpu_custom_call" | custom-call | flops 32212254720 | bytes 13631488 | tf_op jit(solution)/shard_map/attention_backward/pallas_call | solution.py:408
  465.8 20.2 %collective-permute-start.7 = (bf16[1024,2048]{1,0:T(8,128)(2,1)}, bf16[1024,2048]{1,0:T(8,128)(2,1)}, u32[]{:S(2)}, u32[]{:S(2)}) collective-permute-start(bf16[1024,2048]{1,0:T(8,128)(2,1)} %get-tuple-element.99), channel_id=1, source_target_pairs={{0,16},{16,0},{1,17},{17,1},{2,18},{18,2},{3,19},{19,3},{4,20},{20... | collective-permute-start | bytes 12582920 | tf_op jit(solution)/shard_map/ppermute | solution.py:872
  490.7 14.9 %first_norm.1 = (bf16[1024,1024]{1,0:T(8,128)(2,1)}, f32[128,1024]{1,0:T(8,128)}) custom-call(s32[1]{0:T(128)} %bitcast.1.scalars, bf16[1024,1024]{1,0:T(8,128)(2,1)} %bitcast.78, f32[1024,1024]{1,0:T(8,128)} %get-tuple-element.162.dh_ref, f32[1,1024]{1,0:T(1,128)} %get-tuple-element.164.gain_ref, bf16[512,3072]{1,0:T(8,128)(2,1)} %w_own_ref.1, ...), custom_call_target="tpu_custom_call" | custom-call | flops 6442450944 | bytes 20971520 | tf_op jit(solution)/shard_map/first_norm/pallas_call | solution.py:832
  506.0 8.6 %pair_weights.3 = (bf16[512,1664]{1,0:T(8,128)(2,1)}, bf16[512,1664]{1,0:T(8,128)(2,1)}) custom-call(s32[1]{0:T(128)} %bitcast.1.scalars, bf16[1024,1024]{1,0:T(8,128)(2,1)} %get-tuple-element.60.in_ref.refs_0_, bf16[1024,512]{1,0:T(8,128)(2,1)} %get-tuple-element.89.refs_3_.refs_1_, bf16[2,1024,512]{2,1,0:T(8,128)(2,1)} %get-tuple-element.90.refs_4_.refs_2_, ...), custom_call_target="tpu_custom_call" | custom-call | flops 3489660928 | bytes 13631488 | tf_op jit(solution)/shard_map/pair_weights/pallas_call | solution.py:688
  521.6 6.9 %all-to-all-start.7 = ((bf16[16,32,1664]{2,1,0:T(8,128)(2,1)}), bf16[16,32,1664]{2,1,0:T(8,128)(2,1)S(1)}, u32[]{:S(2)}, u32[]{:S(2)}) async-start(bf16[16,32,1664]{2,1,0:T(8,128)(2,1)} %bitcast.29), calls=%async_computation.7 | async-start | bytes 3407872 | tf_op jit(solution)/shard_map/all_to_all | solution.py:876
  528.7 26.8 %expert_weights.3 = (f32[1024,2048]{1,0:T(8,128)}, f32[2048,1024]{1,0:T(8,128)}) custom-call(bf16[1024,1024]{1,0:T(8,128)(2,1)} %bitcast.14.rows_ref.refs_0_, bf16[1024,1024]{1,0:T(8,128)(2,1)} %bitcast.56, bf16[1024,1024]{1,0:T(8,128)(2,1)} %get-tuple-element.69.refs_2_, bf16[1024,1024]{1,0:T(8,128)(2,1)} %get-tuple-element.70.refs_3_, ...), custom_call_target="tpu_custom_call" | custom-call | flops 17179869184 | bytes 41943040 | tf_op jit(solution)/shard_map/expert_weights/pallas_call | solution.py:625
  555.5 8.2 %fusion.10 = bf16[1,1024,1024]{2,1,0:T(8,128)(2,1)} fusion(f32[1024,1024]{1,0:T(8,128)S(1)} %copy-done.2, f32[1024]{0:T(1024)S(1)} %bitcast.75, f32[1024]{0:T(1024)S(1)} %select_reduce_fusion, bf16[2048,1024]{1,0:T(8,128)(2,1)} %bitcast.25, s32[1024]{0:T(1024)S(1)} %copy-done.20), kind=kOutput, calls=%fused_computation.32 | convolution fusion | flops 4301258752 | bytes 10498048 | tf_op jit(solution)/shard_map/dot_general | solution.py:28
  (146 shorter events, 57.1 us)
Async XLA Ops:
  7.3 79.7 %all-gather.4.cloned.1.call-start = ((), (), s32[]{:S(2)}) async-start(), calls=%async_computation.8 | async-start | bytes 3145728 | tf_op jit(solution)/shard_map/all_gather | solution.py:939
  8.0 172.6 %all-gather.6.cloned.1.call-start = ((), (), s32[]{:S(2)}) async-start(), calls=%async_computation.9 | async-start | bytes 12582912 | tf_op jit(solution)/shard_map/all_gather | solution.py:940
  9.1 19.2 %collective-permute-start.1 = (bf16[512,3072]{1,0:T(8,128)(2,1)S(1)}, bf16[512,3072]{1,0:T(8,128)(2,1)}, u32[]{:S(2)}, u32[]{:S(2)}) collective-permute-start(bf16[512,3072]{1,0:T(8,128)(2,1)S(1)} %copy-done.7), channel_id=1, source_target_pairs={{0,16},{16,0},{1,17},{17,1},{2,18},{18,2},{3,19},{19,3},{4,20},{20... | collective-permute-start | bytes 9437192 | tf_op jit(solution)/shard_map/ppermute | solution.py:872
  9.7 16.7 %collective-permute-start = (bf16[24,512]{1,0:T(8,128)(2,1)S(1)}, bf16[24,512]{1,0:T(8,128)(2,1)S(1)}, u32[]{:S(2)}, u32[]{:S(2)}) collective-permute-start(bf16[24,512]{1,0:T(8,128)(2,1)S(1)} %concatenate.15), channel_id=1, source_target_pairs={{0,16},{16,0},{1,17},{17,1},{2,18},{18,2},{3,19},{19,3},{4,20},{20... | collective-permute-start | bytes 73736 | tf_op jit(solution)/shard_map/ppermute | solution.py:872
  18.0 88.5 %all-to-all-start.1 = ((bf16[16,128,1024]{2,1,0:T(8,128)(2,1)}), bf16[16,128,1024]{2,1,0:T(8,128)(2,1)}, u32[]{:S(2)}, u32[]{:S(2)}) async-start(bf16[16,128,1024]{2,1,0:T(8,128)(2,1)} %bitcast.58), calls=%async_computation.1 | async-start | bytes 8388608 | tf_op jit(solution)/shard_map/all_to_all | solution.py:876
  26.4 154.2 %all-gather.8.cloned.1.call-start = ((), (), s32[]{:S(2)}) async-start(), calls=%async_computation.10 | async-start | bytes 12582912 | tf_op jit(solution)/shard_map/all_gather | solution.py:941
  26.4 153.4 %copy-start.10 = (bf16[24,1024]{1,0:T(8,128)(2,1)}, bf16[24,1024]{1,0:T(8,128)(2,1)S(1)}, u32[]{:S(2)}) copy-start(bf16[24,1024]{1,0:T(8,128)(2,1)S(1)} %maximum_select_fusion) | copy-start | bytes 147460
  38.5 13.0 %collective-permute-start.2 = (bf16[1024,2048]{1,0:T(8,128)(2,1)}, bf16[1024,2048]{1,0:T(8,128)(2,1)}, u32[]{:S(2)}, u32[]{:S(2)}) collective-permute-start(bf16[1024,2048]{1,0:T(8,128)(2,1)} %get-tuple-element.61.own_k_ref.own_v_ref), channel_id=1, source_target_pairs={{0,16},{1,17},{2,18},{3,19},{4,20},{5,21},{6,22},{7,23},{8,24},{9,... | collective-permute-start | bytes 12582920 | tf_op jit(solution)/shard_map/ppermute | solution.py:988
  49.5 37.5 %copy-start.29 = (bf16[1,1024,1024]{2,1,0:T(8,128)(2,1)S(1)}, bf16[1,1024,1024]{2,1,0:T(8,128)(2,1)}, u32[]{:S(2)}) copy-start(bf16[1,1024,1024]{2,1,0:T(8,128)(2,1)} %param.17) | copy-start | bytes 6291460
  93.7 33.3 %copy-start.3 = (bf16[1024,1024]{1,0:T(8,128)(2,1)}, bf16[1024,1024]{1,0:T(8,128)(2,1)S(1)}, u32[]{:S(2)}) copy-start(bf16[1024,1024]{1,0:T(8,128)(2,1)S(1)} %add_convert_fusion.2) | copy-start | bytes 6291460
  106.5 63.0 %all-to-all-start = ((bf16[16,64,1024]{2,1,0:T(8,128)(2,1)}), bf16[16,64,1024]{2,1,0:T(8,128)(2,1)}, u32[]{:S(2)}, u32[]{:S(2)}) async-start(bf16[16,64,1024]{2,1,0:T(8,128)(2,1)} %bitcast.64), calls=%async_computation | async-start | bytes 4194304 | tf_op jit(solution)/shard_map/all_to_all | solution.py:876
  169.5 58.9 %all-to-all-start.3 = ((bf16[16,64,1024]{2,1,0:T(8,128)(2,1)}), bf16[16,64,1024]{2,1,0:T(8,128)(2,1)S(1)}, u32[]{:S(2)}, u32[]{:S(2)}) async-start(bf16[16,64,1024]{2,1,0:T(8,128)(2,1)} %bitcast.60), calls=%async_computation.3 | async-start | bytes 4194304 | tf_op jit(solution)/shard_map/all_to_all | solution.py:876
  228.4 55.2 %all-to-all-start.2 = ((bf16[16,64,1024]{2,1,0:T(8,128)(2,1)}), bf16[16,64,1024]{2,1,0:T(8,128)(2,1)}, u32[]{:S(2)}, u32[]{:S(2)}) async-start(bf16[16,64,1024]{2,1,0:T(8,128)(2,1)} %bitcast.61), calls=%async_computation.2 | async-start | bytes 4194304 | tf_op jit(solution)/shard_map/all_to_all | solution.py:876
  283.7 48.6 %all-to-all-start.4 = ((bf16[16,64,1024]{2,1,0:T(8,128)(2,1)}), bf16[16,64,1024]{2,1,0:T(8,128)(2,1)S(1)}, u32[]{:S(2)}, u32[]{:S(2)}) async-start(bf16[16,64,1024]{2,1,0:T(8,128)(2,1)} %bitcast.62), calls=%async_computation.4 | async-start | bytes 4194304 | tf_op jit(solution)/shard_map/all_to_all | solution.py:876
  332.2 96.5 %all-to-all-start.5 = ((bf16[16,128,1024]{2,1,0:T(8,128)(2,1)}), bf16[16,128,1024]{2,1,0:T(8,128)(2,1)}, u32[]{:S(2)}, u32[]{:S(2)}) async-start(bf16[16,128,1024]{2,1,0:T(8,128)(2,1)} %bitcast.59), calls=%async_computation.5 | async-start | bytes 8388608 | tf_op jit(solution)/shard_map/all_to_all | solution.py:876
  355.9 26.2 %copy-start.13 = (bf16[1024,128]{1,0:T(8,128)(2,1)S(1)}, bf16[1024,128]{1,0:T(8,128)(2,1)}, u32[]{:S(2)}) copy-start(bf16[1024,128]{1,0:T(8,128)(2,1)} %get-tuple-element.82) | copy-start | bytes 786436
  355.9 28.2 %copy-start.6 = (bf16[16,64,1024]{2,1,0:T(8,128)(2,1)S(1)}, bf16[16,64,1024]{2,1,0:T(8,128)(2,1)}, u32[]{:S(2)}) copy-start(bf16[16,64,1024]{2,1,0:T(8,128)(2,1)} %copy-done.5) | copy-start | bytes 6291460
  355.9 28.3 %copy-start.12 = (bf16[1024,128]{1,0:T(8,128)(2,1)S(1)}, bf16[1024,128]{1,0:T(8,128)(2,1)}, u32[]{:S(2)}) copy-start(bf16[1024,128]{1,0:T(8,128)(2,1)} %get-tuple-element.83) | copy-start | bytes 786436
  380.5 25.0 %collective-permute-start.3 = (bf16[2,1024,512]{2,1,0:T(8,128)(2,1)}, bf16[2,1024,512]{2,1,0:T(8,128)(2,1)S(1)}, u32[]{:S(2)}, u32[]{:S(2)}) collective-permute-start(bf16[2,1024,512]{2,1,0:T(8,128)(2,1)} %get-tuple-element.81), channel_id=1, source_target_pairs={{16,0},{17,1},{18,2},{19,3},{20,4},{21,5},{22,6},{23,7},{24,8},{25... | collective-permute-start | bytes 6291464 | tf_op jit(solution)/shard_map/ppermute | solution.py:1060
  419.4 5.3 collective-permute-start.4
  428.7 76.9 %all-to-all-start.6 = ((bf16[16,32,2688]{2,1,0:T(8,128)(2,1)}), bf16[16,32,2688]{2,1,0:T(8,128)(2,1)S(1)}, u32[]{:S(2)}, u32[]{:S(2)}) async-start(bf16[16,32,2688]{2,1,0:T(8,128)(2,1)} %bitcast.23), calls=%async_computation.6 | async-start | bytes 5505024 | tf_op jit(solution)/shard_map/all_to_all | solution.py:876
  464.2 25.2 %collective-permute-start.5 = (bf16[2,1024,512]{2,1,0:T(8,128)(2,1)}, bf16[2,1024,512]{2,1,0:T(8,128)(2,1)S(1)}, u32[]{:S(2)}, u32[]{:S(2)}) collective-permute-start(bf16[2,1024,512]{2,1,0:T(8,128)(2,1)} %get-tuple-element.91), channel_id=1, source_target_pairs={{16,0},{17,1},{18,2},{19,3},{20,4},{21,5},{22,6},{23,7},{24,8},{25... | collective-permute-start | bytes 6291464 | tf_op jit(solution)/shard_map/ppermute | solution.py:1060
  465.8 62.9 %collective-permute-start.7 = (bf16[1024,2048]{1,0:T(8,128)(2,1)}, bf16[1024,2048]{1,0:T(8,128)(2,1)}, u32[]{:S(2)}, u32[]{:S(2)}) collective-permute-start(bf16[1024,2048]{1,0:T(8,128)(2,1)} %get-tuple-element.99), channel_id=1, source_target_pairs={{0,16},{16,0},{1,17},{17,1},{2,18},{18,2},{3,19},{19,3},{4,20},{20... | collective-permute-start | bytes 12582920 | tf_op jit(solution)/shard_map/ppermute | solution.py:872
  486.0 42.6 %collective-permute-start.8 = (bf16[2048,1024]{1,0:T(8,128)(2,1)}, bf16[2048,1024]{1,0:T(8,128)(2,1)}, u32[]{:S(2)}, u32[]{:S(2)}) collective-permute-start(bf16[2048,1024]{1,0:T(8,128)(2,1)} %get-tuple-element.100), channel_id=1, source_target_pairs={{0,16},{16,0},{1,17},{17,1},{2,18},{18,2},{3,19},{19,3},{4,20},{20... | collective-permute-start | bytes 12582920 | tf_op jit(solution)/shard_map/ppermute | solution.py:872
  506.0 8.8 %copy-start.4 = (bf16[1024,1024]{1,0:T(8,128)(2,1)S(1)}, bf16[1024,1024]{1,0:T(8,128)(2,1)}, u32[]{:S(2)}) copy-start(bf16[1024,1024]{1,0:T(8,128)(2,1)} %copy-done.3) | copy-start | bytes 6291460
  506.0 8.8 %copy-start.11 = (bf16[24,1024]{1,0:T(8,128)(2,1)S(1)}, bf16[24,1024]{1,0:T(8,128)(2,1)}, u32[]{:S(2)}) copy-start(bf16[24,1024]{1,0:T(8,128)(2,1)} %copy-done.10) | copy-start | bytes 147460
  514.7 3.8 collective-permute-start.6
  518.5 10.1 %copy-start.16 = (s32[1,1024,1]{1,2,0:T(1,128)S(1)}, s32[1,1024,1]{1,2,0:T(1,128)}, u32[]{:S(2)}) copy-start(s32[1,1024,1]{1,2,0:T(1,128)} %param.19) | copy-start | bytes 12292
  521.6 44.1 %all-to-all-start.7 = ((bf16[16,32,1664]{2,1,0:T(8,128)(2,1)}), bf16[16,32,1664]{2,1,0:T(8,128)(2,1)S(1)}, u32[]{:S(2)}, u32[]{:S(2)}) async-start(bf16[16,32,1664]{2,1,0:T(8,128)(2,1)} %bitcast.29), calls=%async_computation.7 | async-start | bytes 3407872 | tf_op jit(solution)/shard_map/all_to_all | solution.py:876
  528.6 26.8 %copy-start.2 = (f32[1024,1024]{1,0:T(8,128)S(1)}, f32[1024,1024]{1,0:T(8,128)}, u32[]{:S(2)}) copy-start(f32[1024,1024]{1,0:T(8,128)} %copy-done) | copy-start | bytes 12582916
  528.6 26.8 %copy-start.18 = (f32[1,1024]{1,0:T(1,128)S(1)}, f32[1,1024]{1,0:T(1,128)}, u32[]{:S(2)}) copy-start(f32[1,1024]{1,0:T(1,128)} %get-tuple-element.165) | copy-start | bytes 12292
  528.6 26.8 %copy-start.20 = (s32[1024]{0:T(1024)S(1)}, s32[1024]{0:T(1024)}, u32[]{:S(2)}) copy-start(s32[1024]{0:T(1024)} %copy-done.19) | copy-start | bytes 12292
  (21 other events, 66.1 us)
Sparse Core Ops, SparseCore 0:
  9.7 13.2 all-gather.3
  24.5 25.1 all-gather.5
  51.3 21.4 all-gather.7

commit v4 on v3

--- a/solution.py
+++ b/solution.py
@@ -320,7 +320,7 @@
     prev_grad_ref,
     own_grad_ref,
     grad_aug,
-    keys_both,
+    keys_turned,
     values_both,
     dq_total,
     dk_total,
@@ -342,17 +342,15 @@
     grad_aug[1, :, LANES:] = jnp.where(first, zero, less)
     ones = jnp.where((lane_index(block_k) & (HEAD_DIM - 1)) < 3, 1.0, 0.0).astype(BF16)
     keys_first = lane_index(block_k) < HEAD_DIM
-    queries_first = lane_index(block_q) < HEAD_DIM
     dq_total[...] = jnp.zeros_like(dq_total)
 
-    keys_both[:rows] = prev_k_ref[...]
-    keys_both[rows:] = own_k_ref[...]
+    keys_turned[:, :rows] = prev_k_ref[...].T
+    keys_turned[:, rows:] = own_k_ref[...].T
     values_both[:rows] = prev_v_ref[...]
     values_both[rows:] = own_v_ref[...]
 
     def visit(line, start):
         lines, queries_at = pl.ds(line, block_k), pl.ds(start, block_q)
-        keys = keys_both[lines, :]
         values_aug = jnp.concatenate([values_both[lines, :], ones], axis=1)
         probs, d_scores = [], []
         for h in range(2):
@@ -365,9 +363,9 @@
         dk_total[...] += jnp.where(
             keys_first, nn(d_scores[0], here_queries), nn(d_scores[1], here_queries)
         )
-        dq_total[queries_at, :] += jnp.where(
-            queries_first, tn(d_scores[0], keys), tn(d_scores[1], keys)
-        )
+        for h in range(2):
+            head = slice(h * HEAD_DIM, (h + 1) * HEAD_DIM)
+            dq_total[head, queries_at] += nn(keys_turned[head, lines], d_scores[h])
 
     @pl.when(has_prev == 0)
     def _():
@@ -391,7 +389,7 @@
             own_grad_ref[1, pl.ds(at, block_k), :] = dv_total[...].astype(BF16)
 
     over_visible(has_prev, own_prefix, rows, block_q, block_k, clear, visit, put)
-    dq_ref[...] = (dq_total[...] * (HEAD_DIM**-0.5)).astype(BF16)
+    dq_ref[...] = (dq_total[...].T * (HEAD_DIM**-0.5)).astype(BF16)
 
 
 def attention_backward(
@@ -415,9 +413,9 @@
             out_specs=[pl.BlockSpec((rows, LANES), lambda h, scalars: (0, h)), both, both],
             scratch_shapes=[
                 pltpu.VMEM((2, rows, 2 * LANES), BF16),
+                pltpu.VMEM((LANES, 2 * rows), BF16),
                 pltpu.VMEM((2 * rows, LANES), BF16),
-                pltpu.VMEM((2 * rows, LANES), BF16),
-                pltpu.VMEM((rows, LANES), F32),
+                pltpu.VMEM((LANES, rows), F32),
                 pltpu.VMEM((block_k, LANES), F32),
                 pltpu.VMEM((block_k, LANES), F32),
             ],
@@ -1017,16 +1015,17 @@
     d_mixed_chunks, act, du, dy, dz = ([d[i] for d in done] for i in range(5))
     back = [sent(d) for d in d_mixed_chunks]
     others = expert_weights(mixed_rows, dy, act, du, 1, None)
-    back[-1], others = lax.optimization_barrier((back[-1], others))
-    d_mixed = picked_up(back)
-    got = [swapped(o) for o in others]
     d_router_t = None
     for c in range(CHUNKS):
         part = tn(dz[c], mixed_rows[c])
         d_router_t = part if d_router_t is None else d_router_t + part
-
+    d_expert_bias = jnp.sum(out_grad[0].astype(F32), axis=0)
+    back[-1], others, d_router_t, d_expert_bias = lax.optimization_barrier(
+        (back[-1], others, d_router_t, d_expert_bias)
+    )
+    d_mixed = picked_up(back)
+    got = [swapped(o) for o in others]
     out_cot = out_grad[0].astype(F32)
-    d_expert_bias = jnp.sum(out_cot, axis=0)
     d_norm2_gain = jnp.sum(d_mixed * normed2, axis=0)
     d_norm2_bias = jnp.sum(d_mixed, axis=0)
     d_hidden = out_cot + norm_backward(d_mixed, normed2, inv_std2, norm2_gain)

time: 582 us -> 577 us (level)
  waiting for transfers between devices: 65 us -> 49.8 us
  Pallas kernels: 312 us -> 320 us
    pallas_call x2, Pallas kernels: 49 us -> 56.6 us  [attention_backward(): pl.pallas_call(partial(backward_kernel, block_q, block_k), grid_spec=pltp...]
    all_to_all x8, waiting for transfers between devices: 30.1 us -> 23.1 us  [exchanged(): lax.all_to_all(array, 'expert', split_axis=0, concat_axis=0, tiled=True)]
    ppermute x6, starting transfers between devices: 21.1 us -> 14.3 us  [swapped(): return lax.ppermute(array, 'fsdp', [(0, 1), (1, 0)])]
  transfers between devices with their start and end apart: 20 -> 20, of which waited for: 8 -> 7; matrix products, arithmetic and copies ran while one was open for 12% -> 13% of each run, Pallas kernels for 54% -> 56%
where the time goes in v4:
time: 577 us; the launch traced here: 570 us
  Pallas kernels  320 us (55%)
  starting transfers between devices  106 us (18%)
  matrix products  53.6 us (9%)
  waiting for transfers between devices  49.8 us (9%)
  other arithmetic  16.2 us (3%)
  between operations  15.3 us (3%)
  local copies, waits for them, and re-layouts  8.97 us (2%)
    pallas_call x2, Pallas kernels, run_expert(): pl.pallas_call(partial(expert_kernel, experts, block_r), grid_spec=pltpu....  95.6 us
    all_to_all x8, starting transfers between devices, exchanged(): lax.all_to_all(array, 'expert', split_axis=0, concat_axis=0, tiled=True)  84.7 us
    pallas_call x2, Pallas kernels, attention_backward(): pl.pallas_call(partial(backward_kernel, block_q, block_k), grid_spec=pltp...  56.6 us
    pallas_call x2, Pallas kernels, expert_weights(): pl.pallas_call(partial(expert_weights_kernel, chunks, got is not None), g...  52.1 us
    dot_general x8, matrix products, nn(): lax.dot_general(left, right, (((1,), (0,)), ((), ())), preferred_element_...  43.5 us
    pallas_call x1, Pallas kernels, attention_forward(): pl.pallas_call(partial(forward_kernel, block), grid_spec=pltpu.PrefetchSc...  35.4 us
    pallas_call x1, Pallas kernels, attention_weights(): pl.pallas_call(partial(weights_kernel, block_q, block_k), grid_spec=pltpu...  27.9 us
    all_to_all x8, waiting for transfers between devices, exchanged(): lax.all_to_all(array, 'expert', split_axis=0, concat_axis=0, tiled=True)  23.1 us
  transfers between devices with their start and end apart: 20, of which 7 were waited for; matrix products, arithmetic and copies ran while one was open for 13% of the time, Pallas kernels for 56%

profile of v4, /device:TPU:0, one launch (start us, length us, event | category | flops | bytes accessed | tf_op | source)
XLA Modules:
  0.0 569.8 jit_solution(9744531261405470472)
XLA Ops:
  10.2 6.0 %fusion.9 = bf16[2048,1024]{1,0:T(8,128)(2,1)} fusion(s32[1024]{0:T(1024)S(1)} %get-tuple-element.176, bf16[1,1024,1024]{2,1,0:T(8,128)(2,1)S(1)} %copy-done.3), kind=kOutput, calls=%fused_computation.28 | convolution fusion | flops 4299161600 | bytes 6295552 | tf_op jit(solution)/shard_map/dot_general | solution.py:28
  16.2 8.4 %all-to-all-start.1 = ((bf16[16,128,1024]{2,1,0:T(8,128)(2,1)}), bf16[16,128,1024]{2,1,0:T(8,128)(2,1)}, u32[]{:S(2)}, u32[]{:S(2)}) async-start(bf16[16,128,1024]{2,1,0:T(8,128)(2,1)} %bitcast.54), calls=%async_computation.1 | async-start | bytes 8388608 | tf_op jit(solution)/shard_map/all_to_all | solution.py:874
  26.5 10.2 %project.2 = (bf16[1024,2048]{1,0:T(8,128)(2,1)}, bf16[1024,1024]{1,0:T(8,128)(2,1)}) custom-call(s32[1]{0:T(128)} %bitcast.1.scalars, bf16[1024,1024]{1,0:T(8,128)(2,1)} %bitcast.72, f32[2,1024]{1,0:T(2,128)} %slice.117.norm_ref, bf16[512,3072]{1,0:T(8,128)(2,1)} %w_own_ref.1, bf16[512,3072]{1,0:T(8,128)(2,1)} %collective-permute-done.1.other_ref.w_other_ref, ...), custom_call_target="tpu_custom_call" | custom-call | flops 4294967296 | bytes 10485760 | tf_op jit(solution)/shard_map/project/pallas_call | solution.py:750
  42.0 5.8 %project.3.q_ref = bf16[1024,1024]{1,0:T(8,128)(2,1)} custom-call(s32[1]{0:T(128)} %bitcast.1.scalars, bf16[1024,1024]{1,0:T(8,128)(2,1)} %get-tuple-element.62.in_ref.refs_0_, bf16[512,3072]{1,0:T(8,128)(2,1)} %w_own_ref.1, bf16[512,3072]{1,0:T(8,128)(2,1)} %collective-permute-done.1.other_ref.w_other_ref, f32[1,1024]{1,0:T(1,128)} %get-tuple-element.172.add_ref), custom_call_target="tpu_custom_call" | custom-call | flops 2147483648 | bytes 6291456 | tf_op jit(solution)/shard_map/project/pallas_call | solution.py:750
  47.8 35.4 %attention_forward.1 = (bf16[1024,1024]{1,0:T(8,128)(2,1)}, f32[1024,1024]{1,0:T(8,128)}) custom-call(s32[2]{0:T(128)} %pad_add_fusion.scalars, bf16[1024,1024]{1,0:T(8,128)(2,1)} %project.3.q_ref, bf16[1024,2048]{1,0:T(8,128)(2,1)} %collective-permute-done.2.prev_k_ref.prev_v_ref, bf16[1024,2048]{1,0:T(8,128)(2,1)} %collective-permute-done.2.prev_k_ref.prev_v_ref, ...), custom_call_target="tpu_custom_call" | custom-call | flops 4294967296 | bytes 16777216 | tf_op jit(solution)/shard_map/attention_forward/pallas_call | solution.py:193
  83.2 5.3 fusion.29
  91.2 5.3 fusion.18
  96.4 8.3 %all-to-all-done.1 = bf16[16,128,1024]{2,1,0:T(8,128)(2,1)} async-done(((bf16[16,128,1024]{2,1,0:T(8,128)(2,1)}), bf16[16,128,1024]{2,1,0:T(8,128)(2,1)}, u32[]{:S(2)}, u32[]{:S(2)}) %all-to-all-start.1) | async-done | bytes 4194336 | tf_op jit(solution)/shard_map/all_to_all | solution.py:874
  104.7 20.6 %all-to-all-start = ((bf16[16,64,1024]{2,1,0:T(8,128)(2,1)}), bf16[16,64,1024]{2,1,0:T(8,128)(2,1)}, u32[]{:S(2)}, u32[]{:S(2)}) async-start(bf16[16,64,1024]{2,1,0:T(8,128)(2,1)} %bitcast.59), calls=%async_computation | async-start | bytes 4194304 | tf_op jit(solution)/shard_map/all_to_all | solution.py:874
  130.5 27.9 %attention_weights.1.weights_ref = bf16[8,2,2048,1024]{3,2,1,0:T(8,128)(2,1)} custom-call(s32[2]{0:T(128)} %pad_add_fusion.scalars, bf16[1024,1024]{1,0:T(8,128)(2,1)} %project.3.q_ref, bf16[1024,2048]{1,0:T(8,128)(2,1)} %collective-permute-done.2.prev_k_ref.prev_v_ref, bf16[1024,2048]{1,0:T(8,128)(2,1)} %get-tuple-element.63.own_k_ref.own_v_ref, ...), custom_call_target="tpu_custom_call" | custom-call | flops 8589934592 | bytes 77594624 | tf_op jit(solution)/shard_map/attention_weights/pallas_call | solution.py:284
  158.4 9.3 %all-to-all-done = bf16[16,64,1024]{2,1,0:T(8,128)(2,1)} async-done(((bf16[16,64,1024]{2,1,0:T(8,128)(2,1)}), bf16[16,64,1024]{2,1,0:T(8,128)(2,1)}, u32[]{:S(2)}, u32[]{:S(2)}) %all-to-all-start) | async-done | bytes 2097184 | tf_op jit(solution)/shard_map/all_to_all | solution.py:874
  167.8 9.8 %all-to-all-start.3 = ((bf16[16,64,1024]{2,1,0:T(8,128)(2,1)}), bf16[16,64,1024]{2,1,0:T(8,128)(2,1)}, u32[]{:S(2)}, u32[]{:S(2)}) async-start(bf16[16,64,1024]{2,1,0:T(8,128)(2,1)} %bitcast.56), calls=%async_computation.3 | async-start | bytes 4194304 | tf_op jit(solution)/shard_map/all_to_all | solution.py:874
  178.9 47.8 %expert_rows.2 = (bf16[16,2,64,1024]{3,2,1,0:T(8,128)(2,1)}, bf16[1024,1024]{1,0:T(8,128)(2,1)}, bf16[1024,4096]{1,0:T(8,128)(2,1)}, bf16[1024,4096]{1,0:T(8,128...) custom-call(s32[2]{0:T(128)} %pad_add_fusion.1.scalars.y_before_ref, ...), custom_call_target="tpu_custom_call" | custom-call | flops 34359738368 | bytes 46137344 | tf_op jit(solution)/shard_map/expert_rows/pallas_call | solution.py:536
  226.7 7.4 %all-to-all-start.2 = ((bf16[16,64,1024]{2,1,0:T(8,128)(2,1)}), bf16[16,64,1024]{2,1,0:T(8,128)(2,1)}, u32[]{:S(2)}, u32[]{:S(2)}) async-start(bf16[16,64,1024]{2,1,0:T(8,128)(2,1)} %bitcast.58), calls=%async_computation.2 | async-start | bytes 4194304 | tf_op jit(solution)/shard_map/all_to_all | solution.py:874
  234.2 47.8 %expert_rows.3 = (bf16[16,2,64,1024]{3,2,1,0:T(8,128)(2,1)}, bf16[1024,1024]{1,0:T(8,128)(2,1)}, bf16[1024,4096]{1,0:T(8,128)(2,1)}, bf16[1024,4096]{1,0:T(8,128...) custom-call(s32[2]{0:T(128)} %pad_add_fusion.1.scalars.y_before_ref, ...), custom_call_target="tpu_custom_call", output_to_operand_aliasing={{0}: (6, {})} | custom-call | flops 34359738368 | bytes 46137344 | tf_op jit(solution)/shard_map/expert_rows/pallas_call | solution.py:536
  282.0 7.4 %all-to-all-start.4 = ((bf16[16,64,1024]{2,1,0:T(8,128)(2,1)}), bf16[16,64,1024]{2,1,0:T(8,128)(2,1)}, u32[]{:S(2)}, u32[]{:S(2)}) async-start(bf16[16,64,1024]{2,1,0:T(8,128)(2,1)} %bitcast.57), calls=%async_computation.4 | async-start | bytes 4194304 | tf_op jit(solution)/shard_map/all_to_all | solution.py:874
  293.9 25.4 %expert_weights.2 = (bf16[1024,2048]{1,0:T(8,128)(2,1)}, bf16[2048,1024]{1,0:T(8,128)(2,1)}) custom-call(bf16[1024,1024]{1,0:T(8,128)(2,1)} %bitcast.14.rows_ref.refs_0_, bf16[1024,1024]{1,0:T(8,128)(2,1)} %bitcast.20.rows_ref.refs_1_, bf16[1024,1024]{1,0:T(8,128)(2,1)} %get-tuple-element.71.refs_2_, bf16[1024,1024]{1,0:T(8,128)(2,1)} %get-tuple-element.72.refs_3_, ...), custom_call_target="tpu_custom_call" | custom-call | flops 17179869184 | bytes 41943040 | tf_op jit(solution)/shard_map/expert_weights/pallas_call | solution.py:623
  319.3 6.0 %fusion.4 = f32[1024,1024]{1,0:T(8,128)} fusion(bf16[1024,1024]{1,0:T(8,128)(2,1)} %bitcast.18, s32[1024]{0:T(1024)S(1)} %get-tuple-element.175), kind=kOutput, calls=%fused_computation.22 | convolution fusion | flops 2148532224 | bytes 6295552 | tf_op jit(solution)/shard_map/dot_general | solution.py:28
  325.3 5.5 all-to-all-done.4
  330.8 10.2 %all-to-all-start.5 = ((bf16[16,128,1024]{2,1,0:T(8,128)(2,1)}), bf16[16,128,1024]{2,1,0:T(8,128)(2,1)}, u32[]{:S(2)}, u32[]{:S(2)}) async-start(bf16[16,128,1024]{2,1,0:T(8,128)(2,1)} %bitcast.55), calls=%async_computation.5 | async-start | bytes 8388608 | tf_op jit(solution)/shard_map/all_to_all | solution.py:874
  341.0 7.0 %multiply_reduce_fusion = (f32[1024]{0:T(1024)S(1)}, f32[1024]{0:T(1024)S(1)}, f32[1024]{0:T(1024)S(1)}, f32[1024]{0:T(1024)S(1)}, f32[1024,1024]{1,0:T(8,128)S(1)}) fusion(f32[1024,1024]{1,0:T(8,128)} %copy-done, f32[1024]{0:T(1024)S(1)} %add_rsqrt_fusion, f32[1024]{0:T(1024)S(1)} %broadcast_multiply_fusion.2, f32[1024]{0:T(1024)S(1)} %bitcast.61, ...), kind=kOutput, calls=%fused_computation.10 | convolution fusion | flops 2159013888 | bytes 14712832 | tf_op jit(solution)/shard_map/dot_general | solution.py:28
  354.9 28.3 %attention_backward.2 = (bf16[1024,512]{1,0:T(8,128)(2,1)}, bf16[2,1024,512]{2,1,0:T(8,128)(2,1)}, bf16[2,1024,512]{2,1,0:T(8,128)(2,1)}) custom-call(s32[2]{0:T(128)} %pad_add_fusion.scalars, bf16[1024,1024]{1,0:T(8,128)(2,1)} %project.3.q_ref, bf16[1024,2048]{1,0:T(8,128)(2,1)} %collective-permute-done.2.prev_k_ref.prev_v_ref, ...), custom_call_target="tpu_custom_call" | custom-call | flops 32212254720 | bytes 13631488 | tf_op jit(solution)/shard_map/attention_backward/pallas_call | solution.py:406
  385.9 15.4 %collective-permute-done.3.refs_3_.refs_2_ = bf16[2,1024,512]{2,1,0:T(8,128)(2,1)S(1)} collective-permute-done((bf16[2,1024,512]{2,1,0:T(8,128)(2,1)}, bf16[2,1024,512]{2,1,0:T(8,128)(2,1)S(1)}, u32[]{:S(2)}, u32[]{:S(2)}) %collective-permute-start.3) | collective-permute-done | bytes 2097184 | tf_op jit(solution)/shard_map/ppermute | solution.py:1059
  402.7 12.6 %pair_weights.2 = (bf16[512,2688]{1,0:T(8,128)(2,1)}, bf16[512,2688]{1,0:T(8,128)(2,1)}) custom-call(s32[1]{0:T(128)} %bitcast.1.scalars, bf16[1024,1024]{1,0:T(8,128)(2,1)} %get-tuple-element.62.in_ref.refs_0_, bf16[1024,512]{1,0:T(8,128)(2,1)} %get-tuple-element.83.refs_1_.refs_0_, bf16[2,1024,512]{2,1,0:T(8,128)(2,1)} %get-tuple-element.84.refs_2_.refs_1_, ...), custom_call_target="tpu_custom_call" | custom-call | flops 5637144576 | bytes 22020096 | tf_op jit(solution)/shard_map/pair_weights/pallas_call | solution.py:686
  424.5 13.8 %all-to-all-start.6 = ((bf16[16,32,2688]{2,1,0:T(8,128)(2,1)}), bf16[16,32,2688]{2,1,0:T(8,128)(2,1)S(1)}, u32[]{:S(2)}, u32[]{:S(2)}) async-start(bf16[16,32,2688]{2,1,0:T(8,128)(2,1)} %bitcast.23), calls=%async_computation.6 | async-start | bytes 5505024 | tf_op jit(solution)/shard_map/all_to_all | solution.py:874
  438.3 28.3 %attention_backward.3 = (bf16[1024,512]{1,0:T(8,128)(2,1)}, bf16[2,1024,512]{2,1,0:T(8,128)(2,1)}, bf16[2,1024,512]{2,1,0:T(8,128)(2,1)}) custom-call(s32[2]{0:T(128)} %pad_add_fusion.scalars, bf16[1024,1024]{1,0:T(8,128)(2,1)} %project.3.q_ref, bf16[1024,2048]{1,0:T(8,128)(2,1)} %collective-permute-done.2.prev_k_ref.prev_v_ref, ...), custom_call_target="tpu_custom_call" | custom-call | flops 32212254720 | bytes 13631488 | tf_op jit(solution)/shard_map/attention_backward/pallas_call | solution.py:406
  468.2 13.3 %collective-permute-start.7 = (bf16[1024,2048]{1,0:T(8,128)(2,1)}, bf16[1024,2048]{1,0:T(8,128)(2,1)}, u32[]{:S(2)}, u32[]{:S(2)}) collective-permute-start(bf16[1024,2048]{1,0:T(8,128)(2,1)} %get-tuple-element.103), channel_id=1, source_target_pairs={{0,16},{16,0},{1,17},{17,1},{2,18},{18,2},{3,19},{19,3},{4,20},{20... | collective-permute-start | bytes 12582920 | tf_op jit(solution)/shard_map/ppermute | solution.py:870
  486.2 15.0 %first_norm.1 = (bf16[1024,1024]{1,0:T(8,128)(2,1)}, f32[128,1024]{1,0:T(8,128)}) custom-call(s32[1]{0:T(128)} %bitcast.1.scalars, bf16[1024,1024]{1,0:T(8,128)(2,1)} %bitcast.73, f32[1024,1024]{1,0:T(8,128)} %get-tuple-element.166.dh_ref, f32[1,1024]{1,0:T(1,128)} %get-tuple-element.167.gain_ref, bf16[512,3072]{1,0:T(8,128)(2,1)} %w_own_ref.1, ...), custom_call_target="tpu_custom_call" | custom-call | flops 6442450944 | bytes 20971520 | tf_op jit(solution)/shard_map/first_norm/pallas_call | solution.py:830
  501.5 8.5 %pair_weights.3 = (bf16[512,1664]{1,0:T(8,128)(2,1)}, bf16[512,1664]{1,0:T(8,128)(2,1)}) custom-call(s32[1]{0:T(128)} %bitcast.1.scalars, bf16[1024,1024]{1,0:T(8,128)(2,1)} %get-tuple-element.62.in_ref.refs_0_, bf16[1024,512]{1,0:T(8,128)(2,1)} %get-tuple-element.93.refs_3_.refs_1_, bf16[2,1024,512]{2,1,0:T(8,128)(2,1)} %get-tuple-element.94.refs_4_.refs_2_, ...), custom_call_target="tpu_custom_call" | custom-call | flops 3489660928 | bytes 13631488 | tf_op jit(solution)/shard_map/pair_weights/pallas_call | solution.py:686
  517.0 7.1 %all-to-all-start.7 = ((bf16[16,32,1664]{2,1,0:T(8,128)(2,1)}), bf16[16,32,1664]{2,1,0:T(8,128)(2,1)S(1)}, u32[]{:S(2)}, u32[]{:S(2)}) async-start(bf16[16,32,1664]{2,1,0:T(8,128)(2,1)} %bitcast.29), calls=%async_computation.7 | async-start | bytes 3407872 | tf_op jit(solution)/shard_map/all_to_all | solution.py:874
  524.2 26.8 %expert_weights.3 = (f32[1024,2048]{1,0:T(8,128)}, f32[2048,1024]{1,0:T(8,128)}) custom-call(bf16[1024,1024]{1,0:T(8,128)(2,1)} %bitcast.14.rows_ref.refs_0_, bf16[1024,1024]{1,0:T(8,128)(2,1)} %bitcast.20.rows_ref.refs_1_, bf16[1024,1024]{1,0:T(8,128)(2,1)} %get-tuple-element.71.refs_2_, bf16[1024,1024]{1,0:T(8,128)(2,1)} %get-tuple-element.72.refs_3_, ...), custom_call_target="tpu_custom_call" | custom-call | flops 17179869184 | bytes 41943040 | tf_op jit(solution)/shard_map/expert_weights/pallas_call | solution.py:623
  551.0 8.2 %fusion.10 = bf16[1,1024,1024]{2,1,0:T(8,128)(2,1)} fusion(f32[1024,1024]{1,0:T(8,128)S(1)} %copy-done.2, f32[1024]{0:T(1024)S(1)} %bitcast.70, f32[1024]{0:T(1024)S(1)} %select_reduce_fusion, bf16[2048,1024]{1,0:T(8,128)(2,1)} %bitcast.25, s32[1024]{0:T(1024)S(1)} %copy-done.15), kind=kOutput, calls=%fused_computation.32 | convolution fusion | flops 4301258752 | bytes 10498048 | tf_op jit(solution)/shard_map/dot_general | solution.py:28
  (136 shorter events, 60.5 us)
Async XLA Ops:
  7.3 75.9 %all-gather.4.cloned.1.call-start = ((), (), s32[]{:S(2)}) async-start(), calls=%async_computation.8 | async-start | bytes 3145728 | tf_op jit(solution)/shard_map/all_gather | solution.py:937
  8.0 170.9 %all-gather.6.cloned.1.call-start = ((), (), s32[]{:S(2)}) async-start(), calls=%async_computation.9 | async-start | bytes 12582912 | tf_op jit(solution)/shard_map/all_gather | solution.py:938
  8.8 17.7 %collective-permute-start.1 = (bf16[512,3072]{1,0:T(8,128)(2,1)}, bf16[512,3072]{1,0:T(8,128)(2,1)}, u32[]{:S(2)}, u32[]{:S(2)}) collective-permute-start(bf16[512,3072]{1,0:T(8,128)(2,1)} %w_own_ref.1), channel_id=1, source_target_pairs={{0,16},{16,0},{1,17},{17,1},{2,18},{18,2},{3,19},{19,3},{4,20},{20... | collective-permute-start | bytes 9437192 | tf_op jit(solution)/shard_map/ppermute | solution.py:870
  9.5 15.1 %collective-permute-start = (bf16[24,512]{1,0:T(8,128)(2,1)S(1)}, bf16[24,512]{1,0:T(8,128)(2,1)S(1)}, u32[]{:S(2)}, u32[]{:S(2)}) collective-permute-start(bf16[24,512]{1,0:T(8,128)(2,1)S(1)} %concatenate.15), channel_id=1, source_target_pairs={{0,16},{16,0},{1,17},{17,1},{2,18},{18,2},{3,19},{19,3},{4,20},{20... | collective-permute-start | bytes 73736 | tf_op jit(solution)/shard_map/ppermute | solution.py:870
  10.2 6.0 %copy-start.14 = (s32[1024]{0:T(1024)}, s32[1024]{0:T(1024)S(1)}, u32[]{:S(2)}) copy-start(s32[1024]{0:T(1024)S(1)} %get-tuple-element.176) | copy-start | bytes 12292
  16.2 88.5 %all-to-all-start.1 = ((bf16[16,128,1024]{2,1,0:T(8,128)(2,1)}), bf16[16,128,1024]{2,1,0:T(8,128)(2,1)}, u32[]{:S(2)}, u32[]{:S(2)}) async-start(bf16[16,128,1024]{2,1,0:T(8,128)(2,1)} %bitcast.54), calls=%async_computation.1 | async-start | bytes 8388608 | tf_op jit(solution)/shard_map/all_to_all | solution.py:874
  24.5 154.4 %all-gather.8.cloned.1.call-start = ((), (), s32[]{:S(2)}) async-start(), calls=%async_computation.10 | async-start | bytes 12582912 | tf_op jit(solution)/shard_map/all_gather | solution.py:939
  24.6 153.6 %copy-start.5 = (bf16[24,1024]{1,0:T(8,128)(2,1)}, bf16[24,1024]{1,0:T(8,128)(2,1)S(1)}, u32[]{:S(2)}) copy-start(bf16[24,1024]{1,0:T(8,128)(2,1)S(1)} %maximum_select_fusion) | copy-start | bytes 147460
  36.7 11.1 %collective-permute-start.2 = (bf16[1024,2048]{1,0:T(8,128)(2,1)}, bf16[1024,2048]{1,0:T(8,128)(2,1)}, u32[]{:S(2)}, u32[]{:S(2)}) collective-permute-start(bf16[1024,2048]{1,0:T(8,128)(2,1)} %get-tuple-element.63.own_k_ref.own_v_ref), channel_id=1, source_target_pairs={{0,16},{1,17},{2,18},{3,19},{4,20},{5,21},{6,22},{7,23},{8,24},{9,... | collective-permute-start | bytes 12582920 | tf_op jit(solution)/shard_map/ppermute | solution.py:986
  104.7 63.1 %all-to-all-start = ((bf16[16,64,1024]{2,1,0:T(8,128)(2,1)}), bf16[16,64,1024]{2,1,0:T(8,128)(2,1)}, u32[]{:S(2)}, u32[]{:S(2)}) async-start(bf16[16,64,1024]{2,1,0:T(8,128)(2,1)} %bitcast.59), calls=%async_computation | async-start | bytes 4194304 | tf_op jit(solution)/shard_map/all_to_all | solution.py:874
  167.8 58.9 %all-to-all-start.3 = ((bf16[16,64,1024]{2,1,0:T(8,128)(2,1)}), bf16[16,64,1024]{2,1,0:T(8,128)(2,1)}, u32[]{:S(2)}, u32[]{:S(2)}) async-start(bf16[16,64,1024]{2,1,0:T(8,128)(2,1)} %bitcast.56), calls=%async_computation.3 | async-start | bytes 4194304 | tf_op jit(solution)/shard_map/all_to_all | solution.py:874
  226.7 55.3 %all-to-all-start.2 = ((bf16[16,64,1024]{2,1,0:T(8,128)(2,1)}), bf16[16,64,1024]{2,1,0:T(8,128)(2,1)}, u32[]{:S(2)}, u32[]{:S(2)}) async-start(bf16[16,64,1024]{2,1,0:T(8,128)(2,1)} %bitcast.58), calls=%async_computation.2 | async-start | bytes 4194304 | tf_op jit(solution)/shard_map/all_to_all | solution.py:874
  282.0 7.8 %copy-start.7 = (bf16[1024,128]{1,0:T(8,128)(2,1)S(1)}, bf16[1024,128]{1,0:T(8,128)(2,1)}, u32[]{:S(2)}) copy-start(bf16[1024,128]{1,0:T(8,128)(2,1)} %get-tuple-element.79) | copy-start | bytes 786436
  282.0 9.8 %copy-start.8 = (bf16[1024,128]{1,0:T(8,128)(2,1)S(1)}, bf16[1024,128]{1,0:T(8,128)(2,1)}, u32[]{:S(2)}) copy-start(bf16[1024,128]{1,0:T(8,128)(2,1)} %get-tuple-element.80) | copy-start | bytes 786436
  282.0 48.8 %all-to-all-start.4 = ((bf16[16,64,1024]{2,1,0:T(8,128)(2,1)}), bf16[16,64,1024]{2,1,0:T(8,128)(2,1)}, u32[]{:S(2)}, u32[]{:S(2)}) async-start(bf16[16,64,1024]{2,1,0:T(8,128)(2,1)} %bitcast.57), calls=%async_computation.4 | async-start | bytes 4194304 | tf_op jit(solution)/shard_map/all_to_all | solution.py:874
  330.8 93.7 %all-to-all-start.5 = ((bf16[16,128,1024]{2,1,0:T(8,128)(2,1)}), bf16[16,128,1024]{2,1,0:T(8,128)(2,1)}, u32[]{:S(2)}, u32[]{:S(2)}) async-start(bf16[16,128,1024]{2,1,0:T(8,128)(2,1)} %bitcast.55), calls=%async_computation.5 | async-start | bytes 8388608 | tf_op jit(solution)/shard_map/all_to_all | solution.py:874
  341.0 7.1 %copy-start.1 = (f32[1024,1024]{1,0:T(8,128)S(1)}, f32[1024,1024]{1,0:T(8,128)}, u32[]{:S(2)}) copy-start(f32[1024,1024]{1,0:T(8,128)} %copy-done) | copy-start | bytes 12582916
  348.1 3.2 copy-start.24
  351.2 3.7 copy-start.4
  383.3 18.1 %collective-permute-start.3 = (bf16[2,1024,512]{2,1,0:T(8,128)(2,1)}, bf16[2,1024,512]{2,1,0:T(8,128)(2,1)S(1)}, u32[]{:S(2)}, u32[]{:S(2)}) collective-permute-start(bf16[2,1024,512]{2,1,0:T(8,128)(2,1)} %get-tuple-element.85), channel_id=1, source_target_pairs={{16,0},{17,1},{18,2},{19,3},{20,4},{21,5},{22,6},{23,7},{24,8},{25... | collective-permute-start | bytes 6291464 | tf_op jit(solution)/shard_map/ppermute | solution.py:1059
  415.3 5.3 collective-permute-start.4
  424.5 76.6 %all-to-all-start.6 = ((bf16[16,32,2688]{2,1,0:T(8,128)(2,1)}), bf16[16,32,2688]{2,1,0:T(8,128)(2,1)S(1)}, u32[]{:S(2)}, u32[]{:S(2)}) async-start(bf16[16,32,2688]{2,1,0:T(8,128)(2,1)} %bitcast.23), calls=%async_computation.6 | async-start | bytes 5505024 | tf_op jit(solution)/shard_map/all_to_all | solution.py:874
  466.6 18.2 %collective-permute-start.5 = (bf16[2,1024,512]{2,1,0:T(8,128)(2,1)}, bf16[2,1024,512]{2,1,0:T(8,128)(2,1)S(1)}, u32[]{:S(2)}, u32[]{:S(2)}) collective-permute-start(bf16[2,1024,512]{2,1,0:T(8,128)(2,1)} %get-tuple-element.95), channel_id=1, source_target_pairs={{16,0},{17,1},{18,2},{19,3},{20,4},{21,5},{22,6},{23,7},{24,8},{25... | collective-permute-start | bytes 6291464 | tf_op jit(solution)/shard_map/ppermute | solution.py:1059
  468.2 56.0 %collective-permute-start.7 = (bf16[1024,2048]{1,0:T(8,128)(2,1)}, bf16[1024,2048]{1,0:T(8,128)(2,1)}, u32[]{:S(2)}, u32[]{:S(2)}) collective-permute-start(bf16[1024,2048]{1,0:T(8,128)(2,1)} %get-tuple-element.103), channel_id=1, source_target_pairs={{0,16},{16,0},{1,17},{17,1},{2,18},{18,2},{3,19},{19,3},{4,20},{20... | collective-permute-start | bytes 12582920 | tf_op jit(solution)/shard_map/ppermute | solution.py:870
  481.5 42.7 %collective-permute-start.8 = (bf16[2048,1024]{1,0:T(8,128)(2,1)}, bf16[2048,1024]{1,0:T(8,128)(2,1)}, u32[]{:S(2)}, u32[]{:S(2)}) collective-permute-start(bf16[2048,1024]{1,0:T(8,128)(2,1)} %get-tuple-element.104), channel_id=1, source_target_pairs={{0,16},{16,0},{1,17},{17,1},{2,18},{18,2},{3,19},{19,3},{4,20},{20... | collective-permute-start | bytes 12582920 | tf_op jit(solution)/shard_map/ppermute | solution.py:870
  501.5 8.7 %copy-start.6 = (bf16[24,1024]{1,0:T(8,128)(2,1)S(1)}, bf16[24,1024]{1,0:T(8,128)(2,1)}, u32[]{:S(2)}) copy-start(bf16[24,1024]{1,0:T(8,128)(2,1)} %copy-done.5) | copy-start | bytes 147460
  510.0 3.8 collective-permute-start.6
  513.8 10.3 %copy-start.11 = (s32[1,1024,1]{1,2,0:T(1,128)S(1)}, s32[1,1024,1]{1,2,0:T(1,128)}, u32[]{:S(2)}) copy-start(s32[1,1024,1]{1,2,0:T(1,128)} %param.19) | copy-start | bytes 12292
  517.0 44.3 %all-to-all-start.7 = ((bf16[16,32,1664]{2,1,0:T(8,128)(2,1)}), bf16[16,32,1664]{2,1,0:T(8,128)(2,1)S(1)}, u32[]{:S(2)}, u32[]{:S(2)}) async-start(bf16[16,32,1664]{2,1,0:T(8,128)(2,1)} %bitcast.29), calls=%async_computation.7 | async-start | bytes 3407872 | tf_op jit(solution)/shard_map/all_to_all | solution.py:874
  524.2 26.8 %copy-start.2 = (f32[1024,1024]{1,0:T(8,128)S(1)}, f32[1024,1024]{1,0:T(8,128)}, u32[]{:S(2)}) copy-start(f32[1024,1024]{1,0:T(8,128)} %copy-done) | copy-start | bytes 12582916
  524.2 26.8 %copy-start.13 = (f32[1,1024]{1,0:T(1,128)S(1)}, f32[1,1024]{1,0:T(1,128)}, u32[]{:S(2)}) copy-start(f32[1,1024]{1,0:T(1,128)} %get-tuple-element.168) | copy-start | bytes 12292
  524.2 26.8 %copy-start.15 = (s32[1024]{0:T(1024)S(1)}, s32[1024]{0:T(1024)}, u32[]{:S(2)}) copy-start(s32[1024]{0:T(1024)} %copy-done.14) | copy-start | bytes 12292
  (15 other events, 30.6 us)
Sparse Core Ops, SparseCore 0:
  9.7 13.2 all-gather.3
  24.5 25.9 all-gather.5
  52.1 20.8 all-gather.7

commit v5 on v4

--- a/solution.py
+++ b/solution.py
@@ -692,7 +692,7 @@
             out_specs=[out, out],
         ),
         out_shape=[jax.ShapeDtypeStruct((width // 2, columns), BF16)] * 2,
-        compiler_params=pltpu.CompilerParams(vmem_limit_bytes=VMEM_LIMIT),
+        compiler_params=pltpu.CompilerParams(vmem_limit_bytes=40 << 20),
         cost_estimate=pl.CostEstimate(
             flops=2 * rows * width * columns,
             bytes_accessed=4 * (rows + width) * columns,
@@ -840,7 +840,7 @@
             jax.ShapeDtypeStruct((rows, width), BF16),
             jax.ShapeDtypeStruct((LANES, width), F32),
         ],
-        compiler_params=pltpu.CompilerParams(vmem_limit_bytes=VMEM_LIMIT),
+        compiler_params=pltpu.CompilerParams(vmem_limit_bytes=40 << 20),
         cost_estimate=pl.CostEstimate(
             flops=6 * rows * width * width,
             bytes_accessed=14 * rows * width + 6 * width * width,

time: 577 us -> 583 us (1.010)
  local copies, waits for them, and re-layouts: 8.97 us -> 24.1 us
  Pallas kernels: 320 us -> 311 us
  waiting for transfers between devices: 49.8 us -> 57.3 us
  matrix products: 53.6 us -> 47.2 us
    unnamed x60 -> x100, local copies, waits for them, and re-layouts: 4.2 us -> 19.4 us
    pallas_call x2, Pallas kernels: 21.1 us -> 11.6 us  [pair_weights(): pl.pallas_call(partial(pair_weights_kernel, bool(context_side)), grid_spe...]
  transfers between devices with their start and end apart: 20 -> 20, of which waited for: 7 -> 7; matrix products, arithmetic and copies ran while one was open for 13% -> 11% of each run, Pallas kernels for 56% -> 54%
where the time goes in v5:
time: 583 us; the launch traced here: 575 us
  Pallas kernels  311 us (53%)
  starting transfers between devices  106 us (18%)
  waiting for transfers between devices  57.3 us (10%)
  matrix products  47.2 us (8%)
  local copies, waits for them, and re-layouts  24.1 us (4%)
  between operations  15.5 us (3%)
  other arithmetic  14.4 us (2%)
    pallas_call x2, Pallas kernels, run_expert(): pl.pallas_call(partial(expert_kernel, experts, block_r), grid_spec=pltpu....  95.6 us
    all_to_all x8, starting transfers between devices, exchanged(): lax.all_to_all(array, 'expert', split_axis=0, concat_axis=0, tiled=True)  84.6 us
    pallas_call x2, Pallas kernels, attention_backward(): pl.pallas_call(partial(backward_kernel, block_q, block_k), grid_spec=pltp...  57.4 us
    pallas_call x2, Pallas kernels, expert_weights(): pl.pallas_call(partial(expert_weights_kernel, chunks, got is not None), g...  52.2 us
    dot_general x8, matrix products, nn(): lax.dot_general(left, right, (((1,), (0,)), ((), ())), preferred_element_...  40 us
    pallas_call x1, Pallas kernels, attention_forward(): pl.pallas_call(partial(forward_kernel, block), grid_spec=pltpu.PrefetchSc...  35.7 us
    all_to_all x8, waiting for transfers between devices, exchanged(): lax.all_to_all(array, 'expert', split_axis=0, concat_axis=0, tiled=True)  28.2 us
    pallas_call x1, Pallas kernels, attention_weights(): pl.pallas_call(partial(weights_kernel, block_q, block_k), grid_spec=pltpu...  28 us
  transfers between devices with their start and end apart: 20, of which 7 were waited for; matrix products, arithmetic and copies ran while one was open for 11% of the time, Pallas kernels for 54%

profile of v5, /device:TPU:0, one launch (start us, length us, event | category | flops | bytes accessed | tf_op | source)
XLA Modules:
  0.0 575.5 jit_solution(8531176683091226247)
XLA Ops:
  10.2 6.0 %fusion.9 = bf16[2048,1024]{1,0:T(8,128)(2,1)} fusion(s32[1024]{0:T(1024)S(1)} %get-tuple-element.176, bf16[1,1024,1024]{2,1,0:T(8,128)(2,1)S(1)} %copy-done.21), kind=kOutput, calls=%fused_computation.28 | convolution fusion | flops 4299161600 | bytes 6295552 | tf_op jit(solution)/shard_map/dot_general | solution.py:28
  16.2 8.4 %all-to-all-start.1 = ((bf16[16,128,1024]{2,1,0:T(8,128)(2,1)}), bf16[16,128,1024]{2,1,0:T(8,128)(2,1)}, u32[]{:S(2)}, u32[]{:S(2)}) async-start(bf16[16,128,1024]{2,1,0:T(8,128)(2,1)} %bitcast.61), calls=%async_computation.1 | async-start | bytes 8388608 | tf_op jit(solution)/shard_map/all_to_all | solution.py:874
  26.5 10.2 %project.2 = (bf16[1024,2048]{1,0:T(8,128)(2,1)}, bf16[1024,1024]{1,0:T(8,128)(2,1)}) custom-call(s32[1]{0:T(128)} %bitcast.1.scalars, bf16[1024,1024]{1,0:T(8,128)(2,1)} %bitcast.54, f32[2,1024]{1,0:T(2,128)} %slice.117.norm_ref, bf16[512,3072]{1,0:T(8,128)(2,1)} %w_own_ref.1, bf16[512,3072]{1,0:T(8,128)(2,1)} %collective-permute-done.1.other_ref.w_other_ref, ...), custom_call_target="tpu_custom_call" | custom-call | flops 4294967296 | bytes 10485760 | tf_op jit(solution)/shard_map/project/pallas_call | solution.py:750
  36.7 4.3 collective-permute-start.2
  42.3 5.8 %project.3.q_ref = bf16[1024,1024]{1,0:T(8,128)(2,1)} custom-call(s32[1]{0:T(128)} %bitcast.1.scalars, bf16[1024,1024]{1,0:T(8,128)(2,1)} %get-tuple-element.62.in_ref.refs_0_, bf16[512,3072]{1,0:T(8,128)(2,1)} %w_own_ref.1, bf16[512,3072]{1,0:T(8,128)(2,1)} %collective-permute-done.1.other_ref.w_other_ref, f32[1,1024]{1,0:T(1,128)} %get-tuple-element.172.add_ref), custom_call_target="tpu_custom_call" | custom-call | flops 2147483648 | bytes 6291456 | tf_op jit(solution)/shard_map/project/pallas_call | solution.py:750
  48.1 35.7 %attention_forward.1 = (bf16[1024,1024]{1,0:T(8,128)(2,1)}, f32[1024,1024]{1,0:T(8,128)}) custom-call(s32[2]{0:T(128)} %pad_add_fusion.scalars, bf16[1024,1024]{1,0:T(8,128)(2,1)} %project.3.q_ref, bf16[1024,2048]{1,0:T(8,128)(2,1)} %collective-permute-done.2.prev_k_ref.prev_v_ref, bf16[1024,2048]{1,0:T(8,128)(2,1)} %collective-permute-done.2.prev_k_ref.prev_v_ref, ...), custom_call_target="tpu_custom_call" | custom-call | flops 4294967296 | bytes 16777216 | tf_op jit(solution)/shard_map/attention_forward/pallas_call | solution.py:193
  83.8 4.7 fusion.29
  94.2 10.5 %all-to-all-done.1 = bf16[16,128,1024]{2,1,0:T(8,128)(2,1)} async-done(((bf16[16,128,1024]{2,1,0:T(8,128)(2,1)}), bf16[16,128,1024]{2,1,0:T(8,128)(2,1)}, u32[]{:S(2)}, u32[]{:S(2)}) %all-to-all-start.1) | async-done | bytes 4194336 | tf_op jit(solution)/shard_map/all_to_all | solution.py:874
  104.7 20.5 %all-to-all-start = ((bf16[16,64,1024]{2,1,0:T(8,128)(2,1)}), bf16[16,64,1024]{2,1,0:T(8,128)(2,1)}, u32[]{:S(2)}, u32[]{:S(2)}) async-start(bf16[16,64,1024]{2,1,0:T(8,128)(2,1)} %bitcast.66), calls=%async_computation | async-start | bytes 4194304 | tf_op jit(solution)/shard_map/all_to_all | solution.py:874
  128.9 28.0 %attention_weights.1.weights_ref = bf16[8,2,2048,1024]{3,2,1,0:T(8,128)(2,1)} custom-call(s32[2]{0:T(128)} %pad_add_fusion.scalars, bf16[1024,1024]{1,0:T(8,128)(2,1)} %project.3.q_ref, bf16[1024,2048]{1,0:T(8,128)(2,1)} %collective-permute-done.2.prev_k_ref.prev_v_ref, bf16[1024,2048]{1,0:T(8,128)(2,1)} %get-tuple-element.63.own_k_ref.own_v_ref, ...), custom_call_target="tpu_custom_call" | custom-call | flops 8589934592 | bytes 77594624 | tf_op jit(solution)/shard_map/attention_weights/pallas_call | solution.py:284
  156.8 10.9 %all-to-all-done = bf16[16,64,1024]{2,1,0:T(8,128)(2,1)} async-done(((bf16[16,64,1024]{2,1,0:T(8,128)(2,1)}), bf16[16,64,1024]{2,1,0:T(8,128)(2,1)}, u32[]{:S(2)}, u32[]{:S(2)}) %all-to-all-start) | async-done | bytes 2097184 | tf_op jit(solution)/shard_map/all_to_all | solution.py:874
  167.7 9.7 %all-to-all-start.3 = ((bf16[16,64,1024]{2,1,0:T(8,128)(2,1)}), bf16[16,64,1024]{2,1,0:T(8,128)(2,1)S(1)}, u32[]{:S(2)}, u32[]{:S(2)}) async-start(bf16[16,64,1024]{2,1,0:T(8,128)(2,1)} %bitcast.63), calls=%async_computation.3 | async-start | bytes 4194304 | tf_op jit(solution)/shard_map/all_to_all | solution.py:874
  178.8 47.8 %expert_rows.2 = (bf16[16,2,64,1024]{3,2,1,0:T(8,128)(2,1)}, bf16[1024,1024]{1,0:T(8,128)(2,1)}, bf16[1024,4096]{1,0:T(8,128)(2,1)}, bf16[1024,4096]{1,0:T(8,128...) custom-call(s32[2]{0:T(128)} %pad_add_fusion.1.scalars.y_before_ref, ...), custom_call_target="tpu_custom_call" | custom-call | flops 34359738368 | bytes 46137344 | tf_op jit(solution)/shard_map/expert_rows/pallas_call | solution.py:536
  226.7 7.2 %all-to-all-start.2 = ((bf16[16,64,1024]{2,1,0:T(8,128)(2,1)}), bf16[16,64,1024]{2,1,0:T(8,128)(2,1)}, u32[]{:S(2)}, u32[]{:S(2)}) async-start(bf16[16,64,1024]{2,1,0:T(8,128)(2,1)} %bitcast.65), calls=%async_computation.2 | async-start | bytes 4194304 | tf_op jit(solution)/shard_map/all_to_all | solution.py:874
  233.9 47.8 %expert_rows.3 = (bf16[16,2,64,1024]{3,2,1,0:T(8,128)(2,1)}, bf16[1024,1024]{1,0:T(8,128)(2,1)}, bf16[1024,4096]{1,0:T(8,128)(2,1)}, bf16[1024,4096]{1,0:T(8,128...) custom-call(s32[2]{0:T(128)} %pad_add_fusion.1.scalars.y_before_ref, ...), custom_call_target="tpu_custom_call", output_to_operand_aliasing={{0}: (6, {})} | custom-call | flops 34359738368 | bytes 46137344 | tf_op jit(solution)/shard_map/expert_rows/pallas_call | solution.py:536
  281.7 7.5 %all-to-all-start.4 = ((bf16[16,64,1024]{2,1,0:T(8,128)(2,1)}), bf16[16,64,1024]{2,1,0:T(8,128)(2,1)}, u32[]{:S(2)}, u32[]{:S(2)}) async-start(bf16[16,64,1024]{2,1,0:T(8,128)(2,1)} %bitcast.64), calls=%async_computation.4 | async-start | bytes 4194304 | tf_op jit(solution)/shard_map/all_to_all | solution.py:874
  292.3 25.4 %expert_weights.2 = (bf16[1024,2048]{1,0:T(8,128)(2,1)}, bf16[2048,1024]{1,0:T(8,128)(2,1)}) custom-call(bf16[1024,1024]{1,0:T(8,128)(2,1)} %bitcast.14.rows_ref.refs_0_, bf16[1024,1024]{1,0:T(8,128)(2,1)} %bitcast.58, bf16[1024,1024]{1,0:T(8,128)(2,1)} %get-tuple-element.71.refs_2_, bf16[1024,1024]{1,0:T(8,128)(2,1)} %get-tuple-element.72.refs_3_, ...), custom_call_target="tpu_custom_call" | custom-call | flops 17179869184 | bytes 41943040 | tf_op jit(solution)/shard_map/expert_weights/pallas_call | solution.py:623
  317.7 6.0 %fusion.4 = f32[1024,1024]{1,0:T(8,128)} fusion(bf16[1024,1024]{1,0:T(8,128)(2,1)} %bitcast.18, s32[1024]{0:T(1024)S(1)} %get-tuple-element.175), kind=kOutput, calls=%fused_computation.22 | convolution fusion | flops 2148532224 | bytes 6295552 | tf_op jit(solution)/shard_map/dot_general | solution.py:28
  323.7 6.8 %all-to-all-done.4 = bf16[16,64,1024]{2,1,0:T(8,128)(2,1)} async-done(((bf16[16,64,1024]{2,1,0:T(8,128)(2,1)}), bf16[16,64,1024]{2,1,0:T(8,128)(2,1)}, u32[]{:S(2)}, u32[]{:S(2)}) %all-to-all-start.4) | async-done | bytes 2097184 | tf_op jit(solution)/shard_map/all_to_all | solution.py:874
  330.5 10.5 %all-to-all-start.5 = ((bf16[16,128,1024]{2,1,0:T(8,128)(2,1)}), bf16[16,128,1024]{2,1,0:T(8,128)(2,1)}, u32[]{:S(2)}, u32[]{:S(2)}) async-start(bf16[16,128,1024]{2,1,0:T(8,128)(2,1)} %bitcast.62), calls=%async_computation.5 | async-start | bytes 8388608 | tf_op jit(solution)/shard_map/all_to_all | solution.py:874
  341.0 7.2 %multiply_reduce_fusion = (f32[1024]{0:T(1024)S(1)}, f32[1024]{0:T(1024)S(1)}, f32[1024]{0:T(1024)S(1)}, f32[1024]{0:T(1024)S(1)}, f32[1024,1024]{1,0:T(8,128)S(1)}) fusion(f32[1024,1024]{1,0:T(8,128)} %copy-done.18, f32[1024]{0:T(1024)S(1)} %add_rsqrt_fusion, f32[1024]{0:T(1024)S(1)} %broadcast_multiply_fusion.2, f32[1024]{0:T(1024)S(1)} %bitcast.68, ...), kind=kOutput, calls=%fused_computation.10 | convolution fusion | flops 2159013888 | bytes 14712832 | tf_op jit(solution)/shard_map/dot_general | solution.py:28
  355.2 28.5 %attention_backward.2 = (bf16[1024,512]{1,0:T(8,128)(2,1)}, bf16[2,1024,512]{2,1,0:T(8,128)(2,1)}, bf16[2,1024,512]{2,1,0:T(8,128)(2,1)}) custom-call(s32[2]{0:T(128)} %pad_add_fusion.scalars, bf16[1024,1024]{1,0:T(8,128)(2,1)} %project.3.q_ref, bf16[1024,2048]{1,0:T(8,128)(2,1)} %collective-permute-done.2.prev_k_ref.prev_v_ref, ...), custom_call_target="tpu_custom_call" | custom-call | flops 32212254720 | bytes 13631488 | tf_op jit(solution)/shard_map/attention_backward/pallas_call | solution.py:406
  385.4 16.4 %collective-permute-done.3.refs_3_.refs_2_ = bf16[2,1024,512]{2,1,0:T(8,128)(2,1)S(1)} collective-permute-done((bf16[2,1024,512]{2,1,0:T(8,128)(2,1)}, bf16[2,1024,512]{2,1,0:T(8,128)(2,1)S(1)}, u32[]{:S(2)}, u32[]{:S(2)}) %collective-permute-start.3) | collective-permute-done | bytes 2097184 | tf_op jit(solution)/shard_map/ppermute | solution.py:1059
  407.0 8.1 %pair_weights.2 = (bf16[512,2688]{1,0:T(8,128)(2,1)}, bf16[512,2688]{1,0:T(8,128)(2,1)}) custom-call(s32[1]{0:T(128)} %bitcast.1.scalars, bf16[1024,1024]{1,0:T(8,128)(2,1)S(1)} %copy-done, bf16[1024,512]{1,0:T(8,128)(2,1)S(1)} %copy-done.12, bf16[2,1024,512]{2,1,0:T(8,128)(2,1)S(1)} %copy-done.8, ...), custom_call_target="tpu_custom_call" | custom-call | flops 5637144576 | bytes 22020096 | tf_op jit(solution)/shard_map/pair_weights/pallas_call | solution.py:686
  415.2 5.2 collective-permute-done.4
  424.3 14.0 %all-to-all-start.6 = ((bf16[16,32,2688]{2,1,0:T(8,128)(2,1)}), bf16[16,32,2688]{2,1,0:T(8,128)(2,1)}, u32[]{:S(2)}, u32[]{:S(2)}) async-start(bf16[16,32,2688]{2,1,0:T(8,128)(2,1)} %bitcast.56), calls=%async_computation.6 | async-start | bytes 5505024 | tf_op jit(solution)/shard_map/all_to_all | solution.py:874
  438.4 28.9 %attention_backward.3 = (bf16[1024,512]{1,0:T(8,128)(2,1)}, bf16[2,1024,512]{2,1,0:T(8,128)(2,1)}, bf16[2,1024,512]{2,1,0:T(8,128)(2,1)}) custom-call(s32[2]{0:T(128)} %pad_add_fusion.scalars, bf16[1024,1024]{1,0:T(8,128)(2,1)} %project.3.q_ref, bf16[1024,2048]{1,0:T(8,128)(2,1)} %collective-permute-done.2.prev_k_ref.prev_v_ref, ...), custom_call_target="tpu_custom_call" | custom-call | flops 32212254720 | bytes 13631488 | tf_op jit(solution)/shard_map/attention_backward/pallas_call | solution.py:406
  468.8 13.3 %collective-permute-start.7 = (bf16[1024,2048]{1,0:T(8,128)(2,1)}, bf16[1024,2048]{1,0:T(8,128)(2,1)}, u32[]{:S(2)}, u32[]{:S(2)}) collective-permute-start(bf16[1024,2048]{1,0:T(8,128)(2,1)} %get-tuple-element.103), channel_id=1, source_target_pairs={{0,16},{16,0},{1,17},{17,1},{2,18},{18,2},{3,19},{19,3},{4,20},{20... | collective-permute-start | bytes 12582920 | tf_op jit(solution)/shard_map/ppermute | solution.py:870
  490.0 14.1 %first_norm.1 = (bf16[1024,1024]{1,0:T(8,128)(2,1)}, f32[128,1024]{1,0:T(8,128)S(1)}) custom-call(s32[1]{0:T(128)} %bitcast.1.scalars, bf16[1024,1024]{1,0:T(8,128)(2,1)S(1)} %bitcast.55, f32[1024,1024]{1,0:T(8,128)} %get-tuple-element.166.dh_ref, f32[1,1024]{1,0:T(1,128)S(1)} %get-tuple-element.167.gain_ref, bf16[512,3072]{1,0:T(8,128)(2,1)} %w_own_ref.1, ...), custom_call_target="tpu_custom_call" | custom-call | flops 6442450944 | bytes 20971520 | tf_op jit(solution)/shard_map/first_norm/pallas_call | solution.py:830
  522.8 6.8 %all-to-all-start.7 = ((bf16[16,32,1664]{2,1,0:T(8,128)(2,1)}), bf16[16,32,1664]{2,1,0:T(8,128)(2,1)S(1)}, u32[]{:S(2)}, u32[]{:S(2)}) async-start(bf16[16,32,1664]{2,1,0:T(8,128)(2,1)} %bitcast.29), calls=%async_computation.7 | async-start | bytes 3407872 | tf_op jit(solution)/shard_map/all_to_all | solution.py:874
  529.7 26.8 %expert_weights.3 = (f32[1024,2048]{1,0:T(8,128)}, f32[2048,1024]{1,0:T(8,128)}) custom-call(bf16[1024,1024]{1,0:T(8,128)(2,1)} %bitcast.14.rows_ref.refs_0_, bf16[1024,1024]{1,0:T(8,128)(2,1)} %bitcast.59, bf16[1024,1024]{1,0:T(8,128)(2,1)} %get-tuple-element.71.refs_2_, bf16[1024,1024]{1,0:T(8,128)(2,1)} %get-tuple-element.72.refs_3_, ...), custom_call_target="tpu_custom_call" | custom-call | flops 17179869184 | bytes 41943040 | tf_op jit(solution)/shard_map/expert_weights/pallas_call | solution.py:623
  556.5 8.3 %fusion.10 = bf16[1,1024,1024]{2,1,0:T(8,128)(2,1)} fusion(f32[1024,1024]{1,0:T(8,128)S(1)} %copy-done.20, f32[1024]{0:T(1024)S(1)} %bitcast.77, f32[1024]{0:T(1024)S(1)} %select_reduce_fusion, bf16[2048,1024]{1,0:T(8,128)(2,1)} %bitcast.25, s32[1024]{0:T(1024)S(1)} %copy-done.37), kind=kOutput, calls=%fused_computation.32 | convolution fusion | flops 4301258752 | bytes 10498048 | tf_op jit(solution)/shard_map/dot_general | solution.py:28
  (176 shorter events, 68.7 us)
Async XLA Ops:
  7.3 76.5 %all-gather.4.cloned.1.call-start = ((), (), s32[]{:S(2)}) async-start(), calls=%async_computation.8 | async-start | bytes 3145728 | tf_op jit(solution)/shard_map/all_gather | solution.py:937
  8.0 170.8 %all-gather.6.cloned.1.call-start = ((), (), s32[]{:S(2)}) async-start(), calls=%async_computation.9 | async-start | bytes 12582912 | tf_op jit(solution)/shard_map/all_gather | solution.py:938
  8.8 17.7 %collective-permute-start.1 = (bf16[512,3072]{1,0:T(8,128)(2,1)}, bf16[512,3072]{1,0:T(8,128)(2,1)}, u32[]{:S(2)}, u32[]{:S(2)}) collective-permute-start(bf16[512,3072]{1,0:T(8,128)(2,1)} %w_own_ref.1), channel_id=1, source_target_pairs={{0,16},{16,0},{1,17},{17,1},{2,18},{18,2},{3,19},{19,3},{4,20},{20... | collective-permute-start | bytes 9437192 | tf_op jit(solution)/shard_map/ppermute | solution.py:870
  9.5 15.1 %collective-permute-start = (bf16[24,512]{1,0:T(8,128)(2,1)S(1)}, bf16[24,512]{1,0:T(8,128)(2,1)S(1)}, u32[]{:S(2)}, u32[]{:S(2)}) collective-permute-start(bf16[24,512]{1,0:T(8,128)(2,1)S(1)} %concatenate.15), channel_id=1, source_target_pairs={{0,16},{16,0},{1,17},{17,1},{2,18},{18,2},{3,19},{19,3},{4,20},{20... | collective-permute-start | bytes 73736 | tf_op jit(solution)/shard_map/ppermute | solution.py:870
  16.2 88.5 %all-to-all-start.1 = ((bf16[16,128,1024]{2,1,0:T(8,128)(2,1)}), bf16[16,128,1024]{2,1,0:T(8,128)(2,1)}, u32[]{:S(2)}, u32[]{:S(2)}) async-start(bf16[16,128,1024]{2,1,0:T(8,128)(2,1)} %bitcast.61), calls=%async_computation.1 | async-start | bytes 8388608 | tf_op jit(solution)/shard_map/all_to_all | solution.py:874
  24.6 154.2 %all-gather.8.cloned.1.call-start = ((), (), s32[]{:S(2)}) async-start(), calls=%async_computation.10 | async-start | bytes 12582912 | tf_op jit(solution)/shard_map/all_gather | solution.py:939
  24.7 153.4 %copy-start.27 = (bf16[24,1024]{1,0:T(8,128)(2,1)}, bf16[24,1024]{1,0:T(8,128)(2,1)S(1)}, u32[]{:S(2)}) copy-start(bf16[24,1024]{1,0:T(8,128)(2,1)S(1)} %maximum_select_fusion) | copy-start | bytes 147460
  36.7 11.4 %collective-permute-start.2 = (bf16[1024,2048]{1,0:T(8,128)(2,1)}, bf16[1024,2048]{1,0:T(8,128)(2,1)}, u32[]{:S(2)}, u32[]{:S(2)}) collective-permute-start(bf16[1024,2048]{1,0:T(8,128)(2,1)} %get-tuple-element.63.own_k_ref.own_v_ref), channel_id=1, source_target_pairs={{0,16},{1,17},{2,18},{3,19},{4,20},{5,21},{6,22},{7,23},{8,24},{9,... | collective-permute-start | bytes 12582920 | tf_op jit(solution)/shard_map/ppermute | solution.py:986
  48.1 35.7 %copy-start.1 = (bf16[1,1024,1024]{2,1,0:T(8,128)(2,1)S(1)}, bf16[1,1024,1024]{2,1,0:T(8,128)(2,1)}, u32[]{:S(2)}) copy-start(bf16[1,1024,1024]{2,1,0:T(8,128)(2,1)} %param.17) | copy-start | bytes 6291460
  90.5 34.7 %copy-start.23 = (bf16[1024,1024]{1,0:T(8,128)(2,1)}, bf16[1024,1024]{1,0:T(8,128)(2,1)S(1)}, u32[]{:S(2)}) copy-start(bf16[1024,1024]{1,0:T(8,128)(2,1)S(1)} %add_convert_fusion.2) | copy-start | bytes 6291460
  104.7 63.0 %all-to-all-start = ((bf16[16,64,1024]{2,1,0:T(8,128)(2,1)}), bf16[16,64,1024]{2,1,0:T(8,128)(2,1)}, u32[]{:S(2)}, u32[]{:S(2)}) async-start(bf16[16,64,1024]{2,1,0:T(8,128)(2,1)} %bitcast.66), calls=%async_computation | async-start | bytes 4194304 | tf_op jit(solution)/shard_map/all_to_all | solution.py:874
  167.7 58.9 %all-to-all-start.3 = ((bf16[16,64,1024]{2,1,0:T(8,128)(2,1)}), bf16[16,64,1024]{2,1,0:T(8,128)(2,1)S(1)}, u32[]{:S(2)}, u32[]{:S(2)}) async-start(bf16[16,64,1024]{2,1,0:T(8,128)(2,1)} %bitcast.63), calls=%async_computation.3 | async-start | bytes 4194304 | tf_op jit(solution)/shard_map/all_to_all | solution.py:874
  226.7 55.0 %all-to-all-start.2 = ((bf16[16,64,1024]{2,1,0:T(8,128)(2,1)}), bf16[16,64,1024]{2,1,0:T(8,128)(2,1)}, u32[]{:S(2)}, u32[]{:S(2)}) async-start(bf16[16,64,1024]{2,1,0:T(8,128)(2,1)} %bitcast.65), calls=%async_computation.2 | async-start | bytes 4194304 | tf_op jit(solution)/shard_map/all_to_all | solution.py:874
  281.7 10.1 %copy-start.30 = (bf16[1024,128]{1,0:T(8,128)(2,1)S(1)}, bf16[1024,128]{1,0:T(8,128)(2,1)}, u32[]{:S(2)}) copy-start(bf16[1024,128]{1,0:T(8,128)(2,1)} %get-tuple-element.80) | copy-start | bytes 786436
  281.7 48.8 %all-to-all-start.4 = ((bf16[16,64,1024]{2,1,0:T(8,128)(2,1)}), bf16[16,64,1024]{2,1,0:T(8,128)(2,1)}, u32[]{:S(2)}, u32[]{:S(2)}) async-start(bf16[16,64,1024]{2,1,0:T(8,128)(2,1)} %bitcast.64), calls=%async_computation.4 | async-start | bytes 4194304 | tf_op jit(solution)/shard_map/all_to_all | solution.py:874
  330.5 93.8 %all-to-all-start.5 = ((bf16[16,128,1024]{2,1,0:T(8,128)(2,1)}), bf16[16,128,1024]{2,1,0:T(8,128)(2,1)}, u32[]{:S(2)}, u32[]{:S(2)}) async-start(bf16[16,128,1024]{2,1,0:T(8,128)(2,1)} %bitcast.62), calls=%async_computation.5 | async-start | bytes 8388608 | tf_op jit(solution)/shard_map/all_to_all | solution.py:874
  355.2 46.6 %copy-start = (bf16[1024,1024]{1,0:T(8,128)(2,1)S(1)}, bf16[1024,1024]{1,0:T(8,128)(2,1)}, u32[]{:S(2)}) copy-start(bf16[1024,1024]{1,0:T(8,128)(2,1)} %get-tuple-element.62.in_ref.refs_0_) | copy-start | bytes 6291460
  383.7 18.1 %collective-permute-start.3 = (bf16[2,1024,512]{2,1,0:T(8,128)(2,1)}, bf16[2,1024,512]{2,1,0:T(8,128)(2,1)S(1)}, u32[]{:S(2)}, u32[]{:S(2)}) collective-permute-start(bf16[2,1024,512]{2,1,0:T(8,128)(2,1)} %get-tuple-element.85), channel_id=1, source_target_pairs={{16,0},{17,1},{18,2},{19,3},{20,4},{21,5},{22,6},{23,7},{24,8},{25... | collective-permute-start | bytes 6291464 | tf_op jit(solution)/shard_map/ppermute | solution.py:1059
  401.8 13.3 %copy-start.4 = (bf16[2,1024,512]{2,1,0:T(8,128)(2,1)}, bf16[2,1024,512]{2,1,0:T(8,128)(2,1)S(1)}, u32[]{:S(2)}) copy-start(bf16[2,1024,512]{2,1,0:T(8,128)(2,1)S(1)} %collective-permute-done.3.refs_3_.refs_2_) | copy-start | bytes 6291460
  415.1 5.3 collective-permute-start.4
  424.3 81.9 %all-to-all-start.6 = ((bf16[16,32,2688]{2,1,0:T(8,128)(2,1)}), bf16[16,32,2688]{2,1,0:T(8,128)(2,1)}, u32[]{:S(2)}, u32[]{:S(2)}) async-start(bf16[16,32,2688]{2,1,0:T(8,128)(2,1)} %bitcast.56), calls=%async_computation.6 | async-start | bytes 5505024 | tf_op jit(solution)/shard_map/all_to_all | solution.py:874
  438.4 47.2 %copy-start.2 = (bf16[1,1024,1024]{2,1,0:T(8,128)(2,1)S(1)}, bf16[1,1024,1024]{2,1,0:T(8,128)(2,1)}, u32[]{:S(2)}) copy-start(bf16[1,1024,1024]{2,1,0:T(8,128)(2,1)} %param.17) | copy-start | bytes 6291460
  438.4 47.2 %copy-start.9 = (bf16[2,1024,512]{2,1,0:T(8,128)(2,1)S(1)}, bf16[2,1024,512]{2,1,0:T(8,128)(2,1)}, u32[]{:S(2)}) copy-start(bf16[2,1024,512]{2,1,0:T(8,128)(2,1)} %get-tuple-element.84.refs_2_.refs_1_) | copy-start | bytes 6291460
  438.4 47.2 %copy-start.13 = (bf16[1024,512]{1,0:T(8,128)(2,1)S(1)}, bf16[1024,512]{1,0:T(8,128)(2,1)}, u32[]{:S(2)}) copy-start(bf16[1024,512]{1,0:T(8,128)(2,1)} %get-tuple-element.83.refs_1_.refs_0_) | copy-start | bytes 3145732
  467.3 18.3 %collective-permute-start.5 = (bf16[2,1024,512]{2,1,0:T(8,128)(2,1)}, bf16[2,1024,512]{2,1,0:T(8,128)(2,1)S(1)}, u32[]{:S(2)}, u32[]{:S(2)}) collective-permute-start(bf16[2,1024,512]{2,1,0:T(8,128)(2,1)} %get-tuple-element.95), channel_id=1, source_target_pairs={{16,0},{17,1},{18,2},{19,3},{20,4},{21,5},{22,6},{23,7},{24,8},{25... | collective-permute-start | bytes 6291464 | tf_op jit(solution)/shard_map/ppermute | solution.py:1059
  468.8 60.9 %collective-permute-start.7 = (bf16[1024,2048]{1,0:T(8,128)(2,1)}, bf16[1024,2048]{1,0:T(8,128)(2,1)}, u32[]{:S(2)}, u32[]{:S(2)}) collective-permute-start(bf16[1024,2048]{1,0:T(8,128)(2,1)} %get-tuple-element.103), channel_id=1, source_target_pairs={{0,16},{16,0},{1,17},{17,1},{2,18},{18,2},{3,19},{19,3},{4,20},{20... | collective-permute-start | bytes 12582920 | tf_op jit(solution)/shard_map/ppermute | solution.py:870
  482.1 47.6 %collective-permute-start.8 = (bf16[2048,1024]{1,0:T(8,128)(2,1)}, bf16[2048,1024]{1,0:T(8,128)(2,1)}, u32[]{:S(2)}, u32[]{:S(2)}) collective-permute-start(bf16[2048,1024]{1,0:T(8,128)(2,1)} %get-tuple-element.104), channel_id=1, source_target_pairs={{0,16},{16,0},{1,17},{17,1},{2,18},{18,2},{3,19},{19,3},{4,20},{20... | collective-permute-start | bytes 12582920 | tf_op jit(solution)/shard_map/ppermute | solution.py:870
  517.4 3.7 collective-permute-start.6
  522.8 44.1 %all-to-all-start.7 = ((bf16[16,32,1664]{2,1,0:T(8,128)(2,1)}), bf16[16,32,1664]{2,1,0:T(8,128)(2,1)S(1)}, u32[]{:S(2)}, u32[]{:S(2)}) async-start(bf16[16,32,1664]{2,1,0:T(8,128)(2,1)} %bitcast.29), calls=%async_computation.7 | async-start | bytes 3407872 | tf_op jit(solution)/shard_map/all_to_all | solution.py:874
  529.7 26.8 %copy-start.20 = (f32[1024,1024]{1,0:T(8,128)S(1)}, f32[1024,1024]{1,0:T(8,128)}, u32[]{:S(2)}) copy-start(f32[1024,1024]{1,0:T(8,128)} %copy-done.18) | copy-start | bytes 12582916
  529.7 26.8 %copy-start.35 = (f32[1,1024]{1,0:T(1,128)S(1)}, f32[1,1024]{1,0:T(1,128)}, u32[]{:S(2)}) copy-start(f32[1,1024]{1,0:T(1,128)} %get-tuple-element.168) | copy-start | bytes 12292
  529.7 26.8 %copy-start.37 = (s32[1024]{0:T(1024)S(1)}, s32[1024]{0:T(1024)}, u32[]{:S(2)}) copy-start(s32[1024]{0:T(1024)} %copy-done.36) | copy-start | bytes 12292
  (35 other events, 102.1 us)
Sparse Core Ops, SparseCore 0:
  9.7 13.2 all-gather.3
  24.5 26.0 all-gather.5
  52.1 20.8 all-gather.7
